TPU v7x, 256 devices: a whole 4x4x8 slice. The times are simulated.
256 devices in a mesh: section: 32 (over x, z), expert: 8 (over y, core).
Axes of the slice: x: 4, y: 4, z: 8, core: 2. Of those that a mesh axis runs over, the one named last changes fastest.
Arguments:
- tokens: bfloat16 [2048, 4096], P('expert', 'section'), may hold values from -6 to 6
- routes: int32 [2048, 2], P('expert'), may hold values from 0 to 7, all different within a row; in each aligned block of 256 rows (0 to 255, 256 to 511, ...) at most 80 rows name the same one
- mix_weights: float32 [2048, 2], P('expert'), may hold values from 0.2 to 1
- w_gate: bfloat16 [8, 4096, 8192], P('expert', None, 'section'), may hold values from -0.1875 to 0.1875
- w_up: bfloat16 [8, 4096, 8192], P('expert', None, 'section'), may hold values from -0.1875 to 0.1875
- w_down: bfloat16 [8, 8192, 4096], P('expert', 'section'), may hold values from -0.125 to 0.125
- upstream: bfloat16 [2048, 4096], P('expert', 'section'), may hold values from -6 to 6
Outputs:
- mixed: bfloat16 [2048, 4096], P('expert', 'section')
- grad_tokens: bfloat16 [2048, 4096], P('expert', 'section')
- grad_mix: float32 [2048, 2], P('expert')
- grad_gate: bfloat16 [8, 4096, 8192], P('expert', None, 'section')
- grad_up: bfloat16 [8, 4096, 8192], P('expert', None, 'section')
- grad_down: bfloat16 [8, 8192, 4096], P('expert', 'section')
Inputs may be any that keep to these rules, and one draw needn't show every extreme that they name: `routes`: each token names 2 different experts. Among the 256 tokens of one index of the expert axis no expert is named more than 80 times, and in some such block one expert is named exactly 80 times.
All inputs are finite; a program needn't handle non-finite values.
Results may differ from a plain program's by a relative error of at most 0.02.
Values may be sent and summed in bfloat16 or wider, within the bound.
No kernel may reach another device: no remote copies, remote signals or barrier semaphores. Data moves between devices by JAX's collectives and lax.ppermute only.
A program may use at most 128 MiB of HBM per device.

v0:
```python
import functools

import jax
import jax.numpy as jnp
from jax import lax
from jax.experimental import pallas as pl
from jax.experimental.pallas import tpu as pltpu
from jax.sharding import PartitionSpec as P

highest = lax.Precision.HIGHEST
f32, bf16 = jnp.float32, jnp.bfloat16
NX, NZ = 4, 8
Z_GROUPS = [[x * NZ + z for z in range(NZ)] for x in range(NX)]


def shift_z(value, d):
    pairs = [(x * NZ + z, x * NZ + (z + d) % NZ) for x in range(NX) for z in range(NZ)]
    return lax.ppermute(value, "section", pairs)


def shift_x(value, d):
    pairs = [(x * NZ + z, ((x + d) % NX) * NZ + z) for x in range(NX) for z in range(NZ)]
    return lax.ppermute(value, "section", pairs)


def in_order(relative, own, count):
    held = jnp.stack(relative)
    return jnp.concatenate(
        [lax.dynamic_index_in_dim(held, (own - j) % count, 0, keepdims=False) for j in range(count)],
        axis=1,
    )


def spread_x(value, extra, own):
    parts = value.reshape(value.shape[0], NX, -1).transpose(1, 0, 2)

    def part(d):
        return lax.dynamic_index_in_dim(parts, (own + d) % NX, 0, keepdims=False)

    sent = [
        shift_x(jnp.concatenate([part(d).astype(bf16), extra]), d).astype(f32) for d in range(1, NX)
    ]
    total = sum(sent, jnp.concatenate([part(0), extra.astype(f32)]))
    return total[: value.shape[0]], total[value.shape[0] :]


def high_low(value):
    high = value.astype(bf16)
    return high, (value - high.astype(f32)).astype(bf16)


def spread_z(value, own):
    parts = value.reshape(value.shape[0], NZ, -1).transpose(1, 0, 2)

    def part(d):
        return lax.dynamic_index_in_dim(parts, (own + d) % NZ, 0, keepdims=False)

    sent = [shift_z(part(d).astype(bf16), d) for d in (4, 3, -3, 2, -2, 1, -1)]
    return sum((term.astype(f32) for term in sent), part(0))


def ring_gather_x(value):
    half = value.shape[1] // 2
    a, b = value[:, :half], value[:, half:]
    below_a, above_b = shift_x(a, 1), shift_x(b, -1)
    below_b, above_a = shift_x(b, 1), shift_x(a, -1)
    far_a, far_b = shift_x(below_a, 1), shift_x(above_b, -1)
    return [(a, b), (below_a, below_b), (far_a, far_b), (above_a, above_b)]


def ring_scatter_x(parts):
    far_a, far_b = shift_x(parts[2][0], 1), shift_x(parts[2][1], -1)
    below_b, above_a = shift_x(parts[1][1], 1), shift_x(parts[3][0], -1)
    next_a = (parts[1][0].astype(f32) + far_a.astype(f32)).astype(bf16)
    next_b = (parts[3][1].astype(f32) + far_b.astype(f32)).astype(bf16)
    below_a, above_b = shift_x(next_a, 1), shift_x(next_b, -1)
    return [(below_a, below_b), (above_a, above_b)]


def near_z(value):
    return jnp.stack([shift_z(value, 1), value, shift_z(value, -1)])


def far_z(near):
    low, high = shift_z(near, 3), shift_z(near[:2], -3)
    return [low, near, high]


def side_by_side(pieces, own):
    held = jnp.concatenate(pieces)
    return jnp.concatenate(
        [
            lax.dynamic_index_in_dim(held, (j - own + 4) % NZ, 0, keepdims=False)
            for j in range(NZ)
        ],
        axis=1,
    )


def dot_nt(a, b):
    return lax.dot_general(a, b, (((1,), (1,)), ((), ())), preferred_element_type=f32)


def dot_tn(a, b):
    return lax.dot_general(a, b, (((0,), (0,)), ((), ())), preferred_element_type=f32)


def forward_kernel(
    x_ref, tok_ref, gate_ref, up_ref, down_ref, coef_ref, silu_ref, hid_ref, *rest
):
    outs, (acc_gate, acc_up, made) = rest[: 2 * NX], rest[2 * NX :]
    step = pl.program_id(0)
    width = gate_ref.shape[-1]

    @pl.when(step == 0)
    def _():
        acc_gate[...] = jnp.zeros_like(acc_gate)
        acc_up[...] = jnp.zeros_like(acc_up)

    @pl.when(step < NZ)
    def _():
        block = tok_ref[...]
        gate = gate_ref[...].reshape(-1, width)
        up = up_ref[...].reshape(-1, width)
        acc_gate[...] += jnp.dot(block, gate, preferred_element_type=f32)
        acc_up[...] += jnp.dot(block, up, preferred_element_type=f32)

    @pl.when(step == NZ - 1)
    def _():
        act_gate, act_up = acc_gate[...], acc_up[...]
        sig = jax.nn.sigmoid(act_gate)
        silu_gate = act_gate * sig
        silu_ref[...] = silu_gate
        coef_ref[...] = act_up * (sig * (1.0 + act_gate * (1.0 - sig)))
        hid_ref[...] = (silu_gate * act_up).astype(bf16)

    @pl.when(step >= NZ)
    def _():
        made[...] = jnp.dot(hid_ref[...], down_ref[...], preferred_element_type=f32).astype(bf16)

    for d in range(NX):

        @pl.when(step == NZ + d)
        def _(d=d):
            half = made.shape[1] // 2
            outs[2 * d][...] = made[:, :half]
            outs[2 * d + 1][...] = made[:, half:]


def backward_kernel(x_ref, *refs):
    ups, refs = refs[: 2 * NX], refs[2 * NX :]
    down_ref, gate_ref, up_ref, coef_ref, silu_ref, hid_ref = refs[:6]
    part_ref, gate_out, up_out, acc, piece, mix = refs[6:]
    step = pl.program_id(0)
    width = gate_ref.shape[-1]
    rows = acc.shape[0]

    for d in range(NX):

        @pl.when(step == d)
        def _(d=d):
            half = piece.shape[1] // 2
            piece[:, :half] = ups[2 * d][...]
            piece[:, half:] = ups[2 * d + 1][...]

    @pl.when(step == 0)
    def _():
        acc[...] = jnp.zeros_like(acc)

    @pl.when(step < NX)
    def _():
        acc[...] += dot_nt(piece[...], down_ref[...])

    @pl.when(step == NX - 1)
    def _():
        grad_hidden = acc[...]
        gate_out[...] = (grad_hidden * coef_ref[...]).astype(bf16)
        up_out[...] = (grad_hidden * silu_ref[...]).astype(bf16)
        terms = grad_hidden * hid_ref[...].astype(f32)
        sums = lax.dot_general(
            jnp.ones((8, width), f32),
            terms,
            (((1,), (1,)), ((), ())),
            precision=highest,
            preferred_element_type=f32,
        )
        high, low = high_low(sums)
        cut = part_ref.shape[2]
        tail = jnp.zeros((1, 2 * cut - rows), bf16)
        mix[...] = jnp.concatenate(
            [
                high[:1, :cut],
                jnp.concatenate([high[:1, cut:], tail], axis=1),
                low[:1, :cut],
                jnp.concatenate([low[:1, cut:], tail], axis=1),
                jnp.zeros((4, cut), bf16),
            ]
        )

    @pl.when(step >= NX)
    def _():
        gate = gate_ref[...].reshape(-1, width)
        up = up_ref[...].reshape(-1, width)
        part_ref[0, :rows] = (dot_nt(gate_out[...], gate) + dot_nt(up_out[...], up)).astype(bf16)
        part_ref[0, rows:] = mix[...]


def weight_kernel(x_ref, *refs):
    tok_ref, gact_ref, uact_ref, hid_ref = refs[:4]
    ups = refs[4 : 4 + 2 * NX]
    gate_out, up_out, down_out, piece = refs[4 + 2 * NX :]
    step = pl.program_id(0)

    @pl.when(step < NZ)
    def _():
        block = tok_ref[...]
        gate_out[...] = dot_tn(block, gact_ref[...]).astype(bf16).reshape(gate_out.shape)
        up_out[...] = dot_tn(block, uact_ref[...]).astype(bf16).reshape(up_out.shape)

    for d in range(NX):

        @pl.when(step == NZ + d)
        def _(d=d):
            half = piece.shape[1] // 2
            piece[:, :half] = ups[2 * d][...]
            piece[:, half:] = ups[2 * d + 1][...]

    @pl.when(step >= NZ)
    def _():
        down_out[...] = dot_tn(hid_ref[...], piece[...]).astype(bf16)


def call(kernel, steps, in_specs, out_specs, out_shape, scratch, flops, moved, args):
    return pl.pallas_call(
        kernel,
        grid_spec=pltpu.PrefetchScalarGridSpec(
            num_scalar_prefetch=1,
            grid=(steps,),
            in_specs=in_specs,
            out_specs=out_specs,
            scratch_shapes=scratch,
        ),
        out_shape=out_shape,
        compiler_params=pltpu.CompilerParams(vmem_limit_bytes=50 * 1024 * 1024),
        cost_estimate=pl.CostEstimate(flops=flops, bytes_accessed=moved, transcendentals=0),
    )(*args)


def slot_tables(route_rows, mix_rows, capacity, experts):
    tok_count, top_count = route_rows.shape
    flat_routes = route_rows.reshape(-1)
    onehot = (flat_routes[:, None] == jnp.arange(experts, dtype=jnp.int32)[None, :]).astype(
        jnp.int32
    )
    earlier = jnp.cumsum(onehot, axis=0) - onehot
    position = jnp.sum(earlier * onehot, axis=1)
    target = (flat_routes * capacity + position).reshape(tok_count, top_count)
    slot_ids = jnp.arange(experts * capacity, dtype=jnp.int32)
    hits = target[None, :, :] == slot_ids[:, None, None]
    matches = hits.astype(f32)
    select = jnp.sum(matches, axis=2)
    weighted = jnp.sum(matches * mix_rows[None, :, :], axis=2)
    return (target, select, weighted)


def per_device(tokens, routes, mix_weights, w_gate, w_up, w_down, upstream):
    experts = lax.axis_size("expert")
    section = lax.axis_index("section")
    my_x, my_z = section // NZ, section % NZ
    tok_count, feat = tokens.shape
    top_count = routes.shape[1]
    capacity = 5 * tok_count * top_count // (4 * experts)
    rows = experts * capacity
    ff = w_gate.shape[2]
    wide_x, wide_z = NX * feat, NZ * feat
    full = NX * wide_z
    where = my_x.reshape(1).astype(jnp.int32)
    gate4 = w_gate.reshape(NX, NZ, feat, ff)
    up4 = w_up.reshape(NX, NZ, feat, ff)
    down = w_down[0]

    up_near = near_z(upstream)
    target, select, weighted = slot_tables(routes, mix_weights, capacity, experts)
    slot_scale = jnp.sum(weighted, axis=1)
    select_low = select.astype(bf16)

    def exchange(value):
        return lax.all_to_all(
            value.reshape(experts, -1, value.shape[-1]), "expert", split_axis=0, concat_axis=0, tiled=True
        ).reshape(-1, value.shape[-1])

    tok_sent = jnp.dot(select_low, tokens, preferred_element_type=f32).astype(bf16)
    tok_sent, up_near = lax.optimization_barrier((tok_sent, up_near))
    up_pieces = far_z(up_near)
    tok_rows, up_pieces = lax.optimization_barrier((exchange(tok_sent), up_pieces))
    tok_x = in_order([tok_rows] + [shift_x(tok_rows, d) for d in range(1, NX)], my_x, NX)
    up_z = side_by_side(up_pieces, my_z)
    up_rows = jnp.dot(select_low, up_z, preferred_element_type=f32) * slot_scale[:, None]
    up_rows = exchange(up_rows.astype(bf16))

    dispatched = lax.all_gather(
        tok_x, "section", axis_index_groups=Z_GROUPS, axis=1, tiled=True
    )
    ups = [half for pair in ring_gather_x(up_rows) for half in pair]

    def whole(*shape):
        return pl.BlockSpec(shape, lambda i, s: (0,) * len(shape))

    def clip(i, low, count):
        return jnp.clip(i - low, 0, count - 1)

    def weight_spec(low):
        return pl.BlockSpec((NX, 1, feat, ff), lambda i, s: (0, clip(i, low, NZ), 0, 0))

    def struct(shape, kind):
        return jax.ShapeDtypeStruct(shape, kind)

    tok_spec = pl.BlockSpec((rows, wide_x), lambda i, s: (0, clip(i, 0, NZ)))
    coef, silu_gate, hidden, *outs = call(
        forward_kernel,
        NZ + NX,
        [
            tok_spec,
            weight_spec(0),
            weight_spec(0),
            pl.BlockSpec((ff, wide_z), lambda i, s: (0, (s[0] + clip(i, NZ, NX)) % NX)),
        ],
        [whole(rows, ff)] * 3 + [whole(rows, wide_z // 2)] * (2 * NX),
        [struct((rows, ff), f32)] * 2
        + [struct((rows, ff), bf16)]
        + [struct((rows, wide_z // 2), bf16)] * (2 * NX),
        [pltpu.VMEM((rows, ff), f32)] * 2 + [pltpu.VMEM((rows, wide_z), bf16)],
        6 * rows * full * ff,
        2 * (2 * rows * full + 3 * full * ff),
        (where, dispatched, gate4, up4, down),
    )

    sent_x = ring_scatter_x([(outs[2 * d], outs[2 * d + 1]) for d in range(NX)])

    back, gate_act, up_act = call(
        backward_kernel,
        NX + NZ,
        [whole(rows, wide_z // 2)] * (2 * NX)
        + [
            pl.BlockSpec((ff, wide_z), lambda i, s: (0, (s[0] + NX - clip(i, 0, NX)) % NX)),
            weight_spec(NX),
            weight_spec(NX),
        ]
        + [whole(rows, ff)] * 3,
        [pl.BlockSpec((1, rows + 8, wide_x), lambda i, s: (clip(i, NX, NZ), 0, 0))]
        + [whole(rows, ff)] * 2,
        [struct((NZ, rows + 8, wide_x), bf16)] + [struct((rows, ff), bf16)] * 2,
        [
            pltpu.VMEM((rows, ff), f32),
            pltpu.VMEM((rows, wide_z), bf16),
            pltpu.VMEM((8, wide_x), bf16),
        ],
        0,
        0,
        (where, *ups, down, gate4, up4, coef, silu_gate, hidden),
    )

    back_z = lax.psum_scatter(
        back.reshape(NZ * (rows + 8), wide_x),
        "section",
        axis_index_groups=Z_GROUPS,
        scatter_dimension=0,
        tiled=True,
    )
    grad_gate, grad_up, grad_down = call(
        weight_kernel,
        NZ + NX,
        [tok_spec] + [whole(rows, ff)] * 3 + [whole(rows, wide_z // 2)] * (2 * NX),
        [weight_spec(0)] * 2
        + [pl.BlockSpec((ff, wide_z), lambda i, s: (0, (s[0] + NX - clip(i, NZ, NX)) % NX))],
        [struct((NX, NZ, feat, ff), bf16)] * 2 + [struct((ff, full), bf16)],
        [pltpu.VMEM((rows, wide_z), bf16)],
        0,
        0,
        (where, dispatched, gate_act, up_act, hidden, *ups),
    )

    sent_x, grads = lax.optimization_barrier((sent_x, (grad_gate, grad_up, grad_down)))
    grad_gate, grad_up, grad_down = grads

    summed = jnp.concatenate(
        [
            (outs[h].astype(f32) + sent_x[0][h].astype(f32) + sent_x[1][h].astype(f32)).astype(bf16)
            for h in range(2)
        ],
        axis=1,
    )
    returned = exchange(summed)

    mix = back_z[rows : rows + 4].reshape(2, 2 * wide_x)[:, :rows].reshape(2, experts, capacity)
    mix = jnp.pad(mix.transpose(1, 0, 2), ((0, 0), (0, 6), (0, wide_x - capacity)))
    back = exchange(
        jnp.concatenate([back_z[:rows].reshape(experts, capacity, wide_x), mix], axis=1)
    ).reshape(experts, capacity + 8, wide_x)
    returned, back = lax.optimization_barrier((returned, back))

    moe_out = jnp.dot(weighted.T, returned.astype(f32), precision=highest)
    mixed = (tokens.astype(f32) + spread_z(moe_out, my_z)).astype(bf16)
    grad_moe = dot_tn(select_low, back[:, :capacity].reshape(rows, wide_x))
    mix = jnp.sum(back[:, capacity : capacity + 2, :capacity].astype(f32), axis=1)
    mix = mix.reshape(-1)[target.T].reshape(-1, feat)
    grad_moe, mix = spread_x(grad_moe, jnp.concatenate(high_low(mix)), my_x)
    grad_tokens = (upstream.astype(f32) + grad_moe).astype(bf16)
    mix = jnp.sum(mix.reshape(2, top_count, tok_count), axis=0)
    grad_mix = mix.T / mix_weights
    return (
        mixed,
        grad_tokens,
        grad_mix,
        grad_gate.reshape(1, full, ff),
        grad_up.reshape(1, full, ff),
        grad_down[None],
    )


def solution(mesh):
    return jax.shard_map(
        per_device,
        mesh=mesh,
        in_specs=(
            P("expert", "section"),
            P("expert", None),
            P("expert", None),
            P("expert", None, "section"),
            P("expert", None, "section"),
            P("expert", "section", None),
            P("expert", "section"),
        ),
        out_specs=(
            P("expert", "section"),
            P("expert", "section"),
            P("expert", None),
            P("expert", None, "section"),
            P("expert", None, "section"),
            P("expert", "section", None),
        ),
        check_vma=False,
    )
```

profile of v0, /device:TPU:8, one launch (start us, length us, event | category | flops | bytes accessed | tf_op | source)
XLA Modules:
  0.0 275.7 jit_solution(16670171182821214447)
XLA Ops:
  7.2 2.0 collective-permute-start
  9.2 4.0 %collective-permute-start.1 = (bf16[256,128]{1,0:T(8,128)(2,1)}, bf16[256,128]{1,0:T(8,128)(2,1)S(1)}, u32[]{:S(2)}, u32[]{:S(2)}) collective-permute-start(bf16[256,128]{1,0:T(8,128)(2,1)} %param.13), channel_id=1, source_target_pairs={{0,56},{8,0},{16,8},{24,16},{32,24},{40,32},{48,40},{56,48},{64,12... | collective-permute-start | bytes 196616 | tf_op jit(solution)/shard_map/ppermute | solution.py:18
  13.2 0.8 copy.45
  14.3 1.1 reduce-window.6
  16.1 0.7 fusion.30
  16.8 1.9 select_reduce_fusion.1
  18.7 0.9 convolution_convert_fusion
  19.6 1.9 collective-permute-start.2
  21.5 4.9 %all-to-all-start = ((bf16[8,80,128]{2,1,0:T(8,128)(2,1)}), bf16[8,80,128]{2,1,0:T(8,128)(2,1)S(1)}, u32[]{:S(2)}, u32[]{:S(2)}) async-start(bf16[8,80,128]{2,1,0:T(8,128)(2,1)} %bitcast.7), calls=%async_computation | async-start | bytes 327680 | tf_op jit(solution)/shard_map/all_to_all | solution.py:288
  26.4 3.3 %collective-permute-start.3 = (bf16[2,256,128]{2,1,0:T(8,128)(2,1)S(1)}, bf16[2,256,128]{2,1,0:T(8,128)(2,1)S(1)}, u32[]{:S(2)}, u32[]{:S(2)}) collective-permute-start(bf16[2,256,128]{2,1,0:T(8,128)(2,1)S(1)} %slice.38), channel_id=1, source_target_pairs={{0,40},{8,48},{16,56},{24,0},{32,8},{40,16},{48,24},{56,32},{64,10... | collective-permute-start | bytes 393224 | tf_op jit(solution)/shard_map/ppermute | solution.py:18
  29.7 4.3 %collective-permute-done.3 = bf16[2,256,128]{2,1,0:T(8,128)(2,1)S(1)} collective-permute-done((bf16[2,256,128]{2,1,0:T(8,128)(2,1)S(1)}, bf16[2,256,128]{2,1,0:T(8,128)(2,1)S(1)}, u32[]{:S(2)}, u32[]{:S(2)}) %collective-permute-start.3) | collective-permute-done | bytes 131104 | tf_op jit(solution)/shard_map/ppermute | solution.py:18
  34.1 0.8 collective-permute-done.2
  34.9 1.5 collective-permute-start.4
  36.4 2.7 collective-permute-start.5
  39.1 1.4 collective-permute-start.6
  40.5 1.7 collective-permute-done.4
  42.2 4.5 %collective-permute-done.5 = bf16[640,128]{1,0:T(8,128)(2,1)S(1)} collective-permute-done((bf16[640,128]{1,0:T(8,128)(2,1)S(1)}, bf16[640,128]{1,0:T(8,128)(2,1)S(1)}, u32[]{:S(2)}, u32[]{:S(2)}) %collective-permute-start.5) | collective-permute-done | bytes 163872 | tf_op jit(solution)/shard_map/ppermute | solution.py:23
  46.9 0.9 pad_maximum_fusion.2
  48.9 22.2 %all_to_all.20 = bf16[8,80,1024]{2,1,0:T(8,128)(2,1)S(1)} all-to-all(bf16[8,80,1024]{2,1,0:T(8,128)(2,1)S(1)} %bitcast.131), channel_id=1, replica_groups=mesh['section'=32,'expert'=8] {'expert'}, dimensions={0} | all-to-all | bytes 2621440 | tf_op jit(solution)/shard_map/all_to_all | solution.py:288
  71.2 1.4 collective-permute-start.13
  72.6 1.9 collective-permute-start.16
  74.6 3.1 %collective-permute-start.18 = (bf16[640,512]{1,0:T(8,128)(2,1)S(1)}, bf16[640,512]{1,0:T(8,128)(2,1)}, u32[]{:S(2)}, u32[]{:S(2)}) collective-permute-start(bf16[640,512]{1,0:T(8,128)(2,1)S(1)} %get-tuple-element.78.refs_0_.refs_4_), channel_id=1, source_target_pairs={{0,192},{8,200},{16,208},{24,216},{32,224},{40,232},{48,240},{56,2... | collective-permute-start | bytes 1966088 | tf_op jit(solution)/shard_map/ppermute | solution.py:23
  77.7 12.4 %collective-permute-done.13.refs_2_.refs_6_ = bf16[640,512]{1,0:T(8,128)(2,1)S(1)} collective-permute-done((bf16[640,512]{1,0:T(8,128)(2,1)S(1)}, bf16[640,512]{1,0:T(8,128)(2,1)S(1)}, u32[]{:S(2)}, u32[]{:S(2)}) %collective-permute-start.13) | collective-permute-done | bytes 655392 | tf_op jit(solution)/shard_map/ppermute | solution.py:23
  90.4 3.1 %collective-permute-start.17 = (bf16[640,512]{1,0:T(8,128)(2,1)}, bf16[640,512]{1,0:T(8,128)(2,1)}, u32[]{:S(2)}, u32[]{:S(2)}) collective-permute-start(bf16[640,512]{1,0:T(8,128)(2,1)} %collective-permute-done.16.refs_7_.refs_11_), channel_id=1, source_target_pairs={{0,192},{8,200},{16,208},{24,216},{32,224},{40,232},{48,240},{56,2... | collective-permute-start | bytes 1966088 | tf_op jit(solution)/shard_map/ppermute | solution.py:23
  93.5 22.7 %all-gather.2.cloned.1.call-done.tok_ref.refs_0_ = bf16[640,4096]{1,0:T(8,128)(2,1)} async-done(((bf16[640,512]{1,0:T(8,128)(2,1)}), bf16[640,4096]{1,0:T(8,128)(2,1)}) %all-gather.2.cloned.1.call-update) | async-done | bytes 5242896 | tf_op jit(solution)/shard_map/all_gather | solution.py:301
  116.2 13.7 %shard_map.118 = (f32[640,256]{1,0:T(8,128)S(1)}, f32[640,256]{1,0:T(8,128)S(1)}, bf16[640,256]{1,0:T(8,128)(2,1)S(1)}, bf16[640,512]{1,0:T(8,128)(2,1)S(1)}, bf...) custom-call(s32[1]{0:T(128)} %bitcast.3.x_ref, ...), custom_call_target="tpu_custom_call" | custom-call | flops 4026531840 | bytes 16777216 | tf_op jit(solution)/shard_map/pallas_call | solution.py:234
  130.0 0.8 copy-done
  130.8 0.8 copy-done.1
  131.6 0.9 copy-done.6
  132.5 14.9 %shard_map.119 = (bf16[8,648,512]{2,1,0:T(8,128)(2,1)}, bf16[640,256]{1,0:T(8,128)(2,1)S(1)}, bf16[640,256]{1,0:T(8,128)(2,1)S(1)}) custom-call(s32[1]{0:T(128)} %bitcast.3.x_ref, bf16[640,512]{1,0:T(8,128)(2,1)S(1)} %get-tuple-element.78.refs_0_.refs_4_, bf16[640,512]{1,0:T(8,128)(2,1)S(1)} %get-tuple-element.77.refs_1_.refs_5_, ...), custom_call_target="tpu_custom_call" | custom-call | tf_op jit(solution)/shard_map/pallas_call | solution.py:234
  147.4 0.7 copy-done.8
  148.2 2.8 %collective-permute-start.11 = (bf16[640,512]{1,0:T(8,128)(2,1)}, bf16[640,512]{1,0:T(8,128)(2,1)S(1)}, u32[]{:S(2)}, u32[]{:S(2)}) collective-permute-start(bf16[640,512]{1,0:T(8,128)(2,1)} %get-tuple-element.47), channel_id=1, source_target_pairs={{0,192},{8,200},{16,208},{24,216},{32,224},{40,232},{48,240},{56,2... | collective-permute-start | bytes 1966088 | tf_op jit(solution)/shard_map/ppermute | solution.py:23
  151.0 3.2 %collective-permute-start.10 = (bf16[640,512]{1,0:T(8,128)(2,1)}, bf16[640,512]{1,0:T(8,128)(2,1)S(1)}, u32[]{:S(2)}, u32[]{:S(2)}) collective-permute-start(bf16[640,512]{1,0:T(8,128)(2,1)} %get-tuple-element.45), channel_id=1, source_target_pairs={{0,192},{8,200},{16,208},{24,216},{32,224},{40,232},{48,240},{56,2... | collective-permute-start | bytes 1966088 | tf_op jit(solution)/shard_map/ppermute | solution.py:23
  154.2 12.2 %collective-permute-done.11 = bf16[640,512]{1,0:T(8,128)(2,1)S(1)} collective-permute-done((bf16[640,512]{1,0:T(8,128)(2,1)}, bf16[640,512]{1,0:T(8,128)(2,1)S(1)}, u32[]{:S(2)}, u32[]{:S(2)}) %collective-permute-start.11) | collective-permute-done | bytes 655392 | tf_op jit(solution)/shard_map/ppermute | solution.py:23
  166.4 1.3 add_convert_fusion.2
  167.7 3.7 %collective-permute-start.12 = (bf16[640,512]{1,0:T(8,128)(2,1)S(1)}, bf16[640,512]{1,0:T(8,128)(2,1)S(1)}, u32[]{:S(2)}, u32[]{:S(2)}) collective-permute-start(bf16[640,512]{1,0:T(8,128)(2,1)S(1)} %add_convert_fusion.2), channel_id=1, source_target_pairs={{0,192},{8,200},{16,208},{24,216},{32,224},{40,232},{48,240},{56,2... | collective-permute-start | bytes 1966088 | tf_op jit(solution)/shard_map/ppermute | solution.py:23
  171.7 13.4 %shard_map.120 = (bf16[4,8,128,256]{3,2,1,0:T(8,128)(2,1)}, bf16[4,8,128,256]{3,2,1,0:T(8,128)(2,1)}, bf16[256,4096]{1,0:T(8,128)(2,1)}) custom-call(s32[1]{0:T(128)} %bitcast.3.x_ref, bf16[640,4096]{1,0:T(8,128)(2,1)} %all-gather.2.cloned.1.call-done.tok_ref.refs_0_, bf16[640,256]{1,0:T(8,128)(2,1)S(1)} %get-tuple-element.54.refs_1_, ...), custom_call_target="tpu_custom_call" | custom-call | tf_op jit(solution)/shard_map/pallas_call | solution.py:234
  185.1 8.1 %collective-permute-done.12 = bf16[640,512]{1,0:T(8,128)(2,1)S(1)} collective-permute-done((bf16[640,512]{1,0:T(8,128)(2,1)S(1)}, bf16[640,512]{1,0:T(8,128)(2,1)S(1)}, u32[]{:S(2)}, u32[]{:S(2)}) %collective-permute-start.12) | collective-permute-done | bytes 655392 | tf_op jit(solution)/shard_map/ppermute | solution.py:23
  193.2 3.4 %collective-permute-done.8 = bf16[640,512]{1,0:T(8,128)(2,1)S(1)} collective-permute-done((bf16[640,512]{1,0:T(8,128)(2,1)S(1)}, bf16[640,512]{1,0:T(8,128)(2,1)S(1)}, u32[]{:S(2)}, u32[]{:S(2)}) %collective-permute-start.8) | collective-permute-done | bytes 655392 | tf_op jit(solution)/shard_map/ppermute | solution.py:23
  197.2 1.3 pad_maximum_fusion
  198.5 4.8 %all-to-all-start.2 = ((bf16[8,80,1024]{2,1,0:T(8,128)(2,1)}), bf16[8,80,1024]{2,1,0:T(8,128)(2,1)S(1)}, u32[]{:S(2)}, u32[]{:S(2)}) async-start(bf16[8,80,1024]{2,1,0:T(8,128)(2,1)} %bitcast.30), calls=%async_computation.2 | async-start | bytes 2621440 | tf_op jit(solution)/shard_map/all_to_all | solution.py:288
  203.3 9.5 %reduce-scatter.2.cloned.1.call-done = bf16[648,512]{1,0:T(8,128)(2,1)} async-done(((bf16[5184,512]{1,0:T(8,128)(2,1)}), bf16[648,512]{1,0:T(8,128)(2,1)}) %reduce-scatter.2.cloned.1.call-update) | async-done | bytes 663568 | tf_op jit(solution)/shard_map/reduce_scatter | solution.py:363
  212.8 0.8 slice.54
  213.9 0.9 fusion.1
  214.8 5.8 %all-to-all-done.2 = bf16[8,80,1024]{2,1,0:T(8,128)(2,1)S(1)} async-done(((bf16[8,80,1024]{2,1,0:T(8,128)(2,1)}), bf16[8,80,1024]{2,1,0:T(8,128)(2,1)S(1)}, u32[]{:S(2)}, u32[]{:S(2)}) %all-to-all-start.2) | async-done | bytes 1310752 | tf_op jit(solution)/shard_map/all_to_all | solution.py:288
  220.6 4.9 %all-to-all-start.3 = ((bf16[8,88,512]{2,1,0:T(8,128)(2,1)}), bf16[8,88,512]{2,1,0:T(8,128)(2,1)S(1)}, u32[]{:S(2)}, u32[]{:S(2)}) async-start(bf16[8,88,512]{2,1,0:T(8,128)(2,1)} %fusion.1), calls=%async_computation.4 | async-start | bytes 1441792 | tf_op jit(solution)/shard_map/all_to_all | solution.py:288
  225.5 11.0 %all-to-all-done.3 = bf16[8,88,512]{2,1,0:T(8,128)(2,1)S(1)} async-done(((bf16[8,88,512]{2,1,0:T(8,128)(2,1)}), bf16[8,88,512]{2,1,0:T(8,128)(2,1)S(1)}, u32[]{:S(2)}, u32[]{:S(2)}) %all-to-all-start.3) | async-done | bytes 720928 | tf_op jit(solution)/shard_map/all_to_all | solution.py:288
  237.5 1.2 fusion.4
  238.8 2.3 gather_fusion
  241.1 0.7 copy.49
  242.2 2.3 fusion.2
  244.6 3.2 %collective-permute-start.19 = (bf16[256,128]{1,0:T(8,128)(2,1)S(1)}, bf16[256,128]{1,0:T(8,128)(2,1)S(1)}, u32[]{:S(2)}, u32[]{:S(2)}) collective-permute-start(bf16[256,128]{1,0:T(8,128)(2,1)S(1)} %get-tuple-element.79), channel_id=1, source_target_pairs={{0,32},{8,40},{16,48},{24,56},{32,0},{40,8},{48,16},{56,24},{64,96... | collective-permute-start | bytes 196616 | tf_op jit(solution)/shard_map/ppermute | solution.py:18
  247.7 1.6 collective-permute-start.20
  249.3 3.5 %collective-permute-start.21 = (bf16[256,128]{1,0:T(8,128)(2,1)S(1)}, bf16[256,128]{1,0:T(8,128)(2,1)S(1)}, u32[]{:S(2)}, u32[]{:S(2)}) collective-permute-start(bf16[256,128]{1,0:T(8,128)(2,1)S(1)} %get-tuple-element.84), channel_id=1, source_target_pairs={{0,40},{8,48},{16,56},{24,0},{32,8},{40,16},{48,24},{56,32},{64,10... | collective-permute-start | bytes 196616 | tf_op jit(solution)/shard_map/ppermute | solution.py:18
  252.8 1.5 collective-permute-start.22
  254.2 2.7 collective-permute-start.23
  257.0 1.5 collective-permute-start.24
  258.5 1.0 collective-permute-done.20
  259.5 0.8 collective-permute-start.25
  260.5 1.7 collective-permute-start.27
  262.2 1.6 collective-permute-start.28
  263.8 0.7 fusion.16
  264.5 2.1 collective-permute-done.26
  266.7 0.9 collective-permute-done.28
  (111 shorter events, 6.6 us)
Async XLA Ops:
  7.2 12.4 %copy-start.15 = (bf16[256,128]{1,0:T(8,128)(2,1)S(1)}, bf16[256,128]{1,0:T(8,128)(2,1)}, u32[]{:S(2)}) copy-start(bf16[256,128]{1,0:T(8,128)(2,1)} %param.13) | copy-start | bytes 196612
  7.2 11.5 %copy-start.14 = (bf16[256,128]{1,0:T(8,128)(2,1)S(1)}, bf16[256,128]{1,0:T(8,128)(2,1)}, u32[]{:S(2)}) copy-start(bf16[256,128]{1,0:T(8,128)(2,1)} %param.7) | copy-start | bytes 196612
  7.2 12.4 %collective-permute-start = (bf16[256,128]{1,0:T(8,128)(2,1)}, bf16[256,128]{1,0:T(8,128)(2,1)S(1)}, u32[]{:S(2)}, u32[]{:S(2)}) collective-permute-start(bf16[256,128]{1,0:T(8,128)(2,1)} %param.13), channel_id=1, source_target_pairs={{0,8},{8,16},{16,24},{24,32},{32,40},{40,48},{48,56},{56,0},{64,72... | collective-permute-start | bytes 196616 | tf_op jit(solution)/shard_map/ppermute | solution.py:18
  9.2 10.4 %collective-permute-start.1 = (bf16[256,128]{1,0:T(8,128)(2,1)}, bf16[256,128]{1,0:T(8,128)(2,1)S(1)}, u32[]{:S(2)}, u32[]{:S(2)}) collective-permute-start(bf16[256,128]{1,0:T(8,128)(2,1)} %param.13), channel_id=1, source_target_pairs={{0,56},{8,0},{16,8},{24,16},{32,24},{40,32},{48,40},{56,48},{64,12... | collective-permute-start | bytes 196616 | tf_op jit(solution)/shard_map/ppermute | solution.py:18
  18.7 29.7 %copy-start.10 = (bf16[640,256]{1,0:T(8,128)(2,1)}, bf16[640,256]{1,0:T(8,128)(2,1)S(1)}, u32[]{:S(2)}) copy-start(bf16[640,256]{1,0:T(8,128)(2,1)S(1)} %get-tuple-element.72) | copy-start | bytes 983044
  19.6 15.3 %collective-permute-start.2 = (bf16[3,256,128]{2,1,0:T(8,128)(2,1)S(1)}, bf16[3,256,128]{2,1,0:T(8,128)(2,1)S(1)}, u32[]{:S(2)}, u32[]{:S(2)}) collective-permute-start(bf16[3,256,128]{2,1,0:T(8,128)(2,1)S(1)} %pad_maximum_fusion.3), channel_id=1, source_target_pairs={{0,24},{8,32},{16,40},{24,48},{32,56},{40,0},{48,8},{56,16},{64,88... | collective-permute-start | bytes 589832 | tf_op jit(solution)/shard_map/ppermute | solution.py:18
  21.5 12.6 %all-to-all-start = ((bf16[8,80,128]{2,1,0:T(8,128)(2,1)}), bf16[8,80,128]{2,1,0:T(8,128)(2,1)S(1)}, u32[]{:S(2)}, u32[]{:S(2)}) async-start(bf16[8,80,128]{2,1,0:T(8,128)(2,1)} %bitcast.7), calls=%async_computation | async-start | bytes 327680 | tf_op jit(solution)/shard_map/all_to_all | solution.py:288
  26.4 89.8 %all-gather.2.cloned.1.call-start = ((), (), s32[]{:S(2)}) async-start(), calls=%async_computation.5 | async-start | bytes 5898240 | tf_op jit(solution)/shard_map/all_gather | solution.py:301
  26.4 7.6 %collective-permute-start.3 = (bf16[2,256,128]{2,1,0:T(8,128)(2,1)S(1)}, bf16[2,256,128]{2,1,0:T(8,128)(2,1)S(1)}, u32[]{:S(2)}, u32[]{:S(2)}) collective-permute-start(bf16[2,256,128]{2,1,0:T(8,128)(2,1)S(1)} %slice.38), channel_id=1, source_target_pairs={{0,40},{8,48},{16,56},{24,0},{32,8},{40,16},{48,24},{56,32},{64,10... | collective-permute-start | bytes 393224 | tf_op jit(solution)/shard_map/ppermute | solution.py:18
  34.9 7.3 %collective-permute-start.4 = (bf16[640,128]{1,0:T(8,128)(2,1)S(1)}, bf16[640,128]{1,0:T(8,128)(2,1)S(1)}, u32[]{:S(2)}, u32[]{:S(2)}) collective-permute-start(bf16[640,128]{1,0:T(8,128)(2,1)S(1)} %bitcast.141), channel_id=1, source_target_pairs={{0,64},{8,72},{16,80},{24,88},{32,96},{40,104},{48,112},{56,120},{... | collective-permute-start | bytes 491528 | tf_op jit(solution)/shard_map/ppermute | solution.py:23
  36.4 10.3 %collective-permute-start.5 = (bf16[640,128]{1,0:T(8,128)(2,1)S(1)}, bf16[640,128]{1,0:T(8,128)(2,1)S(1)}, u32[]{:S(2)}, u32[]{:S(2)}) collective-permute-start(bf16[640,128]{1,0:T(8,128)(2,1)S(1)} %bitcast.142), channel_id=1, source_target_pairs={{0,128},{8,136},{16,144},{24,152},{32,160},{40,168},{48,176},{56,1... | collective-permute-start | bytes 491528 | tf_op jit(solution)/shard_map/ppermute | solution.py:23
  39.1 7.6 %collective-permute-start.6 = (bf16[640,128]{1,0:T(8,128)(2,1)S(1)}, bf16[640,128]{1,0:T(8,128)(2,1)S(1)}, u32[]{:S(2)}, u32[]{:S(2)}) collective-permute-start(bf16[640,128]{1,0:T(8,128)(2,1)S(1)} %bitcast.143), channel_id=1, source_target_pairs={{0,192},{8,200},{16,208},{24,216},{32,224},{40,232},{48,240},{56,2... | collective-permute-start | bytes 491528 | tf_op jit(solution)/shard_map/ppermute | solution.py:23
  47.8 165.0 %reduce-scatter.2.cloned.1.call-start = ((), (), s32[]{:S(2)}) async-start(), calls=%async_computation.6 | async-start | bytes 5971968 | tf_op jit(solution)/shard_map/reduce_scatter | solution.py:363
  71.2 18.9 %collective-permute-start.13 = (bf16[640,512]{1,0:T(8,128)(2,1)S(1)}, bf16[640,512]{1,0:T(8,128)(2,1)S(1)}, u32[]{:S(2)}, u32[]{:S(2)}) collective-permute-start(bf16[640,512]{1,0:T(8,128)(2,1)S(1)} %get-tuple-element.78.refs_0_.refs_4_), channel_id=1, source_target_pairs={{0,64},{8,72},{16,80},{24,88},{32,96},{40,104},{48,112},{56,120},{... | collective-permute-start | bytes 1966088 | tf_op jit(solution)/shard_map/ppermute | solution.py:23
  72.6 17.8 %collective-permute-start.16 = (bf16[640,512]{1,0:T(8,128)(2,1)S(1)}, bf16[640,512]{1,0:T(8,128)(2,1)}, u32[]{:S(2)}, u32[]{:S(2)}) collective-permute-start(bf16[640,512]{1,0:T(8,128)(2,1)S(1)} %get-tuple-element.77.refs_1_.refs_5_), channel_id=1, source_target_pairs={{0,192},{8,200},{16,208},{24,216},{32,224},{40,232},{48,240},{56,2... | collective-permute-start | bytes 1966088 | tf_op jit(solution)/shard_map/ppermute | solution.py:23
  74.5 58.0 %collective-permute-start.14 = (bf16[640,512]{1,0:T(8,128)(2,1)S(1)}, bf16[640,512]{1,0:T(8,128)(2,1)S(1)}, u32[]{:S(2)}, u32[]{:S(2)}) collective-permute-start(bf16[640,512]{1,0:T(8,128)(2,1)S(1)} %get-tuple-element.77.refs_1_.refs_5_), channel_id=1, source_target_pairs={{0,64},{8,72},{16,80},{24,88},{32,96},{40,104},{48,112},{56,120},{... | collective-permute-start | bytes 1966088 | tf_op jit(solution)/shard_map/ppermute | solution.py:23
  74.6 57.9 %collective-permute-start.18 = (bf16[640,512]{1,0:T(8,128)(2,1)S(1)}, bf16[640,512]{1,0:T(8,128)(2,1)}, u32[]{:S(2)}, u32[]{:S(2)}) collective-permute-start(bf16[640,512]{1,0:T(8,128)(2,1)S(1)} %get-tuple-element.78.refs_0_.refs_4_), channel_id=1, source_target_pairs={{0,192},{8,200},{16,208},{24,216},{32,224},{40,232},{48,240},{56,2... | collective-permute-start | bytes 1966088 | tf_op jit(solution)/shard_map/ppermute | solution.py:23
  90.1 42.4 %collective-permute-start.15 = (bf16[640,512]{1,0:T(8,128)(2,1)S(1)}, bf16[640,512]{1,0:T(8,128)(2,1)}, u32[]{:S(2)}, u32[]{:S(2)}) collective-permute-start(bf16[640,512]{1,0:T(8,128)(2,1)S(1)} %collective-permute-done.13.refs_2_.refs_6_), channel_id=1, source_target_pairs={{0,64},{8,72},{16,80},{24,88},{32,96},{40,104},{48,112},{56,120},{... | collective-permute-start | bytes 1966088 | tf_op jit(solution)/shard_map/ppermute | solution.py:23
  90.4 42.2 %collective-permute-start.17 = (bf16[640,512]{1,0:T(8,128)(2,1)}, bf16[640,512]{1,0:T(8,128)(2,1)}, u32[]{:S(2)}, u32[]{:S(2)}) collective-permute-start(bf16[640,512]{1,0:T(8,128)(2,1)} %collective-permute-done.16.refs_7_.refs_11_), channel_id=1, source_target_pairs={{0,192},{8,200},{16,208},{24,216},{32,224},{40,232},{48,240},{56,2... | collective-permute-start | bytes 1966088 | tf_op jit(solution)/shard_map/ppermute | solution.py:23
  130.0 0.8 copy-start
  130.8 0.8 copy-start.1
  131.6 0.9 copy-start.6
  132.5 14.9 %copy-start.2 = (bf16[640,512]{1,0:T(8,128)(2,1)}, bf16[640,512]{1,0:T(8,128)(2,1)S(1)}, u32[]{:S(2)}) copy-start(bf16[640,512]{1,0:T(8,128)(2,1)S(1)} %get-tuple-element.41) | copy-start | bytes 1966084
  132.5 14.9 %copy-start.4 = (bf16[640,512]{1,0:T(8,128)(2,1)}, bf16[640,512]{1,0:T(8,128)(2,1)S(1)}, u32[]{:S(2)}) copy-start(bf16[640,512]{1,0:T(8,128)(2,1)S(1)} %get-tuple-element.61) | copy-start | bytes 1966084
  147.4 0.7 copy-start.8
  148.2 23.2 %copy-start.7 = (bf16[640,512]{1,0:T(8,128)(2,1)S(1)}, bf16[640,512]{1,0:T(8,128)(2,1)}, u32[]{:S(2)}) copy-start(bf16[640,512]{1,0:T(8,128)(2,1)} %copy-done.6) | copy-start | bytes 1966084
  148.2 18.2 %collective-permute-start.11 = (bf16[640,512]{1,0:T(8,128)(2,1)}, bf16[640,512]{1,0:T(8,128)(2,1)S(1)}, u32[]{:S(2)}, u32[]{:S(2)}) collective-permute-start(bf16[640,512]{1,0:T(8,128)(2,1)} %get-tuple-element.47), channel_id=1, source_target_pairs={{0,192},{8,200},{16,208},{24,216},{32,224},{40,232},{48,240},{56,2... | collective-permute-start | bytes 1966088 | tf_op jit(solution)/shard_map/ppermute | solution.py:23
  151.0 20.4 %collective-permute-start.7 = (bf16[640,512]{1,0:T(8,128)(2,1)}, bf16[640,512]{1,0:T(8,128)(2,1)S(1)}, u32[]{:S(2)}, u32[]{:S(2)}) collective-permute-start(bf16[640,512]{1,0:T(8,128)(2,1)} %get-tuple-element.43), channel_id=1, source_target_pairs={{0,64},{8,72},{16,80},{24,88},{32,96},{40,104},{48,112},{56,120},{... | collective-permute-start | bytes 1966088 | tf_op jit(solution)/shard_map/ppermute | solution.py:23
  151.0 34.1 %collective-permute-start.10 = (bf16[640,512]{1,0:T(8,128)(2,1)}, bf16[640,512]{1,0:T(8,128)(2,1)S(1)}, u32[]{:S(2)}, u32[]{:S(2)}) collective-permute-start(bf16[640,512]{1,0:T(8,128)(2,1)} %get-tuple-element.45), channel_id=1, source_target_pairs={{0,192},{8,200},{16,208},{24,216},{32,224},{40,232},{48,240},{56,2... | collective-permute-start | bytes 1966088 | tf_op jit(solution)/shard_map/ppermute | solution.py:23
  154.2 30.9 %collective-permute-start.9 = (bf16[640,512]{1,0:T(8,128)(2,1)}, bf16[640,512]{1,0:T(8,128)(2,1)S(1)}, u32[]{:S(2)}, u32[]{:S(2)}) collective-permute-start(bf16[640,512]{1,0:T(8,128)(2,1)} %get-tuple-element.44), channel_id=1, source_target_pairs={{0,64},{8,72},{16,80},{24,88},{32,96},{40,104},{48,112},{56,120},{... | collective-permute-start | bytes 1966088 | tf_op jit(solution)/shard_map/ppermute | solution.py:23
  167.7 3.9 %copy-start.9 = (bf16[640,256]{1,0:T(8,128)(2,1)S(1)}, bf16[640,256]{1,0:T(8,128)(2,1)}, u32[]{:S(2)}) copy-start(bf16[640,256]{1,0:T(8,128)(2,1)} %copy-done.8) | copy-start | bytes 983044
  167.7 25.5 %collective-permute-start.12 = (bf16[640,512]{1,0:T(8,128)(2,1)S(1)}, bf16[640,512]{1,0:T(8,128)(2,1)S(1)}, u32[]{:S(2)}, u32[]{:S(2)}) collective-permute-start(bf16[640,512]{1,0:T(8,128)(2,1)S(1)} %add_convert_fusion.2), channel_id=1, source_target_pairs={{0,192},{8,200},{16,208},{24,216},{32,224},{40,232},{48,240},{56,2... | collective-permute-start | bytes 1966088 | tf_op jit(solution)/shard_map/ppermute | solution.py:23
  171.6 25.1 %collective-permute-start.8 = (bf16[640,512]{1,0:T(8,128)(2,1)S(1)}, bf16[640,512]{1,0:T(8,128)(2,1)S(1)}, u32[]{:S(2)}, u32[]{:S(2)}) collective-permute-start(bf16[640,512]{1,0:T(8,128)(2,1)S(1)} %add_convert_fusion.3), channel_id=1, source_target_pairs={{0,64},{8,72},{16,80},{24,88},{32,96},{40,104},{48,112},{56,120},{... | collective-permute-start | bytes 1966088 | tf_op jit(solution)/shard_map/ppermute | solution.py:23
  171.7 25.0 %copy-start.3 = (bf16[640,512]{1,0:T(8,128)(2,1)S(1)}, bf16[640,512]{1,0:T(8,128)(2,1)}, u32[]{:S(2)}) copy-start(bf16[640,512]{1,0:T(8,128)(2,1)} %copy-done.2) | copy-start | bytes 1966084
  171.7 25.0 %copy-start.5 = (bf16[640,512]{1,0:T(8,128)(2,1)S(1)}, bf16[640,512]{1,0:T(8,128)(2,1)}, u32[]{:S(2)}) copy-start(bf16[640,512]{1,0:T(8,128)(2,1)} %copy-done.4) | copy-start | bytes 1966084
  198.5 22.1 %all-to-all-start.2 = ((bf16[8,80,1024]{2,1,0:T(8,128)(2,1)}), bf16[8,80,1024]{2,1,0:T(8,128)(2,1)S(1)}, u32[]{:S(2)}, u32[]{:S(2)}) async-start(bf16[8,80,1024]{2,1,0:T(8,128)(2,1)} %bitcast.30), calls=%async_computation.2 | async-start | bytes 2621440 | tf_op jit(solution)/shard_map/all_to_all | solution.py:288
  212.8 1.1 slice-start
  220.6 15.9 %all-to-all-start.3 = ((bf16[8,88,512]{2,1,0:T(8,128)(2,1)}), bf16[8,88,512]{2,1,0:T(8,128)(2,1)S(1)}, u32[]{:S(2)}, u32[]{:S(2)}) async-start(bf16[8,88,512]{2,1,0:T(8,128)(2,1)} %fusion.1), calls=%async_computation.4 | async-start | bytes 1441792 | tf_op jit(solution)/shard_map/all_to_all | solution.py:288
  236.5 1.0 copy-start.11
  241.1 1.1 copy-start.12
  242.2 14.7 %copy-start.13 = (f32[256,4,128]{2,0,1:T(8,128)S(1)}, f32[256,4,128]{2,0,1:T(8,128)}, u32[]{:S(2)}) copy-start(f32[256,4,128]{2,0,1:T(8,128)} %fusion.4) | copy-start | bytes 1572868
  244.6 23.7 %copy-start.16 = (f32[256,2]{0,1:T(2,128)S(1)}, f32[256,2]{0,1:T(2,128)}, u32[]{:S(2)}) copy-start(f32[256,2]{0,1:T(2,128)} %param.9) | copy-start | bytes 6148
  244.6 12.4 %collective-permute-start.19 = (bf16[256,128]{1,0:T(8,128)(2,1)S(1)}, bf16[256,128]{1,0:T(8,128)(2,1)S(1)}, u32[]{:S(2)}, u32[]{:S(2)}) collective-permute-start(bf16[256,128]{1,0:T(8,128)(2,1)S(1)} %get-tuple-element.79), channel_id=1, source_target_pairs={{0,32},{8,40},{16,48},{24,56},{32,0},{40,8},{48,16},{56,24},{64,96... | collective-permute-start | bytes 196616 | tf_op jit(solution)/shard_map/ppermute | solution.py:18
  247.7 11.8 %collective-permute-start.20 = (bf16[256,128]{1,0:T(8,128)(2,1)S(1)}, bf16[256,128]{1,0:T(8,128)(2,1)S(1)}, u32[]{:S(2)}, u32[]{:S(2)}) collective-permute-start(bf16[256,128]{1,0:T(8,128)(2,1)S(1)} %get-tuple-element.85), channel_id=1, source_target_pairs={{0,24},{8,32},{16,40},{24,48},{32,56},{40,0},{48,8},{56,16},{64,88... | collective-permute-start | bytes 196616 | tf_op jit(solution)/shard_map/ppermute | solution.py:18
  249.3 11.0 %collective-permute-start.21 = (bf16[256,128]{1,0:T(8,128)(2,1)S(1)}, bf16[256,128]{1,0:T(8,128)(2,1)S(1)}, u32[]{:S(2)}, u32[]{:S(2)}) collective-permute-start(bf16[256,128]{1,0:T(8,128)(2,1)S(1)} %get-tuple-element.84), channel_id=1, source_target_pairs={{0,40},{8,48},{16,56},{24,0},{32,8},{40,16},{48,24},{56,32},{64,10... | collective-permute-start | bytes 196616 | tf_op jit(solution)/shard_map/ppermute | solution.py:18
  252.8 7.7 %collective-permute-start.22 = (bf16[256,128]{1,0:T(8,128)(2,1)S(1)}, bf16[256,128]{1,0:T(8,128)(2,1)S(1)}, u32[]{:S(2)}, u32[]{:S(2)}) collective-permute-start(bf16[256,128]{1,0:T(8,128)(2,1)S(1)} %get-tuple-element.83), channel_id=1, source_target_pairs={{0,16},{8,24},{16,32},{24,40},{32,48},{40,56},{48,0},{56,8},{64,80... | collective-permute-start | bytes 196616 | tf_op jit(solution)/shard_map/ppermute | solution.py:18
  254.2 7.9 %collective-permute-start.23 = (bf16[256,128]{1,0:T(8,128)(2,1)S(1)}, bf16[256,128]{1,0:T(8,128)(2,1)S(1)}, u32[]{:S(2)}, u32[]{:S(2)}) collective-permute-start(bf16[256,128]{1,0:T(8,128)(2,1)S(1)} %get-tuple-element.82), channel_id=1, source_target_pairs={{0,48},{8,56},{16,0},{24,8},{32,16},{40,24},{48,32},{56,40},{64,11... | collective-permute-start | bytes 196616 | tf_op jit(solution)/shard_map/ppermute | solution.py:18
  257.0 6.7 %collective-permute-start.24 = (bf16[256,128]{1,0:T(8,128)(2,1)S(1)}, bf16[256,128]{1,0:T(8,128)(2,1)S(1)}, u32[]{:S(2)}, u32[]{:S(2)}) collective-permute-start(bf16[256,128]{1,0:T(8,128)(2,1)S(1)} %get-tuple-element.81), channel_id=1, source_target_pairs={{0,8},{8,16},{16,24},{24,32},{32,40},{40,48},{48,56},{56,0},{64,72... | collective-permute-start | bytes 196616 | tf_op jit(solution)/shard_map/ppermute | solution.py:18
  259.5 4.3 %collective-permute-start.25 = (bf16[256,128]{1,0:T(8,128)(2,1)S(1)}, bf16[256,128]{1,0:T(8,128)(2,1)S(1)}, u32[]{:S(2)}, u32[]{:S(2)}) collective-permute-start(bf16[256,128]{1,0:T(8,128)(2,1)S(1)} %get-tuple-element.80), channel_id=1, source_target_pairs={{0,56},{8,0},{16,8},{24,16},{32,24},{40,32},{48,40},{56,48},{64,12... | collective-permute-start | bytes 196616 | tf_op jit(solution)/shard_map/ppermute | solution.py:18
  260.3 6.3 %collective-permute-start.26 = (bf16[264,128]{1,0:T(8,128)(2,1)S(1)}, bf16[264,128]{1,0:T(8,128)(2,1)S(1)}, u32[]{:S(2)}, u32[]{:S(2)}) collective-permute-start(bf16[264,128]{1,0:T(8,128)(2,1)S(1)} %get-tuple-element.93), channel_id=1, source_target_pairs={{0,64},{8,72},{16,80},{24,88},{32,96},{40,104},{48,112},{56,120},{... | collective-permute-start | bytes 202760 | tf_op jit(solution)/shard_map/ppermute | solution.py:23
  260.5 6.2 %collective-permute-start.27 = (bf16[264,128]{1,0:T(8,128)(2,1)S(1)}, bf16[264,128]{1,0:T(8,128)(2,1)S(1)}, u32[]{:S(2)}, u32[]{:S(2)}) collective-permute-start(bf16[264,128]{1,0:T(8,128)(2,1)S(1)} %get-tuple-element.94), channel_id=1, source_target_pairs={{0,128},{8,136},{16,144},{24,152},{32,160},{40,168},{48,176},{56,1... | collective-permute-start | bytes 202760 | tf_op jit(solution)/shard_map/ppermute | solution.py:23
  262.2 5.3 %collective-permute-start.28 = (bf16[264,128]{1,0:T(8,128)(2,1)S(1)}, bf16[264,128]{1,0:T(8,128)(2,1)S(1)}, u32[]{:S(2)}, u32[]{:S(2)}) collective-permute-start(bf16[264,128]{1,0:T(8,128)(2,1)S(1)} %get-tuple-element.95), channel_id=1, source_target_pairs={{0,192},{8,200},{16,208},{24,216},{32,224},{40,232},{48,240},{56,2... | collective-permute-start | bytes 202760 | tf_op jit(solution)/shard_map/ppermute | solution.py:23
Sparse Core Ops, SparseCore 0:
  47.9 68.2 all-gather.1
  148.3 64.4 reduce-scatter.1
where the time goes:
time: 278 us; the launch traced here: 276 us
  waiting for transfers between devices  101 us (36%)
  starting transfers between devices  69.1 us (25%)
  Pallas kernels  42.1 us (15%)
  blocking collectives  22.2 us (8%)
  between operations  14.6 us (5%)
  other arithmetic  11.2 us (4%)
  local copies, waits for them, and re-layouts  10.8 us (4%)
  matrix products  4.91 us (2%)
    ppermute x18, waiting for transfers between devices, shift_x(): return lax.ppermute(value, 'section', pairs)  45.4 us
    pallas_call x3, Pallas kernels, call(): pl.pallas_call(kernel, grid_spec=pltpu.PrefetchScalarGridSpec(num_scalar_...  42.1 us
    ppermute x18, starting transfers between devices, shift_x(): return lax.ppermute(value, 'section', pairs)  28.6 us
    ppermute x11, starting transfers between devices, shift_z(): return lax.ppermute(value, 'section', pairs)  25.9 us
    all_gather x1, waiting for transfers between devices, per_device(): lax.all_gather(tok_x, 'section', axis_index_groups=Z_GROUPS, axis=1, tile...  22.7 us
    all_to_all x1, blocking collectives, exchange(): lax.all_to_all(value.reshape(experts, -1, value.shape[-1]), 'expert', spl...  22.2 us
    all_to_all x3, waiting for transfers between devices, exchange(): lax.all_to_all(value.reshape(experts, -1, value.shape[-1]), 'expert', spl...  16.8 us
    all_to_all x3, starting transfers between devices, exchange(): lax.all_to_all(value.reshape(experts, -1, value.shape[-1]), 'expert', spl...  14.6 us
  transfers between devices with their start and end apart: 34, of which 16 were waited for; matrix products, arithmetic and copies ran while one was open for 5% of the time, Pallas kernels for 10%

commit v1 on v0

--- a/solution.py
+++ b/solution.py
@@ -68,8 +68,8 @@
     return [(a, b), (below_a, below_b), (far_a, far_b), (above_a, above_b)]
 
 
-def ring_scatter_x(parts):
-    far_a, far_b = shift_x(parts[2][0], 1), shift_x(parts[2][1], -1)
+def ring_scatter_x(parts, far):
+    far_a, far_b = far
     below_b, above_a = shift_x(parts[1][1], 1), shift_x(parts[3][0], -1)
     next_a = (parts[1][0].astype(f32) + far_a.astype(f32)).astype(bf16)
     next_b = (parts[3][1].astype(f32) + far_b.astype(f32)).astype(bf16)
@@ -249,18 +249,20 @@
 def slot_tables(route_rows, mix_rows, capacity, experts):
     tok_count, top_count = route_rows.shape
     flat_routes = route_rows.reshape(-1)
-    onehot = (flat_routes[:, None] == jnp.arange(experts, dtype=jnp.int32)[None, :]).astype(
-        jnp.int32
-    )
-    earlier = jnp.cumsum(onehot, axis=0) - onehot
-    position = jnp.sum(earlier * onehot, axis=1)
+    onehot = flat_routes[:, None] == jnp.arange(experts, dtype=jnp.int32)[None, :]
+    count = tok_count * top_count
+    pairs = jnp.arange(count, dtype=jnp.int32)
+    before = (pairs[None, :] < pairs[:, None]).astype(bf16)
+    earlier = jnp.dot(before, onehot.astype(bf16), preferred_element_type=f32)
+    position = jnp.sum(jnp.where(onehot, earlier, 0.0), axis=1).astype(jnp.int32)
     target = (flat_routes * capacity + position).reshape(tok_count, top_count)
     slot_ids = jnp.arange(experts * capacity, dtype=jnp.int32)
-    hits = target[None, :, :] == slot_ids[:, None, None]
+    hits = target.T[None, :, :] == slot_ids[:, None, None]
     matches = hits.astype(f32)
-    select = jnp.sum(matches, axis=2)
-    weighted = jnp.sum(matches * mix_rows[None, :, :], axis=2)
-    return (target, select, weighted)
+    select = jnp.sum(matches, axis=1)
+    weighted = jnp.sum(matches * mix_rows.T[None, :, :], axis=1)
+    picks = matches.astype(bf16).reshape(experts * capacity, -1)
+    return (select.astype(bf16), weighted, picks)
 
 
 def per_device(tokens, routes, mix_weights, w_gate, w_up, w_down, upstream):
@@ -280,9 +282,8 @@
     down = w_down[0]
 
     up_near = near_z(upstream)
-    target, select, weighted = slot_tables(routes, mix_weights, capacity, experts)
+    select_low, weighted, picks = slot_tables(routes, mix_weights, capacity, experts)
     slot_scale = jnp.sum(weighted, axis=1)
-    select_low = select.astype(bf16)
 
     def exchange(value):
         return lax.all_to_all(
@@ -335,7 +336,8 @@
         (where, dispatched, gate4, up4, down),
     )
 
-    sent_x = ring_scatter_x([(outs[2 * d], outs[2 * d + 1]) for d in range(NX)])
+    outs = [(outs[2 * d], outs[2 * d + 1]) for d in range(NX)]
+    far = shift_x(outs[2][0], 1), shift_x(outs[2][1], -1)
 
     back, gate_act, up_act = call(
         backward_kernel,
@@ -360,6 +362,9 @@
         (where, *ups, down, gate4, up4, coef, silu_gate, hidden),
     )
 
+    back, far = lax.optimization_barrier((back, far))
+    sent_x = ring_scatter_x(outs, far)
+
     back_z = lax.psum_scatter(
         back.reshape(NZ * (rows + 8), wide_x),
         "section",
@@ -385,7 +390,7 @@
 
     summed = jnp.concatenate(
         [
-            (outs[h].astype(f32) + sent_x[0][h].astype(f32) + sent_x[1][h].astype(f32)).astype(bf16)
+            (outs[0][h].astype(f32) + sent_x[0][h].astype(f32) + sent_x[1][h].astype(f32)).astype(bf16)
             for h in range(2)
         ],
         axis=1,
@@ -397,13 +402,13 @@
     back = exchange(
         jnp.concatenate([back_z[:rows].reshape(experts, capacity, wide_x), mix], axis=1)
     ).reshape(experts, capacity + 8, wide_x)
-    returned, back = lax.optimization_barrier((returned, back))
-
     moe_out = jnp.dot(weighted.T, returned.astype(f32), precision=highest)
     mixed = (tokens.astype(f32) + spread_z(moe_out, my_z)).astype(bf16)
+    mixed, back = lax.optimization_barrier((mixed, back))
+
     grad_moe = dot_tn(select_low, back[:, :capacity].reshape(rows, wide_x))
-    mix = jnp.sum(back[:, capacity : capacity + 2, :capacity].astype(f32), axis=1)
-    mix = mix.reshape(-1)[target.T].reshape(-1, feat)
+    mix = back[:, capacity : capacity + 2, :capacity].transpose(1, 0, 2).reshape(2, rows)
+    mix = jnp.sum(jnp.dot(mix, picks, preferred_element_type=f32), axis=0).reshape(-1, feat)
     grad_moe, mix = spread_x(grad_moe, jnp.concatenate(high_low(mix)), my_x)
     grad_tokens = (upstream.astype(f32) + grad_moe).astype(bf16)
     mix = jnp.sum(mix.reshape(2, top_count, tok_count), axis=0)

time: 278 us -> 265 us (0.953)
  waiting for transfers between devices: 101 us -> 90.2 us
    ppermute x18, waiting for transfers between devices: 45.4 us -> 31.9 us  [shift_x(): return lax.ppermute(value, 'section', pairs)]
    ppermute x11, waiting for transfers between devices: 6.2 us -> 9.94 us  [shift_z(): return lax.ppermute(value, 'section', pairs)]
    unnamed x46 -> x52, local copies, waits for them, and re-layouts: 5.27 us -> 7.59 us
  transfers between devices with their start and end apart: 34 -> 34, of which waited for: 16 -> 17; matrix products, arithmetic and copies ran while one was open for 5% -> 5% of each run, Pallas kernels for 10% -> 16%
where the time goes in v1:
time: 265 us; the launch traced here: 264 us
  waiting for transfers between devices  90.2 us (34%)
  starting transfers between devices  69.3 us (26%)
  Pallas kernels  41.8 us (16%)
  blocking collectives  22.2 us (8%)
  between operations  14.6 us (6%)
  other arithmetic  10.9 us (4%)
  local copies, waits for them, and re-layouts  10.5 us (4%)
  matrix products  4.61 us (2%)
    pallas_call x3, Pallas kernels, call(): pl.pallas_call(kernel, grid_spec=pltpu.PrefetchScalarGridSpec(num_scalar_...  41.8 us
    ppermute x18, waiting for transfers between devices, shift_x(): return lax.ppermute(value, 'section', pairs)  31.9 us
    ppermute x18, starting transfers between devices, shift_x(): return lax.ppermute(value, 'section', pairs)  29.1 us
    ppermute x11, starting transfers between devices, shift_z(): return lax.ppermute(value, 'section', pairs)  25.6 us
    all_gather x1, waiting for transfers between devices, per_device(): lax.all_gather(tok_x, 'section', axis_index_groups=Z_GROUPS, axis=1, tile...  23.7 us
    all_to_all x1, blocking collectives, exchange(): lax.all_to_all(value.reshape(experts, -1, value.shape[-1]), 'expert', spl...  22.2 us
    all_to_all x3, waiting for transfers between devices, exchange(): lax.all_to_all(value.reshape(experts, -1, value.shape[-1]), 'expert', spl...  17.3 us
    all_to_all x3, starting transfers between devices, exchange(): lax.all_to_all(value.reshape(experts, -1, value.shape[-1]), 'expert', spl...  14.6 us
  transfers between devices with their start and end apart: 34, of which 17 were waited for; matrix products, arithmetic and copies ran while one was open for 5% of the time, Pallas kernels for 16%

profile of v1, /device:TPU:8, one launch (start us, length us, event | category | flops | bytes accessed | tf_op | source)
XLA Modules:
  0.0 264.2 jit_solution(862476081825949367)
XLA Ops:
  7.2 2.0 collective-permute-start
  9.2 4.0 %collective-permute-start.1 = (bf16[256,128]{1,0:T(8,128)(2,1)}, bf16[256,128]{1,0:T(8,128)(2,1)S(1)}, u32[]{:S(2)}, u32[]{:S(2)}) collective-permute-start(bf16[256,128]{1,0:T(8,128)(2,1)} %param.13), channel_id=1, source_target_pairs={{0,56},{8,0},{16,8},{24,16},{32,24},{40,32},{48,40},{56,48},{64,12... | collective-permute-start | bytes 196616 | tf_op jit(solution)/shard_map/ppermute | solution.py:18
  13.2 0.8 copy.43
  14.7 0.7 fusion.31
  15.4 1.9 select_reduce_fusion.1
  17.3 0.9 convolution_convert_fusion
  18.2 2.6 collective-permute-start.2
  20.8 4.9 %all-to-all-start = ((bf16[8,80,128]{2,1,0:T(8,128)(2,1)}), bf16[8,80,128]{2,1,0:T(8,128)(2,1)S(1)}, u32[]{:S(2)}, u32[]{:S(2)}) async-start(bf16[8,80,128]{2,1,0:T(8,128)(2,1)} %bitcast.7), calls=%async_computation | async-start | bytes 327680 | tf_op jit(solution)/shard_map/all_to_all | solution.py:289
  25.7 2.6 collective-permute-start.3
  28.4 5.0 %collective-permute-done.3 = bf16[2,256,128]{2,1,0:T(8,128)(2,1)S(1)} collective-permute-done((bf16[2,256,128]{2,1,0:T(8,128)(2,1)S(1)}, bf16[2,256,128]{2,1,0:T(8,128)(2,1)S(1)}, u32[]{:S(2)}, u32[]{:S(2)}) %collective-permute-start.3) | collective-permute-done | bytes 131104 | tf_op jit(solution)/shard_map/ppermute | solution.py:18
  33.5 1.5 collective-permute-start.4
  35.0 2.7 %collective-permute-start.5 = (bf16[640,128]{1,0:T(8,128)(2,1)S(1)}, bf16[640,128]{1,0:T(8,128)(2,1)S(1)}, u32[]{:S(2)}, u32[]{:S(2)}) collective-permute-start(bf16[640,128]{1,0:T(8,128)(2,1)S(1)} %bitcast.138), channel_id=1, source_target_pairs={{0,128},{8,136},{16,144},{24,152},{32,160},{40,168},{48,176},{56,1... | collective-permute-start | bytes 491528 | tf_op jit(solution)/shard_map/ppermute | solution.py:23
  37.7 1.4 collective-permute-start.6
  39.2 1.7 collective-permute-done.4
  40.8 4.5 %collective-permute-done.5 = bf16[640,128]{1,0:T(8,128)(2,1)S(1)} collective-permute-done((bf16[640,128]{1,0:T(8,128)(2,1)S(1)}, bf16[640,128]{1,0:T(8,128)(2,1)S(1)}, u32[]{:S(2)}, u32[]{:S(2)}) %collective-permute-start.5) | collective-permute-done | bytes 163872 | tf_op jit(solution)/shard_map/ppermute | solution.py:23
  45.5 0.9 pad_maximum_fusion.2
  47.5 22.2 %all_to_all.20 = bf16[8,80,1024]{2,1,0:T(8,128)(2,1)S(1)} all-to-all(bf16[8,80,1024]{2,1,0:T(8,128)(2,1)S(1)} %bitcast.127), channel_id=1, replica_groups=mesh['section'=32,'expert'=8] {'expert'}, dimensions={0} | all-to-all | bytes 2621440 | tf_op jit(solution)/shard_map/all_to_all | solution.py:289
  69.8 2.3 collective-permute-start.10
  72.1 3.2 %collective-permute-start.12 = (bf16[640,512]{1,0:T(8,128)(2,1)S(1)}, bf16[640,512]{1,0:T(8,128)(2,1)}, u32[]{:S(2)}, u32[]{:S(2)}) collective-permute-start(bf16[640,512]{1,0:T(8,128)(2,1)S(1)} %get-tuple-element.82.refs_0_.refs_4_), channel_id=1, source_target_pairs={{0,192},{8,200},{16,208},{24,216},{32,224},{40,232},{48,240},{56,2... | collective-permute-start | bytes 1966088 | tf_op jit(solution)/shard_map/ppermute | solution.py:23
  75.4 12.2 %collective-permute-done.10.refs_7_.refs_11_ = bf16[640,512]{1,0:T(8,128)(2,1)} collective-permute-done((bf16[640,512]{1,0:T(8,128)(2,1)S(1)}, bf16[640,512]{1,0:T(8,128)(2,1)}, u32[]{:S(2)}, u32[]{:S(2)}) %collective-permute-start.10) | collective-permute-done | bytes 655392 | tf_op jit(solution)/shard_map/ppermute | solution.py:23
  87.6 3.5 %collective-permute-start.11 = (bf16[640,512]{1,0:T(8,128)(2,1)}, bf16[640,512]{1,0:T(8,128)(2,1)}, u32[]{:S(2)}, u32[]{:S(2)}) collective-permute-start(bf16[640,512]{1,0:T(8,128)(2,1)} %collective-permute-done.10.refs_7_.refs_11_), channel_id=1, source_target_pairs={{0,192},{8,200},{16,208},{24,216},{32,224},{40,232},{48,240},{56,2... | collective-permute-start | bytes 1966088 | tf_op jit(solution)/shard_map/ppermute | solution.py:23
  91.1 23.7 %all-gather.2.cloned.1.call-done.tok_ref.refs_0_ = bf16[640,4096]{1,0:T(8,128)(2,1)} async-done(((bf16[640,512]{1,0:T(8,128)(2,1)}), bf16[640,4096]{1,0:T(8,128)(2,1)}) %all-gather.2.cloned.1.call-update) | async-done | bytes 5242896 | tf_op jit(solution)/shard_map/all_gather | solution.py:302
  114.8 13.8 %shard_map.118 = (f32[640,256]{1,0:T(8,128)S(1)}, f32[640,256]{1,0:T(8,128)S(1)}, bf16[640,256]{1,0:T(8,128)(2,1)S(1)}, bf16[640,512]{1,0:T(8,128)(2,1)S(1)}, bf...) custom-call(s32[1]{0:T(128)} %bitcast.3.x_ref, ...), custom_call_target="tpu_custom_call" | custom-call | flops 4026531840 | bytes 16777216 | tf_op jit(solution)/shard_map/pallas_call | solution.py:234
  128.6 0.8 copy-done
  129.4 0.8 copy-done.1
  130.2 0.9 copy-done.6
  131.1 1.5 collective-permute-start.13
  132.6 1.8 collective-permute-start.14
  134.3 14.5 %shard_map.119 = (bf16[8,648,512]{2,1,0:T(8,128)(2,1)}, bf16[640,256]{1,0:T(8,128)(2,1)S(1)}, bf16[640,256]{1,0:T(8,128)(2,1)S(1)}) custom-call(s32[1]{0:T(128)} %bitcast.3.x_ref, bf16[640,512]{1,0:T(8,128)(2,1)S(1)} %get-tuple-element.82.refs_0_.refs_4_, bf16[640,512]{1,0:T(8,128)(2,1)S(1)} %get-tuple-element.81.refs_1_.refs_5_, ...), custom_call_target="tpu_custom_call" | custom-call | tf_op jit(solution)/shard_map/pallas_call | solution.py:234
  148.9 0.7 copy-done.8
  149.6 0.8 copy-done.14
  150.4 0.8 copy-done.16
  151.7 3.0 %collective-permute-start.17 = (bf16[640,512]{1,0:T(8,128)(2,1)}, bf16[640,512]{1,0:T(8,128)(2,1)S(1)}, u32[]{:S(2)}, u32[]{:S(2)}) collective-permute-start(bf16[640,512]{1,0:T(8,128)(2,1)} %get-tuple-element.57), channel_id=1, source_target_pairs={{0,192},{8,200},{16,208},{24,216},{32,224},{40,232},{48,240},{56,2... | collective-permute-start | bytes 1966088 | tf_op jit(solution)/shard_map/ppermute | solution.py:23
  154.6 1.5 add_convert_fusion.2
  156.6 1.8 collective-permute-start.15
  158.5 13.6 %shard_map.120 = (bf16[4,8,128,256]{3,2,1,0:T(8,128)(2,1)}, bf16[4,8,128,256]{3,2,1,0:T(8,128)(2,1)}, bf16[256,4096]{1,0:T(8,128)(2,1)}) custom-call(s32[1]{0:T(128)} %bitcast.3.x_ref, bf16[640,4096]{1,0:T(8,128)(2,1)} %all-gather.2.cloned.1.call-done.tok_ref.refs_0_, bf16[640,256]{1,0:T(8,128)(2,1)S(1)} %get-tuple-element.60.refs_1_, ...), custom_call_target="tpu_custom_call" | custom-call | tf_op jit(solution)/shard_map/pallas_call | solution.py:234
  172.0 10.0 %collective-permute-done.18 = bf16[640,512]{1,0:T(8,128)(2,1)S(1)} collective-permute-done((bf16[640,512]{1,0:T(8,128)(2,1)S(1)}, bf16[640,512]{1,0:T(8,128)(2,1)S(1)}, u32[]{:S(2)}, u32[]{:S(2)}) %collective-permute-start.18) | collective-permute-done | bytes 655392 | tf_op jit(solution)/shard_map/ppermute | solution.py:23
  182.0 0.7 collective-permute-done.15
  183.3 1.3 pad_maximum_fusion
  184.6 4.8 %all-to-all-start.2 = ((bf16[8,80,1024]{2,1,0:T(8,128)(2,1)}), bf16[8,80,1024]{2,1,0:T(8,128)(2,1)S(1)}, u32[]{:S(2)}, u32[]{:S(2)}) async-start(bf16[8,80,1024]{2,1,0:T(8,128)(2,1)} %bitcast.30), calls=%async_computation.2 | async-start | bytes 2621440 | tf_op jit(solution)/shard_map/all_to_all | solution.py:289
  189.4 17.3 %all-to-all-done.2 = bf16[8,80,1024]{2,1,0:T(8,128)(2,1)S(1)} async-done(((bf16[8,80,1024]{2,1,0:T(8,128)(2,1)}), bf16[8,80,1024]{2,1,0:T(8,128)(2,1)S(1)}, u32[]{:S(2)}, u32[]{:S(2)}) %all-to-all-start.2) | async-done | bytes 1310752 | tf_op jit(solution)/shard_map/all_to_all | solution.py:289
  206.7 0.7 copy.45
  207.5 7.3 %reduce-scatter.2.cloned.1.call-done = bf16[648,512]{1,0:T(8,128)(2,1)} async-done(((bf16[5184,512]{1,0:T(8,128)(2,1)}), bf16[648,512]{1,0:T(8,128)(2,1)}) %reduce-scatter.2.cloned.1.call-update) | async-done | bytes 663568 | tf_op jit(solution)/shard_map/reduce_scatter | solution.py:368
  214.7 0.8 slice.43
  215.8 0.9 fusion.2
  216.7 4.8 %all-to-all-start.3 = ((bf16[8,88,512]{2,1,0:T(8,128)(2,1)}), bf16[8,88,512]{2,1,0:T(8,128)(2,1)S(1)}, u32[]{:S(2)}, u32[]{:S(2)}) async-start(bf16[8,88,512]{2,1,0:T(8,128)(2,1)} %fusion.2), calls=%async_computation.4 | async-start | bytes 1441792 | tf_op jit(solution)/shard_map/all_to_all | solution.py:289
  221.6 2.3 fusion.3
  223.9 1.0 copy-done.13
  224.9 3.2 %collective-permute-start.19 = (bf16[256,128]{1,0:T(8,128)(2,1)S(1)}, bf16[256,128]{1,0:T(8,128)(2,1)S(1)}, u32[]{:S(2)}, u32[]{:S(2)}) collective-permute-start(bf16[256,128]{1,0:T(8,128)(2,1)S(1)} %get-tuple-element.83), channel_id=1, source_target_pairs={{0,32},{8,40},{16,48},{24,56},{32,0},{40,8},{48,16},{56,24},{64,96... | collective-permute-start | bytes 196616 | tf_op jit(solution)/shard_map/ppermute | solution.py:18
  228.1 1.6 collective-permute-start.20
  229.7 3.5 %collective-permute-start.21 = (bf16[256,128]{1,0:T(8,128)(2,1)S(1)}, bf16[256,128]{1,0:T(8,128)(2,1)S(1)}, u32[]{:S(2)}, u32[]{:S(2)}) collective-permute-start(bf16[256,128]{1,0:T(8,128)(2,1)S(1)} %get-tuple-element.88), channel_id=1, source_target_pairs={{0,40},{8,48},{16,56},{24,0},{32,8},{40,16},{48,24},{56,32},{64,10... | collective-permute-start | bytes 196616 | tf_op jit(solution)/shard_map/ppermute | solution.py:18
  233.1 1.5 collective-permute-start.22
  234.6 2.7 %collective-permute-start.23 = (bf16[256,128]{1,0:T(8,128)(2,1)S(1)}, bf16[256,128]{1,0:T(8,128)(2,1)S(1)}, u32[]{:S(2)}, u32[]{:S(2)}) collective-permute-start(bf16[256,128]{1,0:T(8,128)(2,1)S(1)} %get-tuple-element.86), channel_id=1, source_target_pairs={{0,48},{8,56},{16,0},{24,8},{32,16},{40,24},{48,32},{56,40},{64,11... | collective-permute-start | bytes 196616 | tf_op jit(solution)/shard_map/ppermute | solution.py:18
  237.3 1.4 collective-permute-start.24
  238.6 1.2 collective-permute-done.20
  239.8 0.7 collective-permute-start.25
  241.4 1.4 collective-permute-done.24
  242.7 1.4 collective-permute-done.25
  244.1 1.6 fusion.18
  247.6 1.5 collective-permute-start.26
  249.1 2.7 %collective-permute-start.27 = (bf16[264,128]{1,0:T(8,128)(2,1)S(1)}, bf16[264,128]{1,0:T(8,128)(2,1)S(1)}, u32[]{:S(2)}, u32[]{:S(2)}) collective-permute-start(bf16[264,128]{1,0:T(8,128)(2,1)S(1)} %get-tuple-element.100), channel_id=1, source_target_pairs={{0,128},{8,136},{16,144},{24,152},{32,160},{40,168},{48,176},{56,1... | collective-permute-start | bytes 202760 | tf_op jit(solution)/shard_map/ppermute | solution.py:23
  251.8 1.5 collective-permute-start.28
  253.3 1.6 collective-permute-done.27
  254.9 1.2 collective-permute-done.28
  (112 shorter events, 7.7 us)
Async XLA Ops:
  7.2 11.0 %copy-start.18 = (bf16[256,128]{1,0:T(8,128)(2,1)S(1)}, bf16[256,128]{1,0:T(8,128)(2,1)}, u32[]{:S(2)}) copy-start(bf16[256,128]{1,0:T(8,128)(2,1)} %param.13) | copy-start | bytes 196612
  7.2 10.1 %copy-start.17 = (bf16[256,128]{1,0:T(8,128)(2,1)S(1)}, bf16[256,128]{1,0:T(8,128)(2,1)}, u32[]{:S(2)}) copy-start(bf16[256,128]{1,0:T(8,128)(2,1)} %param.7) | copy-start | bytes 196612
  7.2 11.0 %collective-permute-start = (bf16[256,128]{1,0:T(8,128)(2,1)}, bf16[256,128]{1,0:T(8,128)(2,1)S(1)}, u32[]{:S(2)}, u32[]{:S(2)}) collective-permute-start(bf16[256,128]{1,0:T(8,128)(2,1)} %param.13), channel_id=1, source_target_pairs={{0,8},{8,16},{16,24},{24,32},{32,40},{40,48},{48,56},{56,0},{64,72... | collective-permute-start | bytes 196616 | tf_op jit(solution)/shard_map/ppermute | solution.py:18
  9.2 9.0 %collective-permute-start.1 = (bf16[256,128]{1,0:T(8,128)(2,1)}, bf16[256,128]{1,0:T(8,128)(2,1)S(1)}, u32[]{:S(2)}, u32[]{:S(2)}) collective-permute-start(bf16[256,128]{1,0:T(8,128)(2,1)} %param.13), channel_id=1, source_target_pairs={{0,56},{8,0},{16,8},{24,16},{32,24},{40,32},{48,40},{56,48},{64,12... | collective-permute-start | bytes 196616 | tf_op jit(solution)/shard_map/ppermute | solution.py:18
  17.3 29.7 %copy-start.10 = (bf16[640,256]{1,0:T(8,128)(2,1)}, bf16[640,256]{1,0:T(8,128)(2,1)S(1)}, u32[]{:S(2)}) copy-start(bf16[640,256]{1,0:T(8,128)(2,1)S(1)} %get-tuple-element.78) | copy-start | bytes 983044
  18.2 15.3 %collective-permute-start.2 = (bf16[3,256,128]{2,1,0:T(8,128)(2,1)S(1)}, bf16[3,256,128]{2,1,0:T(8,128)(2,1)S(1)}, u32[]{:S(2)}, u32[]{:S(2)}) collective-permute-start(bf16[3,256,128]{2,1,0:T(8,128)(2,1)S(1)} %pad_maximum_fusion.3), channel_id=1, source_target_pairs={{0,24},{8,32},{16,40},{24,48},{32,56},{40,0},{48,8},{56,16},{64,88... | collective-permute-start | bytes 589832 | tf_op jit(solution)/shard_map/ppermute | solution.py:18
  20.8 12.6 %all-to-all-start = ((bf16[8,80,128]{2,1,0:T(8,128)(2,1)}), bf16[8,80,128]{2,1,0:T(8,128)(2,1)S(1)}, u32[]{:S(2)}, u32[]{:S(2)}) async-start(bf16[8,80,128]{2,1,0:T(8,128)(2,1)} %bitcast.7), calls=%async_computation | async-start | bytes 327680 | tf_op jit(solution)/shard_map/all_to_all | solution.py:289
  25.7 89.1 %all-gather.2.cloned.1.call-start = ((), (), s32[]{:S(2)}) async-start(), calls=%async_computation.5 | async-start | bytes 5898240 | tf_op jit(solution)/shard_map/all_gather | solution.py:302
  25.7 7.6 %collective-permute-start.3 = (bf16[2,256,128]{2,1,0:T(8,128)(2,1)S(1)}, bf16[2,256,128]{2,1,0:T(8,128)(2,1)S(1)}, u32[]{:S(2)}, u32[]{:S(2)}) collective-permute-start(bf16[2,256,128]{2,1,0:T(8,128)(2,1)S(1)} %slice.30), channel_id=1, source_target_pairs={{0,40},{8,48},{16,56},{24,0},{32,8},{40,16},{48,24},{56,32},{64,10... | collective-permute-start | bytes 393224 | tf_op jit(solution)/shard_map/ppermute | solution.py:18
  33.5 7.3 %collective-permute-start.4 = (bf16[640,128]{1,0:T(8,128)(2,1)S(1)}, bf16[640,128]{1,0:T(8,128)(2,1)S(1)}, u32[]{:S(2)}, u32[]{:S(2)}) collective-permute-start(bf16[640,128]{1,0:T(8,128)(2,1)S(1)} %bitcast.137), channel_id=1, source_target_pairs={{0,64},{8,72},{16,80},{24,88},{32,96},{40,104},{48,112},{56,120},{... | collective-permute-start | bytes 491528 | tf_op jit(solution)/shard_map/ppermute | solution.py:23
  35.0 10.3 %collective-permute-start.5 = (bf16[640,128]{1,0:T(8,128)(2,1)S(1)}, bf16[640,128]{1,0:T(8,128)(2,1)S(1)}, u32[]{:S(2)}, u32[]{:S(2)}) collective-permute-start(bf16[640,128]{1,0:T(8,128)(2,1)S(1)} %bitcast.138), channel_id=1, source_target_pairs={{0,128},{8,136},{16,144},{24,152},{32,160},{40,168},{48,176},{56,1... | collective-permute-start | bytes 491528 | tf_op jit(solution)/shard_map/ppermute | solution.py:23
  37.7 7.6 %collective-permute-start.6 = (bf16[640,128]{1,0:T(8,128)(2,1)S(1)}, bf16[640,128]{1,0:T(8,128)(2,1)S(1)}, u32[]{:S(2)}, u32[]{:S(2)}) collective-permute-start(bf16[640,128]{1,0:T(8,128)(2,1)S(1)} %bitcast.139), channel_id=1, source_target_pairs={{0,192},{8,200},{16,208},{24,216},{32,224},{40,232},{48,240},{56,2... | collective-permute-start | bytes 491528 | tf_op jit(solution)/shard_map/ppermute | solution.py:23
  46.4 168.3 %reduce-scatter.2.cloned.1.call-start = ((), (), s32[]{:S(2)}) async-start(), calls=%async_computation.6 | async-start | bytes 5971968 | tf_op jit(solution)/shard_map/reduce_scatter | solution.py:368
  69.8 17.8 %collective-permute-start.10 = (bf16[640,512]{1,0:T(8,128)(2,1)S(1)}, bf16[640,512]{1,0:T(8,128)(2,1)}, u32[]{:S(2)}, u32[]{:S(2)}) collective-permute-start(bf16[640,512]{1,0:T(8,128)(2,1)S(1)} %get-tuple-element.81.refs_1_.refs_5_), channel_id=1, source_target_pairs={{0,192},{8,200},{16,208},{24,216},{32,224},{40,232},{48,240},{56,2... | collective-permute-start | bytes 1966088 | tf_op jit(solution)/shard_map/ppermute | solution.py:23
  72.1 18.9 %collective-permute-start.7 = (bf16[640,512]{1,0:T(8,128)(2,1)S(1)}, bf16[640,512]{1,0:T(8,128)(2,1)S(1)}, u32[]{:S(2)}, u32[]{:S(2)}) collective-permute-start(bf16[640,512]{1,0:T(8,128)(2,1)S(1)} %get-tuple-element.82.refs_0_.refs_4_), channel_id=1, source_target_pairs={{0,64},{8,72},{16,80},{24,88},{32,96},{40,104},{48,112},{56,120},{... | collective-permute-start | bytes 1966088 | tf_op jit(solution)/shard_map/ppermute | solution.py:23
  72.1 60.4 %collective-permute-start.12 = (bf16[640,512]{1,0:T(8,128)(2,1)S(1)}, bf16[640,512]{1,0:T(8,128)(2,1)}, u32[]{:S(2)}, u32[]{:S(2)}) collective-permute-start(bf16[640,512]{1,0:T(8,128)(2,1)S(1)} %get-tuple-element.82.refs_0_.refs_4_), channel_id=1, source_target_pairs={{0,192},{8,200},{16,208},{24,216},{32,224},{40,232},{48,240},{56,2... | collective-permute-start | bytes 1966088 | tf_op jit(solution)/shard_map/ppermute | solution.py:23
  75.4 59.0 %collective-permute-start.8 = (bf16[640,512]{1,0:T(8,128)(2,1)S(1)}, bf16[640,512]{1,0:T(8,128)(2,1)S(1)}, u32[]{:S(2)}, u32[]{:S(2)}) collective-permute-start(bf16[640,512]{1,0:T(8,128)(2,1)S(1)} %get-tuple-element.81.refs_1_.refs_5_), channel_id=1, source_target_pairs={{0,64},{8,72},{16,80},{24,88},{32,96},{40,104},{48,112},{56,120},{... | collective-permute-start | bytes 1966088 | tf_op jit(solution)/shard_map/ppermute | solution.py:23
  87.6 46.7 %collective-permute-start.11 = (bf16[640,512]{1,0:T(8,128)(2,1)}, bf16[640,512]{1,0:T(8,128)(2,1)}, u32[]{:S(2)}, u32[]{:S(2)}) collective-permute-start(bf16[640,512]{1,0:T(8,128)(2,1)} %collective-permute-done.10.refs_7_.refs_11_), channel_id=1, source_target_pairs={{0,192},{8,200},{16,208},{24,216},{32,224},{40,232},{48,240},{56,2... | collective-permute-start | bytes 1966088 | tf_op jit(solution)/shard_map/ppermute | solution.py:23
  91.1 43.3 %collective-permute-start.9 = (bf16[640,512]{1,0:T(8,128)(2,1)S(1)}, bf16[640,512]{1,0:T(8,128)(2,1)}, u32[]{:S(2)}, u32[]{:S(2)}) collective-permute-start(bf16[640,512]{1,0:T(8,128)(2,1)S(1)} %collective-permute-done.7.refs_2_.refs_6_), channel_id=1, source_target_pairs={{0,64},{8,72},{16,80},{24,88},{32,96},{40,104},{48,112},{56,120},{... | collective-permute-start | bytes 1966088 | tf_op jit(solution)/shard_map/ppermute | solution.py:23
  128.6 0.8 copy-start
  129.4 0.8 copy-start.1
  130.2 0.9 copy-start.6
  131.1 17.8 %copy-start.2 = (bf16[640,512]{1,0:T(8,128)(2,1)}, bf16[640,512]{1,0:T(8,128)(2,1)S(1)}, u32[]{:S(2)}) copy-start(bf16[640,512]{1,0:T(8,128)(2,1)S(1)} %get-tuple-element.44) | copy-start | bytes 1966084
  131.1 17.8 %copy-start.4 = (bf16[640,512]{1,0:T(8,128)(2,1)}, bf16[640,512]{1,0:T(8,128)(2,1)S(1)}, u32[]{:S(2)}) copy-start(bf16[640,512]{1,0:T(8,128)(2,1)S(1)} %get-tuple-element.67) | copy-start | bytes 1966084
  131.1 18.5 %collective-permute-start.13 = (bf16[640,512]{1,0:T(8,128)(2,1)}, bf16[640,512]{1,0:T(8,128)(2,1)S(1)}, u32[]{:S(2)}, u32[]{:S(2)}) collective-permute-start(bf16[640,512]{1,0:T(8,128)(2,1)} %get-tuple-element.53), channel_id=1, source_target_pairs={{0,64},{8,72},{16,80},{24,88},{32,96},{40,104},{48,112},{56,120},{... | collective-permute-start | bytes 1966088 | tf_op jit(solution)/shard_map/ppermute | solution.py:23
  132.6 17.9 %collective-permute-start.14 = (bf16[640,512]{1,0:T(8,128)(2,1)}, bf16[640,512]{1,0:T(8,128)(2,1)S(1)}, u32[]{:S(2)}, u32[]{:S(2)}) collective-permute-start(bf16[640,512]{1,0:T(8,128)(2,1)} %get-tuple-element.54), channel_id=1, source_target_pairs={{0,192},{8,200},{16,208},{24,216},{32,224},{40,232},{48,240},{56,2... | collective-permute-start | bytes 1966088 | tf_op jit(solution)/shard_map/ppermute | solution.py:23
  148.9 0.8 copy-start.8
  149.6 0.8 copy-start.14
  150.4 0.8 copy-start.16
  151.3 5.2 %copy-start.7 = (bf16[640,512]{1,0:T(8,128)(2,1)S(1)}, bf16[640,512]{1,0:T(8,128)(2,1)}, u32[]{:S(2)}) copy-start(bf16[640,512]{1,0:T(8,128)(2,1)} %copy-done.6) | copy-start | bytes 1966084
  151.3 5.1 %copy-start.15 = (bf16[640,512]{1,0:T(8,128)(2,1)S(1)}, bf16[640,512]{1,0:T(8,128)(2,1)}, u32[]{:S(2)}) copy-start(bf16[640,512]{1,0:T(8,128)(2,1)} %copy-done.14) | copy-start | bytes 1966084
  151.3 20.7 %collective-permute-start.16 = (bf16[640,512]{1,0:T(8,128)(2,1)}, bf16[640,512]{1,0:T(8,128)(2,1)S(1)}, u32[]{:S(2)}, u32[]{:S(2)}) collective-permute-start(bf16[640,512]{1,0:T(8,128)(2,1)} %get-tuple-element.56), channel_id=1, source_target_pairs={{0,64},{8,72},{16,80},{24,88},{32,96},{40,104},{48,112},{56,120},{... | collective-permute-start | bytes 1966088 | tf_op jit(solution)/shard_map/ppermute | solution.py:23
  151.7 20.4 %collective-permute-start.17 = (bf16[640,512]{1,0:T(8,128)(2,1)}, bf16[640,512]{1,0:T(8,128)(2,1)S(1)}, u32[]{:S(2)}, u32[]{:S(2)}) collective-permute-start(bf16[640,512]{1,0:T(8,128)(2,1)} %get-tuple-element.57), channel_id=1, source_target_pairs={{0,192},{8,200},{16,208},{24,216},{32,224},{40,232},{48,240},{56,2... | collective-permute-start | bytes 1966088 | tf_op jit(solution)/shard_map/ppermute | solution.py:23
  156.1 2.4 copy-start.9
  156.1 25.9 %collective-permute-start.18 = (bf16[640,512]{1,0:T(8,128)(2,1)S(1)}, bf16[640,512]{1,0:T(8,128)(2,1)S(1)}, u32[]{:S(2)}, u32[]{:S(2)}) collective-permute-start(bf16[640,512]{1,0:T(8,128)(2,1)S(1)} %add_convert_fusion.2), channel_id=1, source_target_pairs={{0,192},{8,200},{16,208},{24,216},{32,224},{40,232},{48,240},{56,2... | collective-permute-start | bytes 1966088 | tf_op jit(solution)/shard_map/ppermute | solution.py:23
  156.6 26.1 %collective-permute-start.15 = (bf16[640,512]{1,0:T(8,128)(2,1)S(1)}, bf16[640,512]{1,0:T(8,128)(2,1)S(1)}, u32[]{:S(2)}, u32[]{:S(2)}) collective-permute-start(bf16[640,512]{1,0:T(8,128)(2,1)S(1)} %add_convert_fusion.3), channel_id=1, source_target_pairs={{0,64},{8,72},{16,80},{24,88},{32,96},{40,104},{48,112},{56,120},{... | collective-permute-start | bytes 1966088 | tf_op jit(solution)/shard_map/ppermute | solution.py:23
  158.5 24.3 %copy-start.3 = (bf16[640,512]{1,0:T(8,128)(2,1)S(1)}, bf16[640,512]{1,0:T(8,128)(2,1)}, u32[]{:S(2)}) copy-start(bf16[640,512]{1,0:T(8,128)(2,1)} %copy-done.2) | copy-start | bytes 1966084
  158.5 24.3 %copy-start.5 = (bf16[640,512]{1,0:T(8,128)(2,1)S(1)}, bf16[640,512]{1,0:T(8,128)(2,1)}, u32[]{:S(2)}) copy-start(bf16[640,512]{1,0:T(8,128)(2,1)} %copy-done.4) | copy-start | bytes 1966084
  184.6 22.1 %all-to-all-start.2 = ((bf16[8,80,1024]{2,1,0:T(8,128)(2,1)}), bf16[8,80,1024]{2,1,0:T(8,128)(2,1)S(1)}, u32[]{:S(2)}, u32[]{:S(2)}) async-start(bf16[8,80,1024]{2,1,0:T(8,128)(2,1)} %bitcast.30), calls=%async_computation.2 | async-start | bytes 2621440 | tf_op jit(solution)/shard_map/all_to_all | solution.py:289
  214.7 1.1 slice-start
  215.8 5.7 %copy-start.12 = (f32[640,256]{1,0:T(8,128)S(1)}, f32[640,256]{1,0:T(8,128)}, u32[]{:S(2)}) copy-start(f32[640,256]{1,0:T(8,128)} %get-tuple-element.76) | copy-start | bytes 1966084
  216.7 29.0 %all-to-all-start.3 = ((bf16[8,88,512]{2,1,0:T(8,128)(2,1)}), bf16[8,88,512]{2,1,0:T(8,128)(2,1)S(1)}, u32[]{:S(2)}, u32[]{:S(2)}) async-start(bf16[8,88,512]{2,1,0:T(8,128)(2,1)} %fusion.2), calls=%async_computation.4 | async-start | bytes 1441792 | tf_op jit(solution)/shard_map/all_to_all | solution.py:289
  223.9 1.0 copy-start.13
  224.9 12.3 %collective-permute-start.19 = (bf16[256,128]{1,0:T(8,128)(2,1)S(1)}, bf16[256,128]{1,0:T(8,128)(2,1)S(1)}, u32[]{:S(2)}, u32[]{:S(2)}) collective-permute-start(bf16[256,128]{1,0:T(8,128)(2,1)S(1)} %get-tuple-element.83), channel_id=1, source_target_pairs={{0,32},{8,40},{16,48},{24,56},{32,0},{40,8},{48,16},{56,24},{64,96... | collective-permute-start | bytes 196616 | tf_op jit(solution)/shard_map/ppermute | solution.py:18
  228.1 11.8 %collective-permute-start.20 = (bf16[256,128]{1,0:T(8,128)(2,1)S(1)}, bf16[256,128]{1,0:T(8,128)(2,1)S(1)}, u32[]{:S(2)}, u32[]{:S(2)}) collective-permute-start(bf16[256,128]{1,0:T(8,128)(2,1)S(1)} %get-tuple-element.89), channel_id=1, source_target_pairs={{0,24},{8,32},{16,40},{24,48},{32,56},{40,0},{48,8},{56,16},{64,88... | collective-permute-start | bytes 196616 | tf_op jit(solution)/shard_map/ppermute | solution.py:18
  229.7 10.9 %collective-permute-start.21 = (bf16[256,128]{1,0:T(8,128)(2,1)S(1)}, bf16[256,128]{1,0:T(8,128)(2,1)S(1)}, u32[]{:S(2)}, u32[]{:S(2)}) collective-permute-start(bf16[256,128]{1,0:T(8,128)(2,1)S(1)} %get-tuple-element.88), channel_id=1, source_target_pairs={{0,40},{8,48},{16,56},{24,0},{32,8},{40,16},{48,24},{56,32},{64,10... | collective-permute-start | bytes 196616 | tf_op jit(solution)/shard_map/ppermute | solution.py:18
  233.1 7.7 %collective-permute-start.22 = (bf16[256,128]{1,0:T(8,128)(2,1)S(1)}, bf16[256,128]{1,0:T(8,128)(2,1)S(1)}, u32[]{:S(2)}, u32[]{:S(2)}) collective-permute-start(bf16[256,128]{1,0:T(8,128)(2,1)S(1)} %get-tuple-element.87), channel_id=1, source_target_pairs={{0,16},{8,24},{16,32},{24,40},{32,48},{40,56},{48,0},{56,8},{64,80... | collective-permute-start | bytes 196616 | tf_op jit(solution)/shard_map/ppermute | solution.py:18
  234.6 6.8 %collective-permute-start.23 = (bf16[256,128]{1,0:T(8,128)(2,1)S(1)}, bf16[256,128]{1,0:T(8,128)(2,1)S(1)}, u32[]{:S(2)}, u32[]{:S(2)}) collective-permute-start(bf16[256,128]{1,0:T(8,128)(2,1)S(1)} %get-tuple-element.86), channel_id=1, source_target_pairs={{0,48},{8,56},{16,0},{24,8},{32,16},{40,24},{48,32},{56,40},{64,11... | collective-permute-start | bytes 196616 | tf_op jit(solution)/shard_map/ppermute | solution.py:18
  237.3 5.5 %collective-permute-start.24 = (bf16[256,128]{1,0:T(8,128)(2,1)S(1)}, bf16[256,128]{1,0:T(8,128)(2,1)S(1)}, u32[]{:S(2)}, u32[]{:S(2)}) collective-permute-start(bf16[256,128]{1,0:T(8,128)(2,1)S(1)} %get-tuple-element.85), channel_id=1, source_target_pairs={{0,8},{8,16},{16,24},{24,32},{32,40},{40,48},{48,56},{56,0},{64,72... | collective-permute-start | bytes 196616 | tf_op jit(solution)/shard_map/ppermute | solution.py:18
  239.8 4.3 %collective-permute-start.25 = (bf16[256,128]{1,0:T(8,128)(2,1)S(1)}, bf16[256,128]{1,0:T(8,128)(2,1)S(1)}, u32[]{:S(2)}, u32[]{:S(2)}) collective-permute-start(bf16[256,128]{1,0:T(8,128)(2,1)S(1)} %get-tuple-element.84), channel_id=1, source_target_pairs={{0,56},{8,0},{16,8},{24,16},{32,24},{40,32},{48,40},{56,48},{64,12... | collective-permute-start | bytes 196616 | tf_op jit(solution)/shard_map/ppermute | solution.py:18
  245.7 1.0 copy-start.11
  247.1 9.7 %copy-start.19 = (f32[256,2]{0,1:T(2,128)S(1)}, f32[256,2]{0,1:T(2,128)}, u32[]{:S(2)}) copy-start(f32[256,2]{0,1:T(2,128)} %param.9) | copy-start | bytes 6148
  247.6 5.7 %collective-permute-start.26 = (bf16[264,128]{1,0:T(8,128)(2,1)S(1)}, bf16[264,128]{1,0:T(8,128)(2,1)S(1)}, u32[]{:S(2)}, u32[]{:S(2)}) collective-permute-start(bf16[264,128]{1,0:T(8,128)(2,1)S(1)} %get-tuple-element.99), channel_id=1, source_target_pairs={{0,64},{8,72},{16,80},{24,88},{32,96},{40,104},{48,112},{56,120},{... | collective-permute-start | bytes 202760 | tf_op jit(solution)/shard_map/ppermute | solution.py:23
  249.1 5.8 %collective-permute-start.27 = (bf16[264,128]{1,0:T(8,128)(2,1)S(1)}, bf16[264,128]{1,0:T(8,128)(2,1)S(1)}, u32[]{:S(2)}, u32[]{:S(2)}) collective-permute-start(bf16[264,128]{1,0:T(8,128)(2,1)S(1)} %get-tuple-element.100), channel_id=1, source_target_pairs={{0,128},{8,136},{16,144},{24,152},{32,160},{40,168},{48,176},{56,1... | collective-permute-start | bytes 202760 | tf_op jit(solution)/shard_map/ppermute | solution.py:23
  251.8 4.3 %collective-permute-start.28 = (bf16[264,128]{1,0:T(8,128)(2,1)S(1)}, bf16[264,128]{1,0:T(8,128)(2,1)S(1)}, u32[]{:S(2)}, u32[]{:S(2)}) collective-permute-start(bf16[264,128]{1,0:T(8,128)(2,1)S(1)} %get-tuple-element.101), channel_id=1, source_target_pairs={{0,192},{8,200},{16,208},{24,216},{32,224},{40,232},{48,240},{56,2... | collective-permute-start | bytes 202760 | tf_op jit(solution)/shard_map/ppermute | solution.py:23
Sparse Core Ops, SparseCore 0:
  46.5 68.2 all-gather.1
  151.4 63.2 reduce-scatter.1

commit v2 on v1

--- a/solution.py
+++ b/solution.py
@@ -55,8 +55,11 @@
     def part(d):
         return lax.dynamic_index_in_dim(parts, (own + d) % NZ, 0, keepdims=False)
 
-    sent = [shift_z(part(d).astype(bf16), d) for d in (4, 3, -3, 2, -2, 1, -1)]
-    return sum((term.astype(f32) for term in sent), part(0))
+    above = shift_z(jnp.stack([part(2), part(3), part(4)]).astype(bf16), 3).astype(f32)
+    below = shift_z(jnp.stack([part(-3), part(-2)]).astype(bf16), -3).astype(f32)
+    right = shift_z((part(1) + above[2] + below[1]).astype(bf16), 1)
+    left = shift_z((part(-1) + above[0]).astype(bf16), -1)
+    return part(0) + above[1] + below[0] + right.astype(f32) + left.astype(f32)
 
 
 def ring_gather_x(value):
@@ -147,15 +150,11 @@
             outs[2 * d + 1][...] = made[:, half:]
 
 
-def backward_kernel(x_ref, *refs):
-    ups, refs = refs[: 2 * NX], refs[2 * NX :]
-    down_ref, gate_ref, up_ref, coef_ref, silu_ref, hid_ref = refs[:6]
-    part_ref, gate_out, up_out, acc, piece, mix = refs[6:]
+def early_kernel(x_ref, *refs):
+    ups, (down_ref, sum_ref, piece) = refs[: 2 * NX - 2], refs[2 * NX - 2 :]
     step = pl.program_id(0)
-    width = gate_ref.shape[-1]
-    rows = acc.shape[0]
-
-    for d in range(NX):
+
+    for d in range(NX - 1):
 
         @pl.when(step == d)
         def _(d=d):
@@ -165,15 +164,23 @@
 
     @pl.when(step == 0)
     def _():
-        acc[...] = jnp.zeros_like(acc)
-
-    @pl.when(step < NX)
-    def _():
-        acc[...] += dot_nt(piece[...], down_ref[...])
-
-    @pl.when(step == NX - 1)
-    def _():
-        grad_hidden = acc[...]
+        sum_ref[...] = jnp.zeros_like(sum_ref)
+
+    sum_ref[...] += dot_nt(piece[...], down_ref[...])
+
+
+def backward_kernel(x_ref, *refs):
+    far_a, far_b, down_ref, sum_ref, gate_ref, up_ref, coef_ref, silu_ref, hid_ref = refs[:9]
+    part_ref, gate_out, up_out, mix = refs[9:]
+    step = pl.program_id(0)
+    width = gate_ref.shape[-1]
+    rows = sum_ref.shape[0]
+
+    @pl.when(step == 0)
+    def _():
+        half = down_ref.shape[1] // 2
+        grad_hidden = sum_ref[...] + dot_nt(far_a[...], down_ref[:, :half])
+        grad_hidden += dot_nt(far_b[...], down_ref[:, half:])
         gate_out[...] = (grad_hidden * coef_ref[...]).astype(bf16)
         up_out[...] = (grad_hidden * silu_ref[...]).astype(bf16)
         terms = grad_hidden * hid_ref[...].astype(f32)
@@ -197,7 +204,7 @@
             ]
         )
 
-    @pl.when(step >= NX)
+    @pl.when(step >= 1)
     def _():
         gate = gate_ref[...].reshape(-1, width)
         up = up_ref[...].reshape(-1, width)
@@ -241,7 +248,7 @@
             scratch_shapes=scratch,
         ),
         out_shape=out_shape,
-        compiler_params=pltpu.CompilerParams(vmem_limit_bytes=50 * 1024 * 1024),
+        compiler_params=pltpu.CompilerParams(vmem_limit_bytes=63 * 1024 * 1024),
         cost_estimate=pl.CostEstimate(flops=flops, bytes_accessed=moved, transcendentals=0),
     )(*args)
 
@@ -317,6 +324,23 @@
         return jax.ShapeDtypeStruct(shape, kind)
 
     tok_spec = pl.BlockSpec((rows, wide_x), lambda i, s: (0, clip(i, 0, NZ)))
+    (early,) = call(
+        early_kernel,
+        NX - 1,
+        [whole(rows, wide_z // 2)] * (2 * NX - 2)
+        + [
+            pl.BlockSpec(
+                (ff, wide_z), lambda i, s: (0, (s[0] + jnp.where(i == 1, NX - 1, i // 2)) % NX)
+            )
+        ],
+        [whole(rows, ff)],
+        [struct((rows, ff), f32)],
+        [pltpu.VMEM((rows, wide_z), bf16)],
+        0,
+        0,
+        (where, *ups[:4], *ups[6:], down),
+    )
+    dispatched, early = lax.optimization_barrier((dispatched, early))
     coef, silu_gate, hidden, *outs = call(
         forward_kernel,
         NZ + NX,
@@ -341,25 +365,19 @@
 
     back, gate_act, up_act = call(
         backward_kernel,
-        NX + NZ,
-        [whole(rows, wide_z // 2)] * (2 * NX)
-        + [
-            pl.BlockSpec((ff, wide_z), lambda i, s: (0, (s[0] + NX - clip(i, 0, NX)) % NX)),
-            weight_spec(NX),
-            weight_spec(NX),
-        ]
+        1 + NZ,
+        [whole(rows, wide_z // 2)] * 2
+        + [pl.BlockSpec((ff, wide_z), lambda i, s: (0, (s[0] + 2) % NX))]
+        + [whole(rows, ff)]
+        + [weight_spec(1)] * 2
         + [whole(rows, ff)] * 3,
-        [pl.BlockSpec((1, rows + 8, wide_x), lambda i, s: (clip(i, NX, NZ), 0, 0))]
+        [pl.BlockSpec((1, rows + 8, wide_x), lambda i, s: (clip(i, 1, NZ), 0, 0))]
         + [whole(rows, ff)] * 2,
         [struct((NZ, rows + 8, wide_x), bf16)] + [struct((rows, ff), bf16)] * 2,
-        [
-            pltpu.VMEM((rows, ff), f32),
-            pltpu.VMEM((rows, wide_z), bf16),
-            pltpu.VMEM((8, wide_x), bf16),
-        ],
-        0,
-        0,
-        (where, *ups, down, gate4, up4, coef, silu_gate, hidden),
+        [pltpu.VMEM((8, wide_x), bf16)],
+        0,
+        0,
+        (where, *ups[4:6], down, early, gate4, up4, coef, silu_gate, hidden),
     )
 
     back, far = lax.optimization_barrier((back, far))
@@ -396,16 +414,15 @@
         axis=1,
     )
     returned = exchange(summed)
+    moe_out = jnp.dot(weighted.T, returned.astype(f32), precision=highest)
+    moe_out, back_z = lax.optimization_barrier((moe_out, back_z))
 
     mix = back_z[rows : rows + 4].reshape(2, 2 * wide_x)[:, :rows].reshape(2, experts, capacity)
     mix = jnp.pad(mix.transpose(1, 0, 2), ((0, 0), (0, 6), (0, wide_x - capacity)))
     back = exchange(
         jnp.concatenate([back_z[:rows].reshape(experts, capacity, wide_x), mix], axis=1)
     ).reshape(experts, capacity + 8, wide_x)
-    moe_out = jnp.dot(weighted.T, returned.astype(f32), precision=highest)
     mixed = (tokens.astype(f32) + spread_z(moe_out, my_z)).astype(bf16)
-    mixed, back = lax.optimization_barrier((mixed, back))
-
     grad_moe = dot_tn(select_low, back[:, :capacity].reshape(rows, wide_x))
     mix = back[:, capacity : capacity + 2, :capacity].transpose(1, 0, 2).reshape(2, rows)
     mix = jnp.sum(jnp.dot(mix, picks, preferred_element_type=f32), axis=0).reshape(-1, feat)

time: 265 us -> 260 us (0.981)
  starting transfers between devices: 69.3 us -> 62.8 us
  Pallas kernels: 41.8 us -> 47.6 us
  local copies, waits for them, and re-layouts: 10.5 us -> 4.92 us
  other arithmetic: 10.9 us -> 14.2 us
    all_gather x1, waiting for transfers between devices: 23.7 us -> 3.67 us  [per_device(): lax.all_gather(tok_x, 'section', axis_index_groups=Z_GROUPS, axis=1, tile...]
    ppermute x18, waiting for transfers between devices: 31.9 us -> 44.6 us  [shift_x(): return lax.ppermute(value, 'section', pairs)]
    ppermute x11 -> x8, waiting for transfers between devices: 9.94 us -> 17.3 us  [shift_z(): return lax.ppermute(value, 'section', pairs)]
    ppermute x11 -> x8, starting transfers between devices: 25.6 us -> 19.4 us  [shift_z(): return lax.ppermute(value, 'section', pairs)]
    pallas_call x3 -> x4, Pallas kernels: 41.8 us -> 47.6 us  [call(): pl.pallas_call(kernel, grid_spec=pltpu.PrefetchScalarGridSpec(num_scalar_...]
    unnamed x52 -> x41, local copies, waits for them, and re-layouts: 7.59 us -> 3.01 us
  transfers between devices with their start and end apart: 34 -> 31, of which waited for: 17 -> 19; matrix products, arithmetic and copies ran while one was open for 5% -> 6% of each run, Pallas kernels for 16% -> 18%
where the time goes in v2:
time: 260 us; the launch traced here: 259 us
  waiting for transfers between devices  88.8 us (34%)
  starting transfers between devices  62.8 us (24%)
  Pallas kernels  47.6 us (18%)
  blocking collectives  22.2 us (9%)
  between operations  14.7 us (6%)
  other arithmetic  14.2 us (5%)
  local copies, waits for them, and re-layouts  4.92 us (2%)
  matrix products  3.76 us (1%)
    pallas_call x4, Pallas kernels, call(): pl.pallas_call(kernel, grid_spec=pltpu.PrefetchScalarGridSpec(num_scalar_...  47.6 us
    ppermute x18, waiting for transfers between devices, shift_x(): return lax.ppermute(value, 'section', pairs)  44.6 us
    ppermute x18, starting transfers between devices, shift_x(): return lax.ppermute(value, 'section', pairs)  28.5 us
    all_to_all x1, blocking collectives, exchange(): lax.all_to_all(value.reshape(experts, -1, value.shape[-1]), 'expert', spl...  22.2 us
    ppermute x8, starting transfers between devices, shift_z(): return lax.ppermute(value, 'section', pairs)  19.4 us
    ppermute x8, waiting for transfers between devices, shift_z(): return lax.ppermute(value, 'section', pairs)  17.3 us
    all_to_all x3, waiting for transfers between devices, exchange(): lax.all_to_all(value.reshape(experts, -1, value.shape[-1]), 'expert', spl...  17.3 us
    all_to_all x3, starting transfers between devices, exchange(): lax.all_to_all(value.reshape(experts, -1, value.shape[-1]), 'expert', spl...  14.8 us
  transfers between devices with their start and end apart: 31, of which 19 were waited for; matrix products, arithmetic and copies ran while one was open for 6% of the time, Pallas kernels for 18%

profile of v2, /device:TPU:8, one launch (start us, length us, event | category | flops | bytes accessed | tf_op | source)
XLA Modules:
  0.0 259.0 jit_solution(7228297544376804698)
XLA Ops:
  7.2 5.9 %collective-permute-start.1 = (bf16[256,128]{1,0:T(8,128)(2,1)}, bf16[256,128]{1,0:T(8,128)(2,1)S(1)}, u32[]{:S(2)}, u32[]{:S(2)}) collective-permute-start(bf16[256,128]{1,0:T(8,128)(2,1)} %param.13), channel_id=1, source_target_pairs={{0,56},{8,0},{16,8},{24,16},{32,24},{40,32},{48,40},{56,48},{64,12... | collective-permute-start | bytes 196616 | tf_op jit(solution)/shard_map/ppermute | solution.py:18
  13.1 0.8 copy.58
  14.6 1.3 fusion.25
  15.9 1.9 select_reduce_fusion
  17.8 0.9 convolution_convert_fusion
  18.8 2.0 collective-permute-start.2
  20.8 4.9 %all-to-all-start = ((bf16[8,80,128]{2,1,0:T(8,128)(2,1)}), bf16[8,80,128]{2,1,0:T(8,128)(2,1)S(1)}, u32[]{:S(2)}, u32[]{:S(2)}) async-start(bf16[8,80,128]{2,1,0:T(8,128)(2,1)} %bitcast.6), calls=%async_computation | async-start | bytes 327680 | tf_op jit(solution)/shard_map/all_to_all | solution.py:296
  25.8 3.2 %collective-permute-start.3 = (bf16[2,256,128]{2,1,0:T(8,128)(2,1)S(1)}, bf16[2,256,128]{2,1,0:T(8,128)(2,1)S(1)}, u32[]{:S(2)}, u32[]{:S(2)}) collective-permute-start(bf16[2,256,128]{2,1,0:T(8,128)(2,1)S(1)} %slice.45), channel_id=1, source_target_pairs={{0,40},{8,48},{16,56},{24,0},{32,8},{40,16},{48,24},{56,32},{64,10... | collective-permute-start | bytes 393224 | tf_op jit(solution)/shard_map/ppermute | solution.py:18
  29.0 5.7 %collective-permute-done.3 = bf16[2,256,128]{2,1,0:T(8,128)(2,1)S(1)} collective-permute-done((bf16[2,256,128]{2,1,0:T(8,128)(2,1)S(1)}, bf16[2,256,128]{2,1,0:T(8,128)(2,1)S(1)}, u32[]{:S(2)}, u32[]{:S(2)}) %collective-permute-start.3) | collective-permute-done | bytes 131104 | tf_op jit(solution)/shard_map/ppermute | solution.py:18
  34.6 2.8 %collective-permute-start.6 = (bf16[640,128]{1,0:T(8,128)(2,1)S(1)}, bf16[640,128]{1,0:T(8,128)(2,1)S(1)}, u32[]{:S(2)}, u32[]{:S(2)}) collective-permute-start(bf16[640,128]{1,0:T(8,128)(2,1)S(1)} %bitcast.158), channel_id=1, source_target_pairs={{0,192},{8,200},{16,208},{24,216},{32,224},{40,232},{48,240},{56,2... | collective-permute-start | bytes 491528 | tf_op jit(solution)/shard_map/ppermute | solution.py:23
  37.4 0.8 collective-permute-start.5
  38.2 0.9 collective-permute-start.4
  39.1 3.9 %collective-permute-done.6 = bf16[640,128]{1,0:T(8,128)(2,1)S(1)} collective-permute-done((bf16[640,128]{1,0:T(8,128)(2,1)S(1)}, bf16[640,128]{1,0:T(8,128)(2,1)S(1)}, u32[]{:S(2)}, u32[]{:S(2)}) %collective-permute-start.6) | collective-permute-done | bytes 163872 | tf_op jit(solution)/shard_map/ppermute | solution.py:23
  43.0 2.0 collective-permute-done.5
  44.9 1.7 collective-permute-done.4
  46.8 0.9 pad_maximum_fusion.2
  48.3 0.5 multiply_convert_fusion
  48.8 22.2 %all_to_all.20 = bf16[8,80,1024]{2,1,0:T(8,128)(2,1)S(1)} all-to-all(bf16[8,80,1024]{2,1,0:T(8,128)(2,1)S(1)} %bitcast.148), channel_id=1, replica_groups=mesh['section'=32,'expert'=8] {'expert'}, dimensions={0} | all-to-all | bytes 2621440 | tf_op jit(solution)/shard_map/all_to_all | solution.py:296
  71.3 3.2 %collective-permute-start.10 = (bf16[640,512]{1,0:T(8,128)(2,1)S(1)}, bf16[640,512]{1,0:T(8,128)(2,1)}, u32[]{:S(2)}, u32[]{:S(2)}) collective-permute-start(bf16[640,512]{1,0:T(8,128)(2,1)S(1)} %get-tuple-element.85.refs_1_.refs_5_), channel_id=1, source_target_pairs={{0,192},{8,200},{16,208},{24,216},{32,224},{40,232},{48,240},{56,2... | collective-permute-start | bytes 1966088 | tf_op jit(solution)/shard_map/ppermute | solution.py:23
  74.5 3.2 %collective-permute-start.9 = (bf16[640,512]{1,0:T(8,128)(2,1)S(1)}, bf16[640,512]{1,0:T(8,128)(2,1)S(1)}, u32[]{:S(2)}, u32[]{:S(2)}) collective-permute-start(bf16[640,512]{1,0:T(8,128)(2,1)S(1)} %get-tuple-element.86.refs_0_.refs_4_), channel_id=1, source_target_pairs={{0,192},{8,200},{16,208},{24,216},{32,224},{40,232},{48,240},{56,2... | collective-permute-start | bytes 1966088 | tf_op jit(solution)/shard_map/ppermute | solution.py:23
  77.7 12.5 %collective-permute-done.7.refs_2_.refs_6_ = bf16[640,512]{1,0:T(8,128)(2,1)} collective-permute-done((bf16[640,512]{1,0:T(8,128)(2,1)S(1)}, bf16[640,512]{1,0:T(8,128)(2,1)}, u32[]{:S(2)}, u32[]{:S(2)}) %collective-permute-start.7) | collective-permute-done | bytes 655392 | tf_op jit(solution)/shard_map/ppermute | solution.py:23
  90.2 3.3 %collective-permute-start.12 = (bf16[640,512]{1,0:T(8,128)(2,1)}, bf16[640,512]{1,0:T(8,128)(2,1)}, u32[]{:S(2)}, u32[]{:S(2)}) collective-permute-start(bf16[640,512]{1,0:T(8,128)(2,1)} %collective-permute-done.10.refs_5_.refs_11_), channel_id=1, source_target_pairs={{0,192},{8,200},{16,208},{24,216},{32,224},{40,232},{48,240},{56,2... | collective-permute-start | bytes 1966088 | tf_op jit(solution)/shard_map/ppermute | solution.py:23
  93.5 10.7 %collective-permute-done.8.refs_3_.refs_7_ = bf16[640,512]{1,0:T(8,128)(2,1)S(1)} collective-permute-done((bf16[640,512]{1,0:T(8,128)(2,1)S(1)}, bf16[640,512]{1,0:T(8,128)(2,1)S(1)}, u32[]{:S(2)}, u32[]{:S(2)}) %collective-permute-start.8) | collective-permute-done | bytes 655392 | tf_op jit(solution)/shard_map/ppermute | solution.py:23
  104.1 0.9 copy-done.2
  105.0 0.8 copy-done.3
  105.8 5.6 %shard_map.118.refs_3_ = f32[640,256]{1,0:T(8,128)} custom-call(s32[1]{0:T(128)} %bitcast.2.x_ref, bf16[640,512]{1,0:T(8,128)(2,1)} %copy-done.1, bf16[640,512]{1,0:T(8,128)(2,1)} %copy-done, bf16[640,512]{1,0:T(8,128)(2,1)} %collective-permute-done.7.refs_2_.refs_6_, bf16[640,512]{1,0:T(8,128)(2,1)} %copy-done.2, bf16[640,512]{1,0:T(8,128)(2,1)} %copy-done.3, ...), custom_call_target="tpu_custom_call" | custom-call | tf_op jit(solution)/shard_map/pallas_call | solution.py:241
  111.4 3.7 %all-gather.2.cloned.1.call-done.tok_ref.refs_0_ = bf16[640,4096]{1,0:T(8,128)(2,1)} async-done(((bf16[640,512]{1,0:T(8,128)(2,1)}), bf16[640,4096]{1,0:T(8,128)(2,1)}) %all-gather.2.cloned.1.call-update) | async-done | bytes 5242896 | tf_op jit(solution)/shard_map/all_gather | solution.py:309
  115.1 14.9 %shard_map.119 = (f32[640,256]{1,0:T(8,128)}, f32[640,256]{1,0:T(8,128)}, bf16[640,256]{1,0:T(8,128)(2,1)}, bf16[640,512]{1,0:T(8,128)(2,1)}, bf16[640,512]{1,0:...) custom-call(s32[1]{0:T(128)} %bitcast.2.x_ref, ...), custom_call_target="tpu_custom_call" | custom-call | flops 4026531840 | bytes 16777216 | tf_op jit(solution)/shard_map/pallas_call | solution.py:241
  130.0 1.5 collective-permute-start.13
  131.5 1.8 collective-permute-start.14
  133.3 12.4 %shard_map.120 = (bf16[8,648,512]{2,1,0:T(8,128)(2,1)}, bf16[640,256]{1,0:T(8,128)(2,1)}, bf16[640,256]{1,0:T(8,128)(2,1)}) custom-call(s32[1]{0:T(128)} %bitcast.2.x_ref, bf16[640,512]{1,0:T(8,128)(2,1)} %collective-permute-done.11.refs_0_.refs_8_, bf16[640,512]{1,0:T(8,128)(2,1)} %collective-permute-done.12.refs_1_.refs_9_, bf16[256,4096]{1,0:T(8,128)(2,1)} %bitcast.144, ...), custom_call_target="tpu_custom_call" | custom-call | tf_op jit(solution)/shard_map/pallas_call | solution.py:241
  145.7 2.3 collective-permute-done.13
  148.0 1.4 collective-permute-start.16
  149.5 1.9 collective-permute-start.17
  151.4 2.1 add_convert_fusion.3
  153.6 1.0 add_convert_fusion.2
  154.6 3.1 %collective-permute-start.18 = (bf16[640,512]{1,0:T(8,128)(2,1)}, bf16[640,512]{1,0:T(8,128)(2,1)}, u32[]{:S(2)}, u32[]{:S(2)}) collective-permute-start(bf16[640,512]{1,0:T(8,128)(2,1)} %add_convert_fusion.2), channel_id=1, source_target_pairs={{0,192},{8,200},{16,208},{24,216},{32,224},{40,232},{48,240},{56,2... | collective-permute-start | bytes 1966088 | tf_op jit(solution)/shard_map/ppermute | solution.py:23
  157.7 14.7 %shard_map.121 = (bf16[4,8,128,256]{3,2,1,0:T(8,128)(2,1)}, bf16[4,8,128,256]{3,2,1,0:T(8,128)(2,1)}, bf16[256,4096]{1,0:T(8,128)(2,1)}) custom-call(s32[1]{0:T(128)} %bitcast.2.x_ref, bf16[640,4096]{1,0:T(8,128)(2,1)} %all-gather.2.cloned.1.call-done.tok_ref.refs_0_, bf16[640,256]{1,0:T(8,128)(2,1)} %get-tuple-element.64.refs_1_, ...), custom_call_target="tpu_custom_call" | custom-call | tf_op jit(solution)/shard_map/pallas_call | solution.py:241
  172.4 6.8 %collective-permute-done.15 = bf16[640,512]{1,0:T(8,128)(2,1)} collective-permute-done((bf16[640,512]{1,0:T(8,128)(2,1)}, bf16[640,512]{1,0:T(8,128)(2,1)}, u32[]{:S(2)}, u32[]{:S(2)}) %collective-permute-start.15) | collective-permute-done | bytes 655392 | tf_op jit(solution)/shard_map/ppermute | solution.py:23
  179.2 2.4 add_convert_fusion
  181.7 1.3 pad_maximum_fusion
  183.0 5.0 %all-to-all-start.2 = ((bf16[8,80,1024]{2,1,0:T(8,128)(2,1)}), bf16[8,80,1024]{2,1,0:T(8,128)(2,1)S(1)}, u32[]{:S(2)}, u32[]{:S(2)}) async-start(bf16[8,80,1024]{2,1,0:T(8,128)(2,1)} %bitcast.29), calls=%async_computation.2 | async-start | bytes 2621440 | tf_op jit(solution)/shard_map/all_to_all | solution.py:296
  187.9 17.3 %all-to-all-done.2 = bf16[8,80,1024]{2,1,0:T(8,128)(2,1)S(1)} async-done(((bf16[8,80,1024]{2,1,0:T(8,128)(2,1)}), bf16[8,80,1024]{2,1,0:T(8,128)(2,1)S(1)}, u32[]{:S(2)}, u32[]{:S(2)}) %all-to-all-start.2) | async-done | bytes 1310752 | tf_op jit(solution)/shard_map/all_to_all | solution.py:296
  205.3 1.4 fusion.31
  206.7 5.8 %reduce-scatter.2.cloned.1.call-done = bf16[648,512]{1,0:T(8,128)(2,1)} async-done(((bf16[5184,512]{1,0:T(8,128)(2,1)}), bf16[648,512]{1,0:T(8,128)(2,1)}) %reduce-scatter.2.cloned.1.call-update) | async-done | bytes 663568 | tf_op jit(solution)/shard_map/reduce_scatter | solution.py:386
  212.7 0.7 constant_dynamic-slice_fusion.1
  213.5 3.0 %collective-permute-start.20 = (bf16[2,256,128]{2,1,0:T(8,128)(2,1)S(1)}, bf16[2,256,128]{2,1,0:T(8,128)(2,1)S(1)}, u32[]{:S(2)}, u32[]{:S(2)}) collective-permute-start(bf16[2,256,128]{2,1,0:T(8,128)(2,1)S(1)} %pad_maximum_fusion.5), channel_id=1, source_target_pairs={{0,40},{8,48},{16,56},{24,0},{32,8},{40,16},{48,24},{56,32},{64,10... | collective-permute-start | bytes 393224 | tf_op jit(solution)/shard_map/ppermute | solution.py:18
  216.7 0.9 collective-permute-start.19
  217.7 0.9 fusion.2
  218.7 5.0 %all-to-all-start.3 = ((bf16[8,88,512]{2,1,0:T(8,128)(2,1)}), bf16[8,88,512]{2,1,0:T(8,128)(2,1)S(1)}, u32[]{:S(2)}, u32[]{:S(2)}) async-start(bf16[8,88,512]{2,1,0:T(8,128)(2,1)} %fusion.2), calls=%async_computation.4 | async-start | bytes 1441792 | tf_op jit(solution)/shard_map/all_to_all | solution.py:296
  223.6 1.7 collective-permute-done.20
  225.3 5.5 %collective-permute-done.19 = bf16[3,256,128]{2,1,0:T(8,128)(2,1)S(1)} collective-permute-done((bf16[3,256,128]{2,1,0:T(8,128)(2,1)S(1)}, bf16[3,256,128]{2,1,0:T(8,128)(2,1)S(1)}, u32[]{:S(2)}, u32[]{:S(2)}) %collective-permute-start.19) | collective-permute-done | bytes 196640 | tf_op jit(solution)/shard_map/ppermute | solution.py:18
  231.2 4.1 %collective-permute-start.21 = (bf16[256,128]{1,0:T(8,128)(2,1)S(1)}, bf16[256,128]{1,0:T(8,128)(2,1)S(1)}, u32[]{:S(2)}, u32[]{:S(2)}) collective-permute-start(bf16[256,128]{1,0:T(8,128)(2,1)S(1)} %get-tuple-element.102), channel_id=1, source_target_pairs={{0,8},{8,16},{16,24},{24,32},{32,40},{40,48},{48,56},{56,0},{64,72... | collective-permute-start | bytes 196616 | tf_op jit(solution)/shard_map/ppermute | solution.py:18
  235.2 2.2 collective-permute-done.22
  237.4 2.2 collective-permute-done.21
  239.6 0.7 fusion.18
  241.0 0.4 fusion.4
  241.5 2.8 %collective-permute-start.25 = (bf16[264,128]{1,0:T(8,128)(2,1)S(1)}, bf16[264,128]{1,0:T(8,128)(2,1)S(1)}, u32[]{:S(2)}, u32[]{:S(2)}) collective-permute-start(bf16[264,128]{1,0:T(8,128)(2,1)S(1)} %get-tuple-element.108), channel_id=1, source_target_pairs={{0,192},{8,200},{16,208},{24,216},{32,224},{40,232},{48,240},{56,2... | collective-permute-start | bytes 202760 | tf_op jit(solution)/shard_map/ppermute | solution.py:23
  244.3 0.8 collective-permute-start.24
  245.1 0.9 collective-permute-start.23
  246.2 3.9 %collective-permute-done.24 = bf16[264,128]{1,0:T(8,128)(2,1)S(1)} collective-permute-done((bf16[264,128]{1,0:T(8,128)(2,1)S(1)}, bf16[264,128]{1,0:T(8,128)(2,1)S(1)}, u32[]{:S(2)}, u32[]{:S(2)}) %collective-permute-start.24) | collective-permute-done | bytes 67616 | tf_op jit(solution)/shard_map/ppermute | solution.py:23
  250.1 0.7 collective-permute-done.23
  250.9 0.7 fusion.8
  251.5 0.6 bitcast_divide_fusion
  (106 shorter events, 3.4 us)
Async XLA Ops:
  7.2 11.6 %copy-start.10 = (bf16[256,128]{1,0:T(8,128)(2,1)S(1)}, bf16[256,128]{1,0:T(8,128)(2,1)}, u32[]{:S(2)}) copy-start(bf16[256,128]{1,0:T(8,128)(2,1)} %param.13) | copy-start | bytes 196612
  7.2 10.6 %copy-start.8 = (bf16[256,128]{1,0:T(8,128)(2,1)S(1)}, bf16[256,128]{1,0:T(8,128)(2,1)}, u32[]{:S(2)}) copy-start(bf16[256,128]{1,0:T(8,128)(2,1)} %param.7) | copy-start | bytes 196612
  7.2 11.5 %collective-permute-start.1 = (bf16[256,128]{1,0:T(8,128)(2,1)}, bf16[256,128]{1,0:T(8,128)(2,1)S(1)}, u32[]{:S(2)}, u32[]{:S(2)}) collective-permute-start(bf16[256,128]{1,0:T(8,128)(2,1)} %param.13), channel_id=1, source_target_pairs={{0,56},{8,0},{16,8},{24,16},{32,24},{40,32},{48,40},{56,48},{64,12... | collective-permute-start | bytes 196616 | tf_op jit(solution)/shard_map/ppermute | solution.py:18
  13.1 5.7 %collective-permute-start = (bf16[256,128]{1,0:T(8,128)(2,1)}, bf16[256,128]{1,0:T(8,128)(2,1)S(1)}, u32[]{:S(2)}, u32[]{:S(2)}) collective-permute-start(bf16[256,128]{1,0:T(8,128)(2,1)} %param.13), channel_id=1, source_target_pairs={{0,8},{8,16},{16,24},{24,32},{32,40},{40,48},{48,56},{56,0},{64,72... | collective-permute-start | bytes 196616 | tf_op jit(solution)/shard_map/ppermute | solution.py:18
  18.8 15.8 %collective-permute-start.2 = (bf16[3,256,128]{2,1,0:T(8,128)(2,1)S(1)}, bf16[3,256,128]{2,1,0:T(8,128)(2,1)S(1)}, u32[]{:S(2)}, u32[]{:S(2)}) collective-permute-start(bf16[3,256,128]{2,1,0:T(8,128)(2,1)S(1)} %pad_maximum_fusion.3), channel_id=1, source_target_pairs={{0,24},{8,32},{16,40},{24,48},{32,56},{40,0},{48,8},{56,16},{64,88... | collective-permute-start | bytes 589832 | tf_op jit(solution)/shard_map/ppermute | solution.py:18
  20.8 13.8 %all-to-all-start = ((bf16[8,80,128]{2,1,0:T(8,128)(2,1)}), bf16[8,80,128]{2,1,0:T(8,128)(2,1)S(1)}, u32[]{:S(2)}, u32[]{:S(2)}) async-start(bf16[8,80,128]{2,1,0:T(8,128)(2,1)} %bitcast.6), calls=%async_computation | async-start | bytes 327680 | tf_op jit(solution)/shard_map/all_to_all | solution.py:296
  25.7 89.4 %all-gather.2.cloned.1.call-start = ((), (), s32[]{:S(2)}) async-start(), calls=%async_computation.5 | async-start | bytes 5898240 | tf_op jit(solution)/shard_map/all_gather | solution.py:309
  25.8 8.9 %collective-permute-start.3 = (bf16[2,256,128]{2,1,0:T(8,128)(2,1)S(1)}, bf16[2,256,128]{2,1,0:T(8,128)(2,1)S(1)}, u32[]{:S(2)}, u32[]{:S(2)}) collective-permute-start(bf16[2,256,128]{2,1,0:T(8,128)(2,1)S(1)} %slice.45), channel_id=1, source_target_pairs={{0,40},{8,48},{16,56},{24,0},{32,8},{40,16},{48,24},{56,32},{64,10... | collective-permute-start | bytes 393224 | tf_op jit(solution)/shard_map/ppermute | solution.py:18
  34.6 8.3 %collective-permute-start.6 = (bf16[640,128]{1,0:T(8,128)(2,1)S(1)}, bf16[640,128]{1,0:T(8,128)(2,1)S(1)}, u32[]{:S(2)}, u32[]{:S(2)}) collective-permute-start(bf16[640,128]{1,0:T(8,128)(2,1)S(1)} %bitcast.158), channel_id=1, source_target_pairs={{0,192},{8,200},{16,208},{24,216},{32,224},{40,232},{48,240},{56,2... | collective-permute-start | bytes 491528 | tf_op jit(solution)/shard_map/ppermute | solution.py:23
  37.4 7.6 %collective-permute-start.5 = (bf16[640,128]{1,0:T(8,128)(2,1)S(1)}, bf16[640,128]{1,0:T(8,128)(2,1)S(1)}, u32[]{:S(2)}, u32[]{:S(2)}) collective-permute-start(bf16[640,128]{1,0:T(8,128)(2,1)S(1)} %bitcast.159), channel_id=1, source_target_pairs={{0,128},{8,136},{16,144},{24,152},{32,160},{40,168},{48,176},{56,1... | collective-permute-start | bytes 491528 | tf_op jit(solution)/shard_map/ppermute | solution.py:23
  38.2 8.5 %collective-permute-start.4 = (bf16[640,128]{1,0:T(8,128)(2,1)S(1)}, bf16[640,128]{1,0:T(8,128)(2,1)S(1)}, u32[]{:S(2)}, u32[]{:S(2)}) collective-permute-start(bf16[640,128]{1,0:T(8,128)(2,1)S(1)} %bitcast.160), channel_id=1, source_target_pairs={{0,64},{8,72},{16,80},{24,88},{32,96},{40,104},{48,112},{56,120},{... | collective-permute-start | bytes 491528 | tf_op jit(solution)/shard_map/ppermute | solution.py:23
  47.7 164.8 %reduce-scatter.2.cloned.1.call-start = ((), (), s32[]{:S(2)}) async-start(), calls=%async_computation.6 | async-start | bytes 5971968 | tf_op jit(solution)/shard_map/reduce_scatter | solution.py:386
  71.2 33.0 %copy-start.1 = (bf16[640,512]{1,0:T(8,128)(2,1)}, bf16[640,512]{1,0:T(8,128)(2,1)S(1)}, u32[]{:S(2)}) copy-start(bf16[640,512]{1,0:T(8,128)(2,1)S(1)} %get-tuple-element.86.refs_0_.refs_4_) | copy-start | bytes 1966084
  71.2 34.7 %copy-start = (bf16[640,512]{1,0:T(8,128)(2,1)}, bf16[640,512]{1,0:T(8,128)(2,1)S(1)}, u32[]{:S(2)}) copy-start(bf16[640,512]{1,0:T(8,128)(2,1)S(1)} %get-tuple-element.85.refs_1_.refs_5_) | copy-start | bytes 1966084
  71.2 19.0 %collective-permute-start.7 = (bf16[640,512]{1,0:T(8,128)(2,1)S(1)}, bf16[640,512]{1,0:T(8,128)(2,1)}, u32[]{:S(2)}, u32[]{:S(2)}) collective-permute-start(bf16[640,512]{1,0:T(8,128)(2,1)S(1)} %get-tuple-element.86.refs_0_.refs_4_), channel_id=1, source_target_pairs={{0,64},{8,72},{16,80},{24,88},{32,96},{40,104},{48,112},{56,120},{... | collective-permute-start | bytes 1966088 | tf_op jit(solution)/shard_map/ppermute | solution.py:23
  71.3 18.9 %collective-permute-start.10 = (bf16[640,512]{1,0:T(8,128)(2,1)S(1)}, bf16[640,512]{1,0:T(8,128)(2,1)}, u32[]{:S(2)}, u32[]{:S(2)}) collective-permute-start(bf16[640,512]{1,0:T(8,128)(2,1)S(1)} %get-tuple-element.85.refs_1_.refs_5_), channel_id=1, source_target_pairs={{0,192},{8,200},{16,208},{24,216},{32,224},{40,232},{48,240},{56,2... | collective-permute-start | bytes 1966088 | tf_op jit(solution)/shard_map/ppermute | solution.py:23
  74.5 29.6 %collective-permute-start.8 = (bf16[640,512]{1,0:T(8,128)(2,1)S(1)}, bf16[640,512]{1,0:T(8,128)(2,1)S(1)}, u32[]{:S(2)}, u32[]{:S(2)}) collective-permute-start(bf16[640,512]{1,0:T(8,128)(2,1)S(1)} %get-tuple-element.85.refs_1_.refs_5_), channel_id=1, source_target_pairs={{0,64},{8,72},{16,80},{24,88},{32,96},{40,104},{48,112},{56,120},{... | collective-permute-start | bytes 1966088 | tf_op jit(solution)/shard_map/ppermute | solution.py:23
  74.5 29.6 %collective-permute-start.9 = (bf16[640,512]{1,0:T(8,128)(2,1)S(1)}, bf16[640,512]{1,0:T(8,128)(2,1)S(1)}, u32[]{:S(2)}, u32[]{:S(2)}) collective-permute-start(bf16[640,512]{1,0:T(8,128)(2,1)S(1)} %get-tuple-element.86.refs_0_.refs_4_), channel_id=1, source_target_pairs={{0,192},{8,200},{16,208},{24,216},{32,224},{40,232},{48,240},{56,2... | collective-permute-start | bytes 1966088 | tf_op jit(solution)/shard_map/ppermute | solution.py:23
  90.2 43.1 %collective-permute-start.11 = (bf16[640,512]{1,0:T(8,128)(2,1)}, bf16[640,512]{1,0:T(8,128)(2,1)}, u32[]{:S(2)}, u32[]{:S(2)}) collective-permute-start(bf16[640,512]{1,0:T(8,128)(2,1)} %collective-permute-done.7.refs_2_.refs_6_), channel_id=1, source_target_pairs={{0,64},{8,72},{16,80},{24,88},{32,96},{40,104},{48,112},{56,120},{... | collective-permute-start | bytes 1966088 | tf_op jit(solution)/shard_map/ppermute | solution.py:23
  90.2 43.1 %collective-permute-start.12 = (bf16[640,512]{1,0:T(8,128)(2,1)}, bf16[640,512]{1,0:T(8,128)(2,1)}, u32[]{:S(2)}, u32[]{:S(2)}) collective-permute-start(bf16[640,512]{1,0:T(8,128)(2,1)} %collective-permute-done.10.refs_5_.refs_11_), channel_id=1, source_target_pairs={{0,192},{8,200},{16,208},{24,216},{32,224},{40,232},{48,240},{56,2... | collective-permute-start | bytes 1966088 | tf_op jit(solution)/shard_map/ppermute | solution.py:23
  104.1 0.9 copy-start.2
  105.0 0.8 copy-start.3
  130.0 18.0 %collective-permute-start.13 = (bf16[640,512]{1,0:T(8,128)(2,1)}, bf16[640,512]{1,0:T(8,128)(2,1)}, u32[]{:S(2)}, u32[]{:S(2)}) collective-permute-start(bf16[640,512]{1,0:T(8,128)(2,1)} %get-tuple-element.57), channel_id=1, source_target_pairs={{0,64},{8,72},{16,80},{24,88},{32,96},{40,104},{48,112},{56,120},{... | collective-permute-start | bytes 1966088 | tf_op jit(solution)/shard_map/ppermute | solution.py:23
  131.5 16.5 %collective-permute-start.14 = (bf16[640,512]{1,0:T(8,128)(2,1)}, bf16[640,512]{1,0:T(8,128)(2,1)S(1)}, u32[]{:S(2)}, u32[]{:S(2)}) collective-permute-start(bf16[640,512]{1,0:T(8,128)(2,1)} %get-tuple-element.58), channel_id=1, source_target_pairs={{0,192},{8,200},{16,208},{24,216},{32,224},{40,232},{48,240},{56,2... | collective-permute-start | bytes 1966088 | tf_op jit(solution)/shard_map/ppermute | solution.py:23
  148.0 3.4 %copy-start.7 = (bf16[640,512]{1,0:T(8,128)(2,1)S(1)}, bf16[640,512]{1,0:T(8,128)(2,1)}, u32[]{:S(2)}) copy-start(bf16[640,512]{1,0:T(8,128)(2,1)} %get-tuple-element.51) | copy-start | bytes 1966084
  148.0 5.6 %copy-start.6 = (bf16[640,512]{1,0:T(8,128)(2,1)S(1)}, bf16[640,512]{1,0:T(8,128)(2,1)}, u32[]{:S(2)}) copy-start(bf16[640,512]{1,0:T(8,128)(2,1)} %get-tuple-element.62) | copy-start | bytes 1966084
  148.0 24.4 %collective-permute-start.16 = (bf16[640,512]{1,0:T(8,128)(2,1)}, bf16[640,512]{1,0:T(8,128)(2,1)}, u32[]{:S(2)}, u32[]{:S(2)}) collective-permute-start(bf16[640,512]{1,0:T(8,128)(2,1)} %get-tuple-element.60), channel_id=1, source_target_pairs={{0,64},{8,72},{16,80},{24,88},{32,96},{40,104},{48,112},{56,120},{... | collective-permute-start | bytes 1966088 | tf_op jit(solution)/shard_map/ppermute | solution.py:23
  149.5 23.0 %collective-permute-start.17 = (bf16[640,512]{1,0:T(8,128)(2,1)}, bf16[640,512]{1,0:T(8,128)(2,1)}, u32[]{:S(2)}, u32[]{:S(2)}) collective-permute-start(bf16[640,512]{1,0:T(8,128)(2,1)} %get-tuple-element.61), channel_id=1, source_target_pairs={{0,192},{8,200},{16,208},{24,216},{32,224},{40,232},{48,240},{56,2... | collective-permute-start | bytes 1966088 | tf_op jit(solution)/shard_map/ppermute | solution.py:23
  153.5 25.8 %collective-permute-start.15 = (bf16[640,512]{1,0:T(8,128)(2,1)}, bf16[640,512]{1,0:T(8,128)(2,1)}, u32[]{:S(2)}, u32[]{:S(2)}) collective-permute-start(bf16[640,512]{1,0:T(8,128)(2,1)} %add_convert_fusion.3), channel_id=1, source_target_pairs={{0,64},{8,72},{16,80},{24,88},{32,96},{40,104},{48,112},{56,120},{... | collective-permute-start | bytes 1966088 | tf_op jit(solution)/shard_map/ppermute | solution.py:23
  154.6 24.6 %collective-permute-start.18 = (bf16[640,512]{1,0:T(8,128)(2,1)}, bf16[640,512]{1,0:T(8,128)(2,1)}, u32[]{:S(2)}, u32[]{:S(2)}) collective-permute-start(bf16[640,512]{1,0:T(8,128)(2,1)} %add_convert_fusion.2), channel_id=1, source_target_pairs={{0,192},{8,200},{16,208},{24,216},{32,224},{40,232},{48,240},{56,2... | collective-permute-start | bytes 1966088 | tf_op jit(solution)/shard_map/ppermute | solution.py:23
  157.7 21.5 %copy-start.5 = (bf16[640,512]{1,0:T(8,128)(2,1)S(1)}, bf16[640,512]{1,0:T(8,128)(2,1)}, u32[]{:S(2)}) copy-start(bf16[640,512]{1,0:T(8,128)(2,1)} %get-tuple-element.50) | copy-start | bytes 1966084
  183.0 22.3 %copy-start.4 = (f32[640,256]{1,0:T(8,128)S(1)}, f32[640,256]{1,0:T(8,128)}, u32[]{:S(2)}) copy-start(f32[640,256]{1,0:T(8,128)} %get-tuple-element.81) | copy-start | bytes 1966084
  183.0 22.3 %all-to-all-start.2 = ((bf16[8,80,1024]{2,1,0:T(8,128)(2,1)}), bf16[8,80,1024]{2,1,0:T(8,128)(2,1)S(1)}, u32[]{:S(2)}, u32[]{:S(2)}) async-start(bf16[8,80,1024]{2,1,0:T(8,128)(2,1)} %bitcast.29), calls=%async_computation.2 | async-start | bytes 2621440 | tf_op jit(solution)/shard_map/all_to_all | solution.py:296
  213.5 4.1 %slice-start = ((bf16[648,512]{1,0:T(8,128)(2,1)}), bf16[4,512]{1,0:T(4,128)(2,1)S(1)}, s32[]{:S(2)}) async-start(bf16[648,512]{1,0:T(8,128)(2,1)} %reduce-scatter.2.cloned.1.call-done), calls=%async_computation.7 | async-start | bytes 8192 | tf_op jit(solution)/shard_map/slice | solution.py:420
  213.5 4.3 %slice-start.1 = ((bf16[648,512]{1,0:T(8,128)(2,1)}), bf16[640,512]{1,0:T(8,128)(2,1)S(1)}, s32[]{:S(2)}) async-start(bf16[648,512]{1,0:T(8,128)(2,1)} %reduce-scatter.2.cloned.1.call-done), calls=%async_computation.8 | async-start | bytes 1310720 | tf_op jit(solution)/shard_map/slice | solution.py:423
  213.5 11.8 %collective-permute-start.20 = (bf16[2,256,128]{2,1,0:T(8,128)(2,1)S(1)}, bf16[2,256,128]{2,1,0:T(8,128)(2,1)S(1)}, u32[]{:S(2)}, u32[]{:S(2)}) collective-permute-start(bf16[2,256,128]{2,1,0:T(8,128)(2,1)S(1)} %pad_maximum_fusion.5), channel_id=1, source_target_pairs={{0,40},{8,48},{16,56},{24,0},{32,8},{40,16},{48,24},{56,32},{64,10... | collective-permute-start | bytes 393224 | tf_op jit(solution)/shard_map/ppermute | solution.py:18
  216.7 14.2 %collective-permute-start.19 = (bf16[3,256,128]{2,1,0:T(8,128)(2,1)S(1)}, bf16[3,256,128]{2,1,0:T(8,128)(2,1)S(1)}, u32[]{:S(2)}, u32[]{:S(2)}) collective-permute-start(bf16[3,256,128]{2,1,0:T(8,128)(2,1)S(1)} %pad_maximum_fusion.4), channel_id=1, source_target_pairs={{0,24},{8,32},{16,40},{24,48},{32,56},{40,0},{48,8},{56,16},{64,88... | collective-permute-start | bytes 589832 | tf_op jit(solution)/shard_map/ppermute | solution.py:18
  218.7 16.6 %copy-start.13 = (s32[1,2,2,128]{3,2,1,0:T(2,128)S(1)}, s32[1,2,2,128]{3,2,1,0:T(2,128)}, u32[]{:S(2)}) copy-start(s32[1,2,2,128]{3,2,1,0:T(2,128)} %get-tuple-element.104) | copy-start | bytes 6148
  218.7 20.9 %copy-start.9 = (bf16[256,128]{1,0:T(8,128)(2,1)S(1)}, bf16[256,128]{1,0:T(8,128)(2,1)}, u32[]{:S(2)}) copy-start(bf16[256,128]{1,0:T(8,128)(2,1)} %param.7) | copy-start | bytes 196612
  218.7 21.6 %all-to-all-start.3 = ((bf16[8,88,512]{2,1,0:T(8,128)(2,1)}), bf16[8,88,512]{2,1,0:T(8,128)(2,1)S(1)}, u32[]{:S(2)}, u32[]{:S(2)}) async-start(bf16[8,88,512]{2,1,0:T(8,128)(2,1)} %fusion.2), calls=%async_computation.4 | async-start | bytes 1441792 | tf_op jit(solution)/shard_map/all_to_all | solution.py:296
  230.9 6.5 %collective-permute-start.22 = (bf16[256,128]{1,0:T(8,128)(2,1)S(1)}, bf16[256,128]{1,0:T(8,128)(2,1)S(1)}, u32[]{:S(2)}, u32[]{:S(2)}) collective-permute-start(bf16[256,128]{1,0:T(8,128)(2,1)S(1)} %get-tuple-element.103), channel_id=1, source_target_pairs={{0,56},{8,0},{16,8},{24,16},{32,24},{40,32},{48,40},{56,48},{64,12... | collective-permute-start | bytes 196616 | tf_op jit(solution)/shard_map/ppermute | solution.py:18
  231.2 8.4 %collective-permute-start.21 = (bf16[256,128]{1,0:T(8,128)(2,1)S(1)}, bf16[256,128]{1,0:T(8,128)(2,1)S(1)}, u32[]{:S(2)}, u32[]{:S(2)}) collective-permute-start(bf16[256,128]{1,0:T(8,128)(2,1)S(1)} %get-tuple-element.102), channel_id=1, source_target_pairs={{0,8},{8,16},{16,24},{24,32},{32,40},{40,48},{48,56},{56,0},{64,72... | collective-permute-start | bytes 196616 | tf_op jit(solution)/shard_map/ppermute | solution.py:18
  241.0 9.9 %copy-start.11 = (bf16[256,128]{1,0:T(8,128)(2,1)S(1)}, bf16[256,128]{1,0:T(8,128)(2,1)}, u32[]{:S(2)}) copy-start(bf16[256,128]{1,0:T(8,128)(2,1)} %param.13) | copy-start | bytes 196612
  241.0 10.6 %copy-start.12 = (f32[256,2]{0,1:T(2,128)S(1)}, f32[256,2]{0,1:T(2,128)}, u32[]{:S(2)}) copy-start(f32[256,2]{0,1:T(2,128)} %param.9) | copy-start | bytes 6148
  241.5 4.7 %collective-permute-start.25 = (bf16[264,128]{1,0:T(8,128)(2,1)S(1)}, bf16[264,128]{1,0:T(8,128)(2,1)S(1)}, u32[]{:S(2)}, u32[]{:S(2)}) collective-permute-start(bf16[264,128]{1,0:T(8,128)(2,1)S(1)} %get-tuple-element.108), channel_id=1, source_target_pairs={{0,192},{8,200},{16,208},{24,216},{32,224},{40,232},{48,240},{56,2... | collective-permute-start | bytes 202760 | tf_op jit(solution)/shard_map/ppermute | solution.py:23
  244.3 5.8 %collective-permute-start.24 = (bf16[264,128]{1,0:T(8,128)(2,1)S(1)}, bf16[264,128]{1,0:T(8,128)(2,1)S(1)}, u32[]{:S(2)}, u32[]{:S(2)}) collective-permute-start(bf16[264,128]{1,0:T(8,128)(2,1)S(1)} %get-tuple-element.107), channel_id=1, source_target_pairs={{0,128},{8,136},{16,144},{24,152},{32,160},{40,168},{48,176},{56,1... | collective-permute-start | bytes 202760 | tf_op jit(solution)/shard_map/ppermute | solution.py:23
  245.1 5.7 %collective-permute-start.23 = (bf16[264,128]{1,0:T(8,128)(2,1)S(1)}, bf16[264,128]{1,0:T(8,128)(2,1)S(1)}, u32[]{:S(2)}, u32[]{:S(2)}) collective-permute-start(bf16[264,128]{1,0:T(8,128)(2,1)S(1)} %get-tuple-element.106), channel_id=1, source_target_pairs={{0,64},{8,72},{16,80},{24,88},{32,96},{40,104},{48,112},{56,120},{... | collective-permute-start | bytes 202760 | tf_op jit(solution)/shard_map/ppermute | solution.py:23
Sparse Core Ops, SparseCore 0:
  47.9 67.1 all-gather.1
  148.1 64.3 reduce-scatter.1

commit v3 on v2

--- a/solution.py
+++ b/solution.py
@@ -10,6 +10,7 @@
 highest = lax.Precision.HIGHEST
 f32, bf16 = jnp.float32, jnp.bfloat16
 NX, NZ = 4, 8
+PAIR = 2
 Z_GROUPS = [[x * NZ + z for z in range(NZ)] for x in range(NX)]
 
 
@@ -49,17 +50,22 @@
     return high, (value - high.astype(f32)).astype(bf16)
 
 
-def spread_z(value, own):
+def spread_z_far(value, own):
     parts = value.reshape(value.shape[0], NZ, -1).transpose(1, 0, 2)
 
     def part(d):
         return lax.dynamic_index_in_dim(parts, (own + d) % NZ, 0, keepdims=False)
 
-    above = shift_z(jnp.stack([part(2), part(3), part(4)]).astype(bf16), 3).astype(f32)
-    below = shift_z(jnp.stack([part(-3), part(-2)]).astype(bf16), -3).astype(f32)
-    right = shift_z((part(1) + above[2] + below[1]).astype(bf16), 1)
-    left = shift_z((part(-1) + above[0]).astype(bf16), -1)
-    return part(0) + above[1] + below[0] + right.astype(f32) + left.astype(f32)
+    above = shift_z(jnp.stack([part(2), part(3), part(4)]).astype(bf16), 3)
+    below = shift_z(jnp.stack([part(-3), part(-2)]).astype(bf16), -3)
+    return part(-1), part(0), part(1), above, below
+
+
+def spread_z_near(behind, here, ahead, above, below):
+    above, below = above.astype(f32), below.astype(f32)
+    right = shift_z((ahead + above[2] + below[1]).astype(bf16), 1)
+    left = shift_z((behind + above[0]).astype(bf16), -1)
+    return here + above[1] + below[0] + right.astype(f32) + left.astype(f32)
 
 
 def ring_gather_x(value):
@@ -108,42 +114,45 @@
     return lax.dot_general(a, b, (((0,), (0,)), ((), ())), preferred_element_type=f32)
 
 
+def weights_by_z(w_ref, gate_ref, up_ref):
+    ff = gate_ref.shape[-1]
+    for j in range(PAIR):
+        block = slice(j * w_ref.shape[0] // PAIR, (j + 1) * w_ref.shape[0] // PAIR)
+        w_ref[block, :ff] = gate_ref[:, j].reshape(-1, ff)
+        w_ref[block, ff:] = up_ref[:, j].reshape(-1, ff)
+
+
 def forward_kernel(
-    x_ref, tok_ref, gate_ref, up_ref, down_ref, coef_ref, silu_ref, hid_ref, *rest
+    x_ref, tok_ref, gate_ref, up_ref, coef_ref, silu_ref, hid_ref, acc, weights
 ):
-    outs, (acc_gate, acc_up, made) = rest[: 2 * NX], rest[2 * NX :]
     step = pl.program_id(0)
-    width = gate_ref.shape[-1]
+    ff = gate_ref.shape[-1]
 
     @pl.when(step == 0)
     def _():
-        acc_gate[...] = jnp.zeros_like(acc_gate)
-        acc_up[...] = jnp.zeros_like(acc_up)
-
-    @pl.when(step < NZ)
-    def _():
-        block = tok_ref[...]
-        gate = gate_ref[...].reshape(-1, width)
-        up = up_ref[...].reshape(-1, width)
-        acc_gate[...] += jnp.dot(block, gate, preferred_element_type=f32)
-        acc_up[...] += jnp.dot(block, up, preferred_element_type=f32)
-
-    @pl.when(step == NZ - 1)
-    def _():
-        act_gate, act_up = acc_gate[...], acc_up[...]
+        acc[...] = jnp.zeros_like(acc)
+
+    weights_by_z(weights, gate_ref, up_ref)
+    acc[...] += jnp.dot(tok_ref[...], weights[...], preferred_element_type=f32)
+
+    @pl.when(step == NZ // PAIR - 1)
+    def _():
+        act_gate, act_up = acc[:, :ff], acc[:, ff:]
         sig = jax.nn.sigmoid(act_gate)
         silu_gate = act_gate * sig
         silu_ref[...] = silu_gate
         coef_ref[...] = act_up * (sig * (1.0 + act_gate * (1.0 - sig)))
         hid_ref[...] = (silu_gate * act_up).astype(bf16)
 
-    @pl.when(step >= NZ)
-    def _():
-        made[...] = jnp.dot(hid_ref[...], down_ref[...], preferred_element_type=f32).astype(bf16)
+
+def output_kernel(x_ref, hid_ref, down_ref, *rest):
+    outs, made = rest[: 2 * NX], rest[2 * NX]
+    step = pl.program_id(0)
+    made[...] = jnp.dot(hid_ref[...], down_ref[...], preferred_element_type=f32).astype(bf16)
 
     for d in range(NX):
 
-        @pl.when(step == NZ + d)
+        @pl.when(step == d)
         def _(d=d):
             half = made.shape[1] // 2
             outs[2 * d][...] = made[:, :half]
@@ -171,7 +180,7 @@
 
 def backward_kernel(x_ref, *refs):
     far_a, far_b, down_ref, sum_ref, gate_ref, up_ref, coef_ref, silu_ref, hid_ref = refs[:9]
-    part_ref, gate_out, up_out, mix = refs[9:]
+    part_ref, act_out, mix, weights = refs[9:]
     step = pl.program_id(0)
     width = gate_ref.shape[-1]
     rows = sum_ref.shape[0]
@@ -181,8 +190,8 @@
         half = down_ref.shape[1] // 2
         grad_hidden = sum_ref[...] + dot_nt(far_a[...], down_ref[:, :half])
         grad_hidden += dot_nt(far_b[...], down_ref[:, half:])
-        gate_out[...] = (grad_hidden * coef_ref[...]).astype(bf16)
-        up_out[...] = (grad_hidden * silu_ref[...]).astype(bf16)
+        act_out[:, :width] = (grad_hidden * coef_ref[...]).astype(bf16)
+        act_out[:, width:] = (grad_hidden * silu_ref[...]).astype(bf16)
         terms = grad_hidden * hid_ref[...].astype(f32)
         sums = lax.dot_general(
             jnp.ones((8, width), f32),
@@ -206,33 +215,39 @@
 
     @pl.when(step >= 1)
     def _():
-        gate = gate_ref[...].reshape(-1, width)
-        up = up_ref[...].reshape(-1, width)
-        part_ref[0, :rows] = (dot_nt(gate_out[...], gate) + dot_nt(up_out[...], up)).astype(bf16)
-        part_ref[0, rows:] = mix[...]
+        weights_by_z(weights, gate_ref, up_ref)
+        part = dot_nt(act_out[...], weights[...]).astype(bf16)
+        cut = part_ref.shape[2]
+        for j in range(PAIR):
+            part_ref[j, :rows] = part[:, j * cut : (j + 1) * cut]
+            part_ref[j, rows:] = mix[...]
 
 
 def weight_kernel(x_ref, *refs):
-    tok_ref, gact_ref, uact_ref, hid_ref = refs[:4]
-    ups = refs[4 : 4 + 2 * NX]
-    gate_out, up_out, down_out, piece = refs[4 + 2 * NX :]
+    tok_ref, act_ref, hid_ref = refs[:3]
+    ups = refs[3 : 3 + 2 * NX]
+    gate_out, up_out, down_out, piece = refs[3 + 2 * NX :]
     step = pl.program_id(0)
-
-    @pl.when(step < NZ)
-    def _():
-        block = tok_ref[...]
-        gate_out[...] = dot_tn(block, gact_ref[...]).astype(bf16).reshape(gate_out.shape)
-        up_out[...] = dot_tn(block, uact_ref[...]).astype(bf16).reshape(up_out.shape)
+    first = NZ // PAIR
+    ff = hid_ref.shape[1]
+
+    @pl.when(step < first)
+    def _():
+        grad = dot_tn(tok_ref[...], act_ref[...]).astype(bf16)
+        for j in range(PAIR):
+            block = grad[j * grad.shape[0] // PAIR : (j + 1) * grad.shape[0] // PAIR]
+            gate_out[:, j] = block[:, :ff].reshape(NX, -1, ff)
+            up_out[:, j] = block[:, ff:].reshape(NX, -1, ff)
 
     for d in range(NX):
 
-        @pl.when(step == NZ + d)
+        @pl.when(step == first + d)
         def _(d=d):
             half = piece.shape[1] // 2
             piece[:, :half] = ups[2 * d][...]
             piece[:, half:] = ups[2 * d + 1][...]
 
-    @pl.when(step >= NZ)
+    @pl.when(step >= first)
     def _():
         down_out[...] = dot_tn(hid_ref[...], piece[...]).astype(bf16)
 
@@ -318,12 +333,15 @@
         return jnp.clip(i - low, 0, count - 1)
 
     def weight_spec(low):
-        return pl.BlockSpec((NX, 1, feat, ff), lambda i, s: (0, clip(i, low, NZ), 0, 0))
+        return pl.BlockSpec(
+            (NX, PAIR, feat, ff), lambda i, s: (0, clip(i, low, NZ // PAIR), 0, 0)
+        )
 
     def struct(shape, kind):
         return jax.ShapeDtypeStruct(shape, kind)
 
-    tok_spec = pl.BlockSpec((rows, wide_x), lambda i, s: (0, clip(i, 0, NZ)))
+    tok_spec = pl.BlockSpec((rows, PAIR * wide_x), lambda i, s: (0, clip(i, 0, NZ // PAIR)))
+    weight_scratch = pltpu.VMEM((PAIR * wide_x, 2 * ff), bf16)
     (early,) = call(
         early_kernel,
         NX - 1,
@@ -341,46 +359,53 @@
         (where, *ups[:4], *ups[6:], down),
     )
     dispatched, early = lax.optimization_barrier((dispatched, early))
-    coef, silu_gate, hidden, *outs = call(
+    coef, silu_gate, hidden = call(
         forward_kernel,
-        NZ + NX,
-        [
-            tok_spec,
-            weight_spec(0),
-            weight_spec(0),
-            pl.BlockSpec((ff, wide_z), lambda i, s: (0, (s[0] + clip(i, NZ, NX)) % NX)),
-        ],
-        [whole(rows, ff)] * 3 + [whole(rows, wide_z // 2)] * (2 * NX),
-        [struct((rows, ff), f32)] * 2
-        + [struct((rows, ff), bf16)]
-        + [struct((rows, wide_z // 2), bf16)] * (2 * NX),
-        [pltpu.VMEM((rows, ff), f32)] * 2 + [pltpu.VMEM((rows, wide_z), bf16)],
-        6 * rows * full * ff,
-        2 * (2 * rows * full + 3 * full * ff),
-        (where, dispatched, gate4, up4, down),
-    )
-
-    outs = [(outs[2 * d], outs[2 * d + 1]) for d in range(NX)]
-    far = shift_x(outs[2][0], 1), shift_x(outs[2][1], -1)
-
-    back, gate_act, up_act = call(
+        NZ // PAIR,
+        [tok_spec, weight_spec(0), weight_spec(0)],
+        [whole(rows, ff)] * 3,
+        [struct((rows, ff), f32)] * 2 + [struct((rows, ff), bf16)],
+        [pltpu.VMEM((rows, 2 * ff), f32), weight_scratch],
+        4 * rows * full * ff,
+        2 * (rows * full + 2 * full * ff),
+        (where, dispatched, gate4, up4),
+    )
+
+    back, grad_act = call(
         backward_kernel,
-        1 + NZ,
+        1 + NZ // PAIR,
         [whole(rows, wide_z // 2)] * 2
         + [pl.BlockSpec((ff, wide_z), lambda i, s: (0, (s[0] + 2) % NX))]
         + [whole(rows, ff)]
         + [weight_spec(1)] * 2
         + [whole(rows, ff)] * 3,
-        [pl.BlockSpec((1, rows + 8, wide_x), lambda i, s: (clip(i, 1, NZ), 0, 0))]
-        + [whole(rows, ff)] * 2,
-        [struct((NZ, rows + 8, wide_x), bf16)] + [struct((rows, ff), bf16)] * 2,
-        [pltpu.VMEM((8, wide_x), bf16)],
+        [
+            pl.BlockSpec(
+                (PAIR, rows + 8, wide_x), lambda i, s: (clip(i, 1, NZ // PAIR), 0, 0)
+            ),
+            whole(rows, 2 * ff),
+        ],
+        [struct((NZ, rows + 8, wide_x), bf16), struct((rows, 2 * ff), bf16)],
+        [pltpu.VMEM((8, wide_x), bf16), weight_scratch],
         0,
         0,
         (where, *ups[4:6], down, early, gate4, up4, coef, silu_gate, hidden),
     )
 
-    back, far = lax.optimization_barrier((back, far))
+    hidden, grad_act = lax.optimization_barrier((hidden, grad_act))
+    outs = call(
+        output_kernel,
+        NX,
+        [whole(rows, ff), pl.BlockSpec((ff, wide_z), lambda i, s: (0, (s[0] + i) % NX))],
+        [whole(rows, wide_z // 2)] * (2 * NX),
+        [struct((rows, wide_z // 2), bf16)] * (2 * NX),
+        [pltpu.VMEM((rows, wide_z), bf16)],
+        0,
+        0,
+        (where, hidden, down),
+    )
+    outs = [(outs[2 * d], outs[2 * d + 1]) for d in range(NX)]
+    far = shift_x(outs[2][0], 1), shift_x(outs[2][1], -1)
     sent_x = ring_scatter_x(outs, far)
 
     back_z = lax.psum_scatter(
@@ -392,15 +417,16 @@
     )
     grad_gate, grad_up, grad_down = call(
         weight_kernel,
-        NZ + NX,
-        [tok_spec] + [whole(rows, ff)] * 3 + [whole(rows, wide_z // 2)] * (2 * NX),
+        NZ // PAIR + NX,
+        [tok_spec, whole(rows, 2 * ff), whole(rows, ff)]
+        + [whole(rows, wide_z // 2)] * (2 * NX),
         [weight_spec(0)] * 2
-        + [pl.BlockSpec((ff, wide_z), lambda i, s: (0, (s[0] + NX - clip(i, NZ, NX)) % NX))],
+        + [pl.BlockSpec((ff, wide_z), lambda i, s: (0, (s[0] + NX - clip(i, NZ // PAIR, NX)) % NX))],
         [struct((NX, NZ, feat, ff), bf16)] * 2 + [struct((ff, full), bf16)],
         [pltpu.VMEM((rows, wide_z), bf16)],
         0,
         0,
-        (where, dispatched, gate_act, up_act, hidden, *ups),
+        (where, dispatched, grad_act, hidden, *ups),
     )
 
     sent_x, grads = lax.optimization_barrier((sent_x, (grad_gate, grad_up, grad_down)))
@@ -415,14 +441,14 @@
     )
     returned = exchange(summed)
     moe_out = jnp.dot(weighted.T, returned.astype(f32), precision=highest)
-    moe_out, back_z = lax.optimization_barrier((moe_out, back_z))
 
     mix = back_z[rows : rows + 4].reshape(2, 2 * wide_x)[:, :rows].reshape(2, experts, capacity)
     mix = jnp.pad(mix.transpose(1, 0, 2), ((0, 0), (0, 6), (0, wide_x - capacity)))
     back = exchange(
         jnp.concatenate([back_z[:rows].reshape(experts, capacity, wide_x), mix], axis=1)
     ).reshape(experts, capacity + 8, wide_x)
-    mixed = (tokens.astype(f32) + spread_z(moe_out, my_z)).astype(bf16)
+    moe_parts, back = lax.optimization_barrier((spread_z_far(moe_out, my_z), back))
+    mixed = (tokens.astype(f32) + spread_z_near(*moe_parts)).astype(bf16)
     grad_moe = dot_tn(select_low, back[:, :capacity].reshape(rows, wide_x))
     mix = back[:, capacity : capacity + 2, :capacity].transpose(1, 0, 2).reshape(2, rows)
     mix = jnp.sum(jnp.dot(mix, picks, preferred_element_type=f32), axis=0).reshape(-1, feat)

time: 260 us -> 265 us (1.019)
  waiting for transfers between devices: 88.8 us -> 94.1 us
  Pallas kernels: 47.6 us -> 42.5 us
    ppermute x18, waiting for transfers between devices: 44.6 us -> 52.6 us  [shift_x(): return lax.ppermute(value, 'section', pairs)]
    reduce_scatter x1, waiting for transfers between devices: 5.81 us -> 0.02 us  [per_device(): lax.psum_scatter(back.reshape(NZ * (rows + 8), wide_x), 'section', axis_i...]
    pallas_call x4 -> x5, Pallas kernels: 47.6 us -> 42.5 us  [call(): pl.pallas_call(kernel, grid_spec=pltpu.PrefetchScalarGridSpec(num_scalar_...]
  transfers between devices with their start and end apart: 31 -> 31, of which waited for: 19 -> 16; matrix products, arithmetic and copies ran while one was open for 6% -> 7% of each run, Pallas kernels for 18% -> 12%
where the time goes in v3:
time: 265 us; the launch traced here: 264 us
  waiting for transfers between devices  94.1 us (36%)
  starting transfers between devices  63.6 us (24%)
  Pallas kernels  42.5 us (16%)
  blocking collectives  22.2 us (8%)
  between operations  14.6 us (6%)
  other arithmetic  14.1 us (5%)
  local copies, waits for them, and re-layouts  7.34 us (3%)
  matrix products  5.69 us (2%)
    ppermute x18, waiting for transfers between devices, shift_x(): return lax.ppermute(value, 'section', pairs)  52.6 us
    pallas_call x5, Pallas kernels, call(): pl.pallas_call(kernel, grid_spec=pltpu.PrefetchScalarGridSpec(num_scalar_...  42.5 us
    ppermute x18, starting transfers between devices, shift_x(): return lax.ppermute(value, 'section', pairs)  28.3 us
    all_to_all x1, blocking collectives, exchange(): lax.all_to_all(value.reshape(experts, -1, value.shape[-1]), 'expert', spl...  22.2 us
    ppermute x8, starting transfers between devices, shift_z(): return lax.ppermute(value, 'section', pairs)  19.9 us
    ppermute x8, waiting for transfers between devices, shift_z(): return lax.ppermute(value, 'section', pairs)  19.2 us
    all_to_all x3, waiting for transfers between devices, exchange(): lax.all_to_all(value.reshape(experts, -1, value.shape[-1]), 'expert', spl...  17.3 us
    all_to_all x3, starting transfers between devices, exchange(): lax.all_to_all(value.reshape(experts, -1, value.shape[-1]), 'expert', spl...  15.3 us
  transfers between devices with their start and end apart: 31, of which 16 were waited for; matrix products, arithmetic and copies ran while one was open for 7% of the time, Pallas kernels for 12%

profile of v3, /device:TPU:8, one launch (start us, length us, event | category | flops | bytes accessed | tf_op | source)
XLA Modules:
  0.0 264.1 jit_solution(10420143447005087670)
XLA Ops:
  7.2 2.0 collective-permute-start
  9.2 4.0 %collective-permute-start.1 = (bf16[256,128]{1,0:T(8,128)(2,1)}, bf16[256,128]{1,0:T(8,128)(2,1)S(1)}, u32[]{:S(2)}, u32[]{:S(2)}) collective-permute-start(bf16[256,128]{1,0:T(8,128)(2,1)} %param.13), channel_id=1, source_target_pairs={{0,56},{8,0},{16,8},{24,16},{32,24},{40,32},{48,40},{56,48},{64,12... | collective-permute-start | bytes 196616 | tf_op jit(solution)/shard_map/ppermute | solution.py:19
  13.2 0.8 copy.43
  14.7 1.3 fusion.32
  16.0 1.9 select_reduce_fusion.1
  17.9 0.9 convolution_convert_fusion
  18.8 2.0 collective-permute-start.2
  20.8 4.9 %all-to-all-start = ((bf16[8,80,128]{2,1,0:T(8,128)(2,1)}), bf16[8,80,128]{2,1,0:T(8,128)(2,1)S(1)}, u32[]{:S(2)}, u32[]{:S(2)}) async-start(bf16[8,80,128]{2,1,0:T(8,128)(2,1)} %bitcast.7), calls=%async_computation | async-start | bytes 327680 | tf_op jit(solution)/shard_map/all_to_all | solution.py:311
  25.7 3.2 %collective-permute-start.3 = (bf16[2,256,128]{2,1,0:T(8,128)(2,1)S(1)}, bf16[2,256,128]{2,1,0:T(8,128)(2,1)S(1)}, u32[]{:S(2)}, u32[]{:S(2)}) collective-permute-start(bf16[2,256,128]{2,1,0:T(8,128)(2,1)S(1)} %slice.45), channel_id=1, source_target_pairs={{0,40},{8,48},{16,56},{24,0},{32,8},{40,16},{48,24},{56,32},{64,10... | collective-permute-start | bytes 393224 | tf_op jit(solution)/shard_map/ppermute | solution.py:19
  28.9 4.4 %collective-permute-done.3 = bf16[2,256,128]{2,1,0:T(8,128)(2,1)S(1)} collective-permute-done((bf16[2,256,128]{2,1,0:T(8,128)(2,1)S(1)}, bf16[2,256,128]{2,1,0:T(8,128)(2,1)S(1)}, u32[]{:S(2)}, u32[]{:S(2)}) %collective-permute-start.3) | collective-permute-done | bytes 131104 | tf_op jit(solution)/shard_map/ppermute | solution.py:19
  33.4 0.7 collective-permute-done.2
  34.1 1.5 collective-permute-start.4
  35.6 2.7 %collective-permute-start.5 = (bf16[640,128]{1,0:T(8,128)(2,1)S(1)}, bf16[640,128]{1,0:T(8,128)(2,1)S(1)}, u32[]{:S(2)}, u32[]{:S(2)}) collective-permute-start(bf16[640,128]{1,0:T(8,128)(2,1)S(1)} %bitcast.159), channel_id=1, source_target_pairs={{0,128},{8,136},{16,144},{24,152},{32,160},{40,168},{48,176},{56,1... | collective-permute-start | bytes 491528 | tf_op jit(solution)/shard_map/ppermute | solution.py:24
  38.3 1.4 collective-permute-start.6
  39.7 1.7 collective-permute-done.4
  41.4 4.5 %collective-permute-done.5 = bf16[640,128]{1,0:T(8,128)(2,1)S(1)} collective-permute-done((bf16[640,128]{1,0:T(8,128)(2,1)S(1)}, bf16[640,128]{1,0:T(8,128)(2,1)S(1)}, u32[]{:S(2)}, u32[]{:S(2)}) %collective-permute-start.5) | collective-permute-done | bytes 163872 | tf_op jit(solution)/shard_map/ppermute | solution.py:24
  46.1 0.9 pad_maximum_fusion.2
  48.1 22.2 %all_to_all.20 = bf16[8,80,1024]{2,1,0:T(8,128)(2,1)S(1)} all-to-all(bf16[8,80,1024]{2,1,0:T(8,128)(2,1)S(1)} %bitcast.150), channel_id=1, replica_groups=mesh['section'=32,'expert'=8] {'expert'}, dimensions={0} | all-to-all | bytes 2621440 | tf_op jit(solution)/shard_map/all_to_all | solution.py:311
  70.4 1.4 collective-permute-start.7
  71.8 1.9 collective-permute-start.10
  73.8 3.1 %collective-permute-start.9 = (bf16[640,512]{1,0:T(8,128)(2,1)S(1)}, bf16[640,512]{1,0:T(8,128)(2,1)S(1)}, u32[]{:S(2)}, u32[]{:S(2)}) collective-permute-start(bf16[640,512]{1,0:T(8,128)(2,1)S(1)} %get-tuple-element.90.refs_0_.refs_3_), channel_id=1, source_target_pairs={{0,192},{8,200},{16,208},{24,216},{32,224},{40,232},{48,240},{56,2... | collective-permute-start | bytes 1966088 | tf_op jit(solution)/shard_map/ppermute | solution.py:24
  76.9 12.5 %collective-permute-done.7.refs_2_.refs_5_ = bf16[640,512]{1,0:T(8,128)(2,1)} collective-permute-done((bf16[640,512]{1,0:T(8,128)(2,1)S(1)}, bf16[640,512]{1,0:T(8,128)(2,1)}, u32[]{:S(2)}, u32[]{:S(2)}) %collective-permute-start.7) | collective-permute-done | bytes 655392 | tf_op jit(solution)/shard_map/ppermute | solution.py:24
  89.6 3.1 %collective-permute-start.12 = (bf16[640,512]{1,0:T(8,128)(2,1)}, bf16[640,512]{1,0:T(8,128)(2,1)}, u32[]{:S(2)}, u32[]{:S(2)}) collective-permute-start(bf16[640,512]{1,0:T(8,128)(2,1)} %collective-permute-done.10.refs_5_.refs_10_), channel_id=1, source_target_pairs={{0,192},{8,200},{16,208},{24,216},{32,224},{40,232},{48,240},{56,2... | collective-permute-start | bytes 1966088 | tf_op jit(solution)/shard_map/ppermute | solution.py:24
  92.7 10.7 %collective-permute-done.8.refs_3_.refs_6_ = bf16[640,512]{1,0:T(8,128)(2,1)S(1)} collective-permute-done((bf16[640,512]{1,0:T(8,128)(2,1)S(1)}, bf16[640,512]{1,0:T(8,128)(2,1)S(1)}, u32[]{:S(2)}, u32[]{:S(2)}) %collective-permute-start.8) | collective-permute-done | bytes 655392 | tf_op jit(solution)/shard_map/ppermute | solution.py:24
  103.5 0.7 copy-done.2
  104.2 0.8 copy-done.3
  105.0 5.5 %shard_map.118.refs_3_ = f32[640,256]{1,0:T(8,128)} custom-call(s32[1]{0:T(128)} %bitcast.3.x_ref, bf16[640,512]{1,0:T(8,128)(2,1)} %copy-done.1, bf16[640,512]{1,0:T(8,128)(2,1)} %copy-done, bf16[640,512]{1,0:T(8,128)(2,1)} %collective-permute-done.7.refs_2_.refs_5_, bf16[640,512]{1,0:T(8,128)(2,1)} %copy-done.2, bf16[640,512]{1,0:T(8,128)(2,1)} %copy-done.3, ...), custom_call_target="tpu_custom_call" | custom-call | tf_op jit(solution)/shard_map/pallas_call | solution.py:256
  110.6 4.8 %all-gather.2.cloned.1.call-done.tok_ref.refs_0_ = bf16[640,4096]{1,0:T(8,128)(2,1)} async-done(((bf16[640,512]{1,0:T(8,128)(2,1)}), bf16[640,4096]{1,0:T(8,128)(2,1)}) %all-gather.2.cloned.1.call-update) | async-done | bytes 5242896 | tf_op jit(solution)/shard_map/all_gather | solution.py:324
  115.4 7.5 %shard_map.119 = (f32[640,256]{1,0:T(8,128)}, f32[640,256]{1,0:T(8,128)}, bf16[640,256]{1,0:T(8,128)(2,1)}) custom-call(s32[1]{0:T(128)} %bitcast.3.x_ref, bf16[640,4096]{1,0:T(8,128)(2,1)} %all-gather.2.cloned.1.call-done.tok_ref.refs_0_, bf16[4,8,128,256]{3,2,1,0:T(8,128)(2,1)} %bitcast.154, bf16[4,8,128,256]{3,2,1,0:T(8,128)(2,1)} %bitcast.156), custom_call_target="tpu_custom_call" | custom-call | flops 2684354560 | bytes 9437184 | tf_op jit(solution)/shard_map/pallas_call | solution.py:256
  122.9 10.3 %shard_map.120 = (bf16[8,648,512]{2,1,0:T(8,128)(2,1)}, bf16[640,512]{1,0:T(8,128)(2,1)}) custom-call(s32[1]{0:T(128)} %bitcast.3.x_ref, bf16[640,512]{1,0:T(8,128)(2,1)} %collective-permute-done.11.refs_0_.refs_7_, bf16[640,512]{1,0:T(8,128)(2,1)} %collective-permute-done.12.refs_1_.refs_8_, bf16[256,4096]{1,0:T(8,128)(2,1)} %bitcast.144, ...), custom_call_target="tpu_custom_call" | custom-call | tf_op jit(solution)/shard_map/pallas_call | solution.py:256
  133.2 6.5 %shard_map.121 = (bf16[640,512]{1,0:T(8,128)(2,1)}, bf16[640,512]{1,0:T(8,128)(2,1)}, bf16[640,512]{1,0:T(8,128)(2,1)}, bf16[640,512]{1,0:T(8,128)(2,1)}, bf16[6...) custom-call(s32[1]{0:T(128)} %bitcast.3.x_ref, ...), custom_call_target="tpu_custom_call" | custom-call | tf_op jit(solution)/shard_map/pallas_call | solution.py:256
  139.7 2.7 %collective-permute-start.17 = (bf16[640,512]{1,0:T(8,128)(2,1)}, bf16[640,512]{1,0:T(8,128)(2,1)S(1)}, u32[]{:S(2)}, u32[]{:S(2)}) collective-permute-start(bf16[640,512]{1,0:T(8,128)(2,1)} %get-tuple-element.64), channel_id=1, source_target_pairs={{0,192},{8,200},{16,208},{24,216},{32,224},{40,232},{48,240},{56,2... | collective-permute-start | bytes 1966088 | tf_op jit(solution)/shard_map/ppermute | solution.py:24
  142.4 0.8 collective-permute-start.15
  143.2 2.5 collective-permute-start.16
  145.7 12.2 %collective-permute-done.17 = bf16[640,512]{1,0:T(8,128)(2,1)S(1)} collective-permute-done((bf16[640,512]{1,0:T(8,128)(2,1)}, bf16[640,512]{1,0:T(8,128)(2,1)S(1)}, u32[]{:S(2)}, u32[]{:S(2)}) %collective-permute-start.17) | collective-permute-done | bytes 655392 | tf_op jit(solution)/shard_map/ppermute | solution.py:24
  157.9 2.1 add_convert_fusion.2
  160.0 3.6 %collective-permute-start.18 = (bf16[640,512]{1,0:T(8,128)(2,1)}, bf16[640,512]{1,0:T(8,128)(2,1)}, u32[]{:S(2)}, u32[]{:S(2)}) collective-permute-start(bf16[640,512]{1,0:T(8,128)(2,1)} %add_convert_fusion.2), channel_id=1, source_target_pairs={{0,192},{8,200},{16,208},{24,216},{32,224},{40,232},{48,240},{56,2... | collective-permute-start | bytes 1966088 | tf_op jit(solution)/shard_map/ppermute | solution.py:24
  163.6 1.0 add_convert_fusion.3
  164.6 12.7 %shard_map.122 = (bf16[4,8,128,256]{3,2,1,0:T(8,128)(2,1)}, bf16[4,8,128,256]{3,2,1,0:T(8,128)(2,1)}, bf16[256,4096]{1,0:T(8,128)(2,1)}) custom-call(s32[1]{0:T(128)} %bitcast.3.x_ref, bf16[640,4096]{1,0:T(8,128)(2,1)} %all-gather.2.cloned.1.call-done.tok_ref.refs_0_, bf16[640,512]{1,0:T(8,128)(2,1)} %get-tuple-element.65.refs_1_, ...), custom_call_target="tpu_custom_call" | custom-call | tf_op jit(solution)/shard_map/pallas_call | solution.py:256
  177.3 7.5 %collective-permute-done.18 = bf16[640,512]{1,0:T(8,128)(2,1)} collective-permute-done((bf16[640,512]{1,0:T(8,128)(2,1)}, bf16[640,512]{1,0:T(8,128)(2,1)}, u32[]{:S(2)}, u32[]{:S(2)}) %collective-permute-start.18) | collective-permute-done | bytes 655392 | tf_op jit(solution)/shard_map/ppermute | solution.py:24
  184.8 3.4 %collective-permute-done.14 = bf16[640,512]{1,0:T(8,128)(2,1)} collective-permute-done((bf16[640,512]{1,0:T(8,128)(2,1)}, bf16[640,512]{1,0:T(8,128)(2,1)}, u32[]{:S(2)}, u32[]{:S(2)}) %collective-permute-start.14) | collective-permute-done | bytes 655392 | tf_op jit(solution)/shard_map/ppermute | solution.py:24
  188.2 2.5 add_convert_fusion
  190.6 1.3 pad_maximum_fusion
  191.9 4.8 %all-to-all-start.2 = ((bf16[8,80,1024]{2,1,0:T(8,128)(2,1)}), bf16[8,80,1024]{2,1,0:T(8,128)(2,1)S(1)}, u32[]{:S(2)}, u32[]{:S(2)}) async-start(bf16[8,80,1024]{2,1,0:T(8,128)(2,1)} %bitcast.30), calls=%async_computation.2 | async-start | bytes 2621440 | tf_op jit(solution)/shard_map/all_to_all | solution.py:311
  196.8 17.3 %all-to-all-done.2 = bf16[8,80,1024]{2,1,0:T(8,128)(2,1)S(1)} async-done(((bf16[8,80,1024]{2,1,0:T(8,128)(2,1)}), bf16[8,80,1024]{2,1,0:T(8,128)(2,1)S(1)}, u32[]{:S(2)}, u32[]{:S(2)}) %all-to-all-start.2) | async-done | bytes 1310752 | tf_op jit(solution)/shard_map/all_to_all | solution.py:311
  214.1 0.7 copy.45
  214.8 0.8 slice.63
  215.9 0.9 fusion.2
  216.9 5.6 %all-to-all-start.3 = ((bf16[8,88,512]{2,1,0:T(8,128)(2,1)}), bf16[8,88,512]{2,1,0:T(8,128)(2,1)}, u32[]{:S(2)}, u32[]{:S(2)}) async-start(bf16[8,88,512]{2,1,0:T(8,128)(2,1)} %fusion.2), calls=%async_computation.4 | async-start | bytes 1441792 | tf_op jit(solution)/shard_map/all_to_all | solution.py:311
  222.4 3.4 %fusion.3 = f32[256,8,128]{2,0,1:T(8,128)S(1)} fusion(bf16[8,128,640]{2,1,0:T(8,128)(2,1)S(1)} %bitcast.148, f32[640,256]{1,0:T(8,128)} %get-tuple-element.84), kind=kOutput, calls=%fused_computation.22 | convolution fusion | flops 2013265920 | bytes 3014656 | tf_op jit(solution)/shard_map/dot_general | solution.py:443
  225.9 3.1 %collective-permute-start.19 = (bf16[3,256,128]{2,1,0:T(8,128)(2,1)S(1)}, bf16[3,256,128]{2,1,0:T(8,128)(2,1)S(1)}, u32[]{:S(2)}, u32[]{:S(2)}) collective-permute-start(bf16[3,256,128]{2,1,0:T(8,128)(2,1)S(1)} %pad_maximum_fusion.4), channel_id=1, source_target_pairs={{0,24},{8,32},{16,40},{24,48},{32,56},{40,0},{48,8},{56,16},{64,88... | collective-permute-start | bytes 589832 | tf_op jit(solution)/shard_map/ppermute | solution.py:19
  229.0 2.1 collective-permute-start.20
  231.2 9.1 %collective-permute-done.20 = bf16[2,256,128]{2,1,0:T(8,128)(2,1)S(1)} collective-permute-done((bf16[2,256,128]{2,1,0:T(8,128)(2,1)S(1)}, bf16[2,256,128]{2,1,0:T(8,128)(2,1)S(1)}, u32[]{:S(2)}, u32[]{:S(2)}) %collective-permute-start.20) | collective-permute-done | bytes 131104 | tf_op jit(solution)/shard_map/ppermute | solution.py:19
  240.3 0.8 collective-permute-done.19
  241.0 1.1 slice.56
  242.2 0.7 slice_bitcast_fusion.5
  244.1 1.8 collective-permute-start.24
  245.9 1.4 collective-permute-start.25
  247.5 3.5 %collective-permute-start.21 = (bf16[256,128]{1,0:T(8,128)(2,1)S(1)}, bf16[256,128]{1,0:T(8,128)(2,1)S(1)}, u32[]{:S(2)}, u32[]{:S(2)}) collective-permute-start(bf16[256,128]{1,0:T(8,128)(2,1)S(1)} %get-tuple-element.106), channel_id=1, source_target_pairs={{0,8},{8,16},{16,24},{24,32},{32,40},{40,48},{48,56},{56,0},{64,72... | collective-permute-start | bytes 196616 | tf_op jit(solution)/shard_map/ppermute | solution.py:19
  251.0 2.0 collective-permute-done.21
  253.0 2.3 collective-permute-done.22
  255.3 0.7 fusion.20
  256.0 0.6 fusion.10
  256.7 0.6 bitcast_divide_fusion
  (98 shorter events, 4.2 us)
Async XLA Ops:
  7.2 11.6 %copy-start.8 = (bf16[256,128]{1,0:T(8,128)(2,1)S(1)}, bf16[256,128]{1,0:T(8,128)(2,1)}, u32[]{:S(2)}) copy-start(bf16[256,128]{1,0:T(8,128)(2,1)} %param.13) | copy-start | bytes 196612
  7.2 10.7 %copy-start.6 = (bf16[256,128]{1,0:T(8,128)(2,1)S(1)}, bf16[256,128]{1,0:T(8,128)(2,1)}, u32[]{:S(2)}) copy-start(bf16[256,128]{1,0:T(8,128)(2,1)} %param.7) | copy-start | bytes 196612
  7.2 11.6 %collective-permute-start = (bf16[256,128]{1,0:T(8,128)(2,1)}, bf16[256,128]{1,0:T(8,128)(2,1)S(1)}, u32[]{:S(2)}, u32[]{:S(2)}) collective-permute-start(bf16[256,128]{1,0:T(8,128)(2,1)} %param.13), channel_id=1, source_target_pairs={{0,8},{8,16},{16,24},{24,32},{32,40},{40,48},{48,56},{56,0},{64,72... | collective-permute-start | bytes 196616 | tf_op jit(solution)/shard_map/ppermute | solution.py:19
  9.2 9.6 %collective-permute-start.1 = (bf16[256,128]{1,0:T(8,128)(2,1)}, bf16[256,128]{1,0:T(8,128)(2,1)S(1)}, u32[]{:S(2)}, u32[]{:S(2)}) collective-permute-start(bf16[256,128]{1,0:T(8,128)(2,1)} %param.13), channel_id=1, source_target_pairs={{0,56},{8,0},{16,8},{24,16},{32,24},{40,32},{48,40},{56,48},{64,12... | collective-permute-start | bytes 196616 | tf_op jit(solution)/shard_map/ppermute | solution.py:19
  18.8 15.3 %collective-permute-start.2 = (bf16[3,256,128]{2,1,0:T(8,128)(2,1)S(1)}, bf16[3,256,128]{2,1,0:T(8,128)(2,1)S(1)}, u32[]{:S(2)}, u32[]{:S(2)}) collective-permute-start(bf16[3,256,128]{2,1,0:T(8,128)(2,1)S(1)} %pad_maximum_fusion.3), channel_id=1, source_target_pairs={{0,24},{8,32},{16,40},{24,48},{32,56},{40,0},{48,8},{56,16},{64,88... | collective-permute-start | bytes 589832 | tf_op jit(solution)/shard_map/ppermute | solution.py:19
  20.8 12.6 %all-to-all-start = ((bf16[8,80,128]{2,1,0:T(8,128)(2,1)}), bf16[8,80,128]{2,1,0:T(8,128)(2,1)S(1)}, u32[]{:S(2)}, u32[]{:S(2)}) async-start(bf16[8,80,128]{2,1,0:T(8,128)(2,1)} %bitcast.7), calls=%async_computation | async-start | bytes 327680 | tf_op jit(solution)/shard_map/all_to_all | solution.py:311
  25.7 89.7 %all-gather.2.cloned.1.call-start = ((), (), s32[]{:S(2)}) async-start(), calls=%async_computation.5 | async-start | bytes 5898240 | tf_op jit(solution)/shard_map/all_gather | solution.py:324
  25.7 7.6 %collective-permute-start.3 = (bf16[2,256,128]{2,1,0:T(8,128)(2,1)S(1)}, bf16[2,256,128]{2,1,0:T(8,128)(2,1)S(1)}, u32[]{:S(2)}, u32[]{:S(2)}) collective-permute-start(bf16[2,256,128]{2,1,0:T(8,128)(2,1)S(1)} %slice.45), channel_id=1, source_target_pairs={{0,40},{8,48},{16,56},{24,0},{32,8},{40,16},{48,24},{56,32},{64,10... | collective-permute-start | bytes 393224 | tf_op jit(solution)/shard_map/ppermute | solution.py:19
  34.1 7.3 %collective-permute-start.4 = (bf16[640,128]{1,0:T(8,128)(2,1)S(1)}, bf16[640,128]{1,0:T(8,128)(2,1)S(1)}, u32[]{:S(2)}, u32[]{:S(2)}) collective-permute-start(bf16[640,128]{1,0:T(8,128)(2,1)S(1)} %bitcast.158), channel_id=1, source_target_pairs={{0,64},{8,72},{16,80},{24,88},{32,96},{40,104},{48,112},{56,120},{... | collective-permute-start | bytes 491528 | tf_op jit(solution)/shard_map/ppermute | solution.py:24
  35.6 10.3 %collective-permute-start.5 = (bf16[640,128]{1,0:T(8,128)(2,1)S(1)}, bf16[640,128]{1,0:T(8,128)(2,1)S(1)}, u32[]{:S(2)}, u32[]{:S(2)}) collective-permute-start(bf16[640,128]{1,0:T(8,128)(2,1)S(1)} %bitcast.159), channel_id=1, source_target_pairs={{0,128},{8,136},{16,144},{24,152},{32,160},{40,168},{48,176},{56,1... | collective-permute-start | bytes 491528 | tf_op jit(solution)/shard_map/ppermute | solution.py:24
  38.3 7.6 %collective-permute-start.6 = (bf16[640,128]{1,0:T(8,128)(2,1)S(1)}, bf16[640,128]{1,0:T(8,128)(2,1)S(1)}, u32[]{:S(2)}, u32[]{:S(2)}) collective-permute-start(bf16[640,128]{1,0:T(8,128)(2,1)S(1)} %bitcast.160), channel_id=1, source_target_pairs={{0,192},{8,200},{16,208},{24,216},{32,224},{40,232},{48,240},{56,2... | collective-permute-start | bytes 491528 | tf_op jit(solution)/shard_map/ppermute | solution.py:24
  47.0 167.8 %reduce-scatter.2.cloned.1.call-start = ((), (), s32[]{:S(2)}) async-start(), calls=%async_computation.6 | async-start | bytes 5971968 | tf_op jit(solution)/shard_map/reduce_scatter | solution.py:411
  70.4 33.0 %copy-start.1 = (bf16[640,512]{1,0:T(8,128)(2,1)}, bf16[640,512]{1,0:T(8,128)(2,1)S(1)}, u32[]{:S(2)}) copy-start(bf16[640,512]{1,0:T(8,128)(2,1)S(1)} %get-tuple-element.90.refs_0_.refs_3_) | copy-start | bytes 1966084
  70.4 34.7 %copy-start = (bf16[640,512]{1,0:T(8,128)(2,1)}, bf16[640,512]{1,0:T(8,128)(2,1)S(1)}, u32[]{:S(2)}) copy-start(bf16[640,512]{1,0:T(8,128)(2,1)S(1)} %get-tuple-element.89.refs_1_.refs_4_) | copy-start | bytes 1966084
  70.4 19.0 %collective-permute-start.7 = (bf16[640,512]{1,0:T(8,128)(2,1)S(1)}, bf16[640,512]{1,0:T(8,128)(2,1)}, u32[]{:S(2)}, u32[]{:S(2)}) collective-permute-start(bf16[640,512]{1,0:T(8,128)(2,1)S(1)} %get-tuple-element.90.refs_0_.refs_3_), channel_id=1, source_target_pairs={{0,64},{8,72},{16,80},{24,88},{32,96},{40,104},{48,112},{56,120},{... | collective-permute-start | bytes 1966088 | tf_op jit(solution)/shard_map/ppermute | solution.py:24
  71.8 17.8 %collective-permute-start.10 = (bf16[640,512]{1,0:T(8,128)(2,1)S(1)}, bf16[640,512]{1,0:T(8,128)(2,1)}, u32[]{:S(2)}, u32[]{:S(2)}) collective-permute-start(bf16[640,512]{1,0:T(8,128)(2,1)S(1)} %get-tuple-element.89.refs_1_.refs_4_), channel_id=1, source_target_pairs={{0,192},{8,200},{16,208},{24,216},{32,224},{40,232},{48,240},{56,2... | collective-permute-start | bytes 1966088 | tf_op jit(solution)/shard_map/ppermute | solution.py:24
  73.7 29.6 %collective-permute-start.8 = (bf16[640,512]{1,0:T(8,128)(2,1)S(1)}, bf16[640,512]{1,0:T(8,128)(2,1)S(1)}, u32[]{:S(2)}, u32[]{:S(2)}) collective-permute-start(bf16[640,512]{1,0:T(8,128)(2,1)S(1)} %get-tuple-element.89.refs_1_.refs_4_), channel_id=1, source_target_pairs={{0,64},{8,72},{16,80},{24,88},{32,96},{40,104},{48,112},{56,120},{... | collective-permute-start | bytes 1966088 | tf_op jit(solution)/shard_map/ppermute | solution.py:24
  73.8 29.7 %collective-permute-start.9 = (bf16[640,512]{1,0:T(8,128)(2,1)S(1)}, bf16[640,512]{1,0:T(8,128)(2,1)S(1)}, u32[]{:S(2)}, u32[]{:S(2)}) collective-permute-start(bf16[640,512]{1,0:T(8,128)(2,1)S(1)} %get-tuple-element.90.refs_0_.refs_3_), channel_id=1, source_target_pairs={{0,192},{8,200},{16,208},{24,216},{32,224},{40,232},{48,240},{56,2... | collective-permute-start | bytes 1966088 | tf_op jit(solution)/shard_map/ppermute | solution.py:24
  89.4 33.5 %collective-permute-start.11 = (bf16[640,512]{1,0:T(8,128)(2,1)}, bf16[640,512]{1,0:T(8,128)(2,1)}, u32[]{:S(2)}, u32[]{:S(2)}) collective-permute-start(bf16[640,512]{1,0:T(8,128)(2,1)} %collective-permute-done.7.refs_2_.refs_5_), channel_id=1, source_target_pairs={{0,64},{8,72},{16,80},{24,88},{32,96},{40,104},{48,112},{56,120},{... | collective-permute-start | bytes 1966088 | tf_op jit(solution)/shard_map/ppermute | solution.py:24
  89.6 33.4 %collective-permute-start.12 = (bf16[640,512]{1,0:T(8,128)(2,1)}, bf16[640,512]{1,0:T(8,128)(2,1)}, u32[]{:S(2)}, u32[]{:S(2)}) collective-permute-start(bf16[640,512]{1,0:T(8,128)(2,1)} %collective-permute-done.10.refs_5_.refs_10_), channel_id=1, source_target_pairs={{0,192},{8,200},{16,208},{24,216},{32,224},{40,232},{48,240},{56,2... | collective-permute-start | bytes 1966088 | tf_op jit(solution)/shard_map/ppermute | solution.py:24
  103.3 0.8 copy-start.2
  104.2 0.8 copy-start.3
  139.7 23.9 %copy-start.5 = (bf16[640,512]{1,0:T(8,128)(2,1)S(1)}, bf16[640,512]{1,0:T(8,128)(2,1)}, u32[]{:S(2)}) copy-start(bf16[640,512]{1,0:T(8,128)(2,1)} %get-tuple-element.59) | copy-start | bytes 1966084
  139.7 18.2 %collective-permute-start.17 = (bf16[640,512]{1,0:T(8,128)(2,1)}, bf16[640,512]{1,0:T(8,128)(2,1)S(1)}, u32[]{:S(2)}, u32[]{:S(2)}) collective-permute-start(bf16[640,512]{1,0:T(8,128)(2,1)} %get-tuple-element.64), channel_id=1, source_target_pairs={{0,192},{8,200},{16,208},{24,216},{32,224},{40,232},{48,240},{56,2... | collective-permute-start | bytes 1966088 | tf_op jit(solution)/shard_map/ppermute | solution.py:24
  142.4 21.2 %collective-permute-start.13 = (bf16[640,512]{1,0:T(8,128)(2,1)}, bf16[640,512]{1,0:T(8,128)(2,1)S(1)}, u32[]{:S(2)}, u32[]{:S(2)}) collective-permute-start(bf16[640,512]{1,0:T(8,128)(2,1)} %get-tuple-element.60), channel_id=1, source_target_pairs={{0,64},{8,72},{16,80},{24,88},{32,96},{40,104},{48,112},{56,120},{... | collective-permute-start | bytes 1966088 | tf_op jit(solution)/shard_map/ppermute | solution.py:24
  142.4 34.8 %collective-permute-start.15 = (bf16[640,512]{1,0:T(8,128)(2,1)}, bf16[640,512]{1,0:T(8,128)(2,1)}, u32[]{:S(2)}, u32[]{:S(2)}) collective-permute-start(bf16[640,512]{1,0:T(8,128)(2,1)} %get-tuple-element.61), channel_id=1, source_target_pairs={{0,64},{8,72},{16,80},{24,88},{32,96},{40,104},{48,112},{56,120},{... | collective-permute-start | bytes 1966088 | tf_op jit(solution)/shard_map/ppermute | solution.py:24
  143.2 34.0 %collective-permute-start.16 = (bf16[640,512]{1,0:T(8,128)(2,1)}, bf16[640,512]{1,0:T(8,128)(2,1)}, u32[]{:S(2)}, u32[]{:S(2)}) collective-permute-start(bf16[640,512]{1,0:T(8,128)(2,1)} %get-tuple-element.62), channel_id=1, source_target_pairs={{0,192},{8,200},{16,208},{24,216},{32,224},{40,232},{48,240},{56,2... | collective-permute-start | bytes 1966088 | tf_op jit(solution)/shard_map/ppermute | solution.py:24
  160.0 24.8 %collective-permute-start.18 = (bf16[640,512]{1,0:T(8,128)(2,1)}, bf16[640,512]{1,0:T(8,128)(2,1)}, u32[]{:S(2)}, u32[]{:S(2)}) collective-permute-start(bf16[640,512]{1,0:T(8,128)(2,1)} %add_convert_fusion.2), channel_id=1, source_target_pairs={{0,192},{8,200},{16,208},{24,216},{32,224},{40,232},{48,240},{56,2... | collective-permute-start | bytes 1966088 | tf_op jit(solution)/shard_map/ppermute | solution.py:24
  164.6 23.6 %copy-start.4 = (bf16[640,512]{1,0:T(8,128)(2,1)S(1)}, bf16[640,512]{1,0:T(8,128)(2,1)}, u32[]{:S(2)}) copy-start(bf16[640,512]{1,0:T(8,128)(2,1)} %get-tuple-element.58) | copy-start | bytes 1966084
  164.6 23.6 %collective-permute-start.14 = (bf16[640,512]{1,0:T(8,128)(2,1)}, bf16[640,512]{1,0:T(8,128)(2,1)}, u32[]{:S(2)}, u32[]{:S(2)}) collective-permute-start(bf16[640,512]{1,0:T(8,128)(2,1)} %add_convert_fusion.3), channel_id=1, source_target_pairs={{0,64},{8,72},{16,80},{24,88},{32,96},{40,104},{48,112},{56,120},{... | collective-permute-start | bytes 1966088 | tf_op jit(solution)/shard_map/ppermute | solution.py:24
  191.9 22.1 %all-to-all-start.2 = ((bf16[8,80,1024]{2,1,0:T(8,128)(2,1)}), bf16[8,80,1024]{2,1,0:T(8,128)(2,1)S(1)}, u32[]{:S(2)}, u32[]{:S(2)}) async-start(bf16[8,80,1024]{2,1,0:T(8,128)(2,1)} %bitcast.30), calls=%async_computation.2 | async-start | bytes 2621440 | tf_op jit(solution)/shard_map/all_to_all | solution.py:311
  214.8 1.1 slice-start
  216.9 24.1 %all-to-all-start.3 = ((bf16[8,88,512]{2,1,0:T(8,128)(2,1)}), bf16[8,88,512]{2,1,0:T(8,128)(2,1)}, u32[]{:S(2)}, u32[]{:S(2)}) async-start(bf16[8,88,512]{2,1,0:T(8,128)(2,1)} %fusion.2), calls=%async_computation.4 | async-start | bytes 1441792 | tf_op jit(solution)/shard_map/all_to_all | solution.py:311
  225.8 5.3 %copy-start.11 = (s32[1,2,2,128]{3,2,1,0:T(2,128)S(1)}, s32[1,2,2,128]{3,2,1,0:T(2,128)}, u32[]{:S(2)}) copy-start(s32[1,2,2,128]{3,2,1,0:T(2,128)} %get-tuple-element.108) | copy-start | bytes 6148
  225.9 15.1 %collective-permute-start.19 = (bf16[3,256,128]{2,1,0:T(8,128)(2,1)S(1)}, bf16[3,256,128]{2,1,0:T(8,128)(2,1)S(1)}, u32[]{:S(2)}, u32[]{:S(2)}) collective-permute-start(bf16[3,256,128]{2,1,0:T(8,128)(2,1)S(1)} %pad_maximum_fusion.4), channel_id=1, source_target_pairs={{0,24},{8,32},{16,40},{24,48},{32,56},{40,0},{48,8},{56,16},{64,88... | collective-permute-start | bytes 589832 | tf_op jit(solution)/shard_map/ppermute | solution.py:19
  229.0 11.2 %collective-permute-start.20 = (bf16[2,256,128]{2,1,0:T(8,128)(2,1)S(1)}, bf16[2,256,128]{2,1,0:T(8,128)(2,1)S(1)}, u32[]{:S(2)}, u32[]{:S(2)}) collective-permute-start(bf16[2,256,128]{2,1,0:T(8,128)(2,1)S(1)} %pad_maximum_fusion.5), channel_id=1, source_target_pairs={{0,40},{8,48},{16,56},{24,0},{32,8},{40,16},{48,24},{56,32},{64,10... | collective-permute-start | bytes 393224 | tf_op jit(solution)/shard_map/ppermute | solution.py:19
  244.0 11.3 %copy-start.7 = (bf16[256,128]{1,0:T(8,128)(2,1)S(1)}, bf16[256,128]{1,0:T(8,128)(2,1)}, u32[]{:S(2)}) copy-start(bf16[256,128]{1,0:T(8,128)(2,1)} %param.7) | copy-start | bytes 196612
  244.0 11.9 %collective-permute-start.23 = (bf16[264,128]{1,0:T(8,128)(2,1)S(1)}, bf16[264,128]{1,0:T(8,128)(2,1)S(1)}, u32[]{:S(2)}, u32[]{:S(2)}) collective-permute-start(bf16[264,128]{1,0:T(8,128)(2,1)S(1)} %get-tuple-element.110), channel_id=1, source_target_pairs={{0,64},{8,72},{16,80},{24,88},{32,96},{40,104},{48,112},{56,120},{... | collective-permute-start | bytes 202760 | tf_op jit(solution)/shard_map/ppermute | solution.py:24
  244.1 11.8 %collective-permute-start.24 = (bf16[264,128]{1,0:T(8,128)(2,1)S(1)}, bf16[264,128]{1,0:T(8,128)(2,1)S(1)}, u32[]{:S(2)}, u32[]{:S(2)}) collective-permute-start(bf16[264,128]{1,0:T(8,128)(2,1)S(1)} %get-tuple-element.111), channel_id=1, source_target_pairs={{0,128},{8,136},{16,144},{24,152},{32,160},{40,168},{48,176},{56,1... | collective-permute-start | bytes 202760 | tf_op jit(solution)/shard_map/ppermute | solution.py:24
  245.9 10.1 %copy-start.9 = (bf16[256,128]{1,0:T(8,128)(2,1)S(1)}, bf16[256,128]{1,0:T(8,128)(2,1)}, u32[]{:S(2)}) copy-start(bf16[256,128]{1,0:T(8,128)(2,1)} %param.13) | copy-start | bytes 196612
  245.9 10.0 %collective-permute-start.25 = (bf16[264,128]{1,0:T(8,128)(2,1)S(1)}, bf16[264,128]{1,0:T(8,128)(2,1)S(1)}, u32[]{:S(2)}, u32[]{:S(2)}) collective-permute-start(bf16[264,128]{1,0:T(8,128)(2,1)S(1)} %get-tuple-element.112), channel_id=1, source_target_pairs={{0,192},{8,200},{16,208},{24,216},{32,224},{40,232},{48,240},{56,2... | collective-permute-start | bytes 202760 | tf_op jit(solution)/shard_map/ppermute | solution.py:24
  247.4 9.3 %copy-start.10 = (f32[256,2]{0,1:T(2,128)S(1)}, f32[256,2]{0,1:T(2,128)}, u32[]{:S(2)}) copy-start(f32[256,2]{0,1:T(2,128)} %param.9) | copy-start | bytes 6148
  247.5 5.6 %collective-permute-start.21 = (bf16[256,128]{1,0:T(8,128)(2,1)S(1)}, bf16[256,128]{1,0:T(8,128)(2,1)S(1)}, u32[]{:S(2)}, u32[]{:S(2)}) collective-permute-start(bf16[256,128]{1,0:T(8,128)(2,1)S(1)} %get-tuple-element.106), channel_id=1, source_target_pairs={{0,8},{8,16},{16,24},{24,32},{32,40},{40,48},{48,56},{56,0},{64,72... | collective-permute-start | bytes 196616 | tf_op jit(solution)/shard_map/ppermute | solution.py:19
  251.0 4.3 %collective-permute-start.22 = (bf16[256,128]{1,0:T(8,128)(2,1)S(1)}, bf16[256,128]{1,0:T(8,128)(2,1)S(1)}, u32[]{:S(2)}, u32[]{:S(2)}) collective-permute-start(bf16[256,128]{1,0:T(8,128)(2,1)S(1)} %get-tuple-element.107), channel_id=1, source_target_pairs={{0,56},{8,0},{16,8},{24,16},{32,24},{40,32},{48,40},{56,48},{64,12... | collective-permute-start | bytes 196616 | tf_op jit(solution)/shard_map/ppermute | solution.py:19
Sparse Core Ops, SparseCore 0:
  47.1 68.2 all-gather.1
  133.4 64.4 reduce-scatter.1

commit v4 on v3

--- a/solution.py
+++ b/solution.py
@@ -146,11 +146,11 @@
 
 
 def output_kernel(x_ref, hid_ref, down_ref, *rest):
-    outs, made = rest[: 2 * NX], rest[2 * NX]
+    outs, made = rest[:-1], rest[-1]
     step = pl.program_id(0)
     made[...] = jnp.dot(hid_ref[...], down_ref[...], preferred_element_type=f32).astype(bf16)
 
-    for d in range(NX):
+    for d in range(len(outs) // 2):
 
         @pl.when(step == d)
         def _(d=d):
@@ -371,6 +371,26 @@
         (where, dispatched, gate4, up4),
     )
 
+    def outputs(hidden, steps, place):
+        outs = call(
+            output_kernel,
+            steps,
+            [
+                whole(rows, ff),
+                pl.BlockSpec((ff, wide_z), lambda i, s: (0, (s[0] + place(i)) % NX)),
+            ],
+            [whole(rows, wide_z // 2)] * (2 * steps),
+            [struct((rows, wide_z // 2), bf16)] * (2 * steps),
+            [pltpu.VMEM((rows, wide_z), bf16)],
+            0,
+            0,
+            (where, hidden, down),
+        )
+        return [(outs[2 * d], outs[2 * d + 1]) for d in range(steps)]
+
+    (farthest,) = outputs(hidden, 1, lambda i: 2)
+    far = shift_x(farthest[0], 1), shift_x(farthest[1], -1)
+
     back, grad_act = call(
         backward_kernel,
         1 + NZ // PAIR,
@@ -393,19 +413,9 @@
     )
 
     hidden, grad_act = lax.optimization_barrier((hidden, grad_act))
-    outs = call(
-        output_kernel,
-        NX,
-        [whole(rows, ff), pl.BlockSpec((ff, wide_z), lambda i, s: (0, (s[0] + i) % NX))],
-        [whole(rows, wide_z // 2)] * (2 * NX),
-        [struct((rows, wide_z // 2), bf16)] * (2 * NX),
-        [pltpu.VMEM((rows, wide_z), bf16)],
-        0,
-        0,
-        (where, hidden, down),
-    )
-    outs = [(outs[2 * d], outs[2 * d + 1]) for d in range(NX)]
-    far = shift_x(outs[2][0], 1), shift_x(outs[2][1], -1)
+    own, above, below = outputs(hidden, 3, lambda i: i + i // 2)
+    back, far, own, above, below = lax.optimization_barrier((back, far, own, above, below))
+    outs = [own, above, None, below]
     sent_x = ring_scatter_x(outs, far)
 
     back_z = lax.psum_scatter(
@@ -441,6 +451,7 @@
     )
     returned = exchange(summed)
     moe_out = jnp.dot(weighted.T, returned.astype(f32), precision=highest)
+    moe_out, back_z = lax.optimization_barrier((moe_out, back_z))
 
     mix = back_z[rows : rows + 4].reshape(2, 2 * wide_x)[:, :rows].reshape(2, experts, capacity)
     mix = jnp.pad(mix.transpose(1, 0, 2), ((0, 0), (0, 6), (0, wide_x - capacity)))

time: 265 us -> 256 us (0.966)
  waiting for transfers between devices: 94.1 us -> 85.7 us
    ppermute x18, waiting for transfers between devices: 52.6 us -> 44.3 us  [shift_x(): return lax.ppermute(value, 'section', pairs)]
    pallas_call x5 -> x6, Pallas kernels: 42.5 us -> 43.8 us  [call(): pl.pallas_call(kernel, grid_spec=pltpu.PrefetchScalarGridSpec(num_scalar_...]
  transfers between devices with their start and end apart: 31 -> 31, of which waited for: 16 -> 15; matrix products, arithmetic and copies ran while one was open for 7% -> 6% of each run, Pallas kernels for 12% -> 17%
where the time goes in v4:
time: 256 us; the launch traced here: 254 us
  waiting for transfers between devices  85.7 us (33%)
  starting transfers between devices  63.4 us (25%)
  Pallas kernels  43.8 us (17%)
  blocking collectives  22.2 us (9%)
  between operations  14.7 us (6%)
  other arithmetic  14.2 us (6%)
  local copies, waits for them, and re-layouts  6.73 us (3%)
  matrix products  3.74 us (1%)
    ppermute x18, waiting for transfers between devices, shift_x(): return lax.ppermute(value, 'section', pairs)  44.3 us
    pallas_call x6, Pallas kernels, call(): pl.pallas_call(kernel, grid_spec=pltpu.PrefetchScalarGridSpec(num_scalar_...  43.8 us
    ppermute x18, starting transfers between devices, shift_x(): return lax.ppermute(value, 'section', pairs)  28.8 us
    all_to_all x1, blocking collectives, exchange(): lax.all_to_all(value.reshape(experts, -1, value.shape[-1]), 'expert', spl...  22.2 us
    ppermute x8, starting transfers between devices, shift_z(): return lax.ppermute(value, 'section', pairs)  19.8 us
    ppermute x8, waiting for transfers between devices, shift_z(): return lax.ppermute(value, 'section', pairs)  19.2 us
    all_to_all x3, waiting for transfers between devices, exchange(): lax.all_to_all(value.reshape(experts, -1, value.shape[-1]), 'expert', spl...  17.3 us
    all_to_all x3, starting transfers between devices, exchange(): lax.all_to_all(value.reshape(experts, -1, value.shape[-1]), 'expert', spl...  14.8 us
  transfers between devices with their start and end apart: 31, of which 15 were waited for; matrix products, arithmetic and copies ran while one was open for 6% of the time, Pallas kernels for 17%

profile of v4, /device:TPU:8, one launch (start us, length us, event | category | flops | bytes accessed | tf_op | source)
XLA Modules:
  0.0 254.5 jit_solution(6383362565013095132)
XLA Ops:
  7.2 2.0 collective-permute-start
  9.2 4.0 %collective-permute-start.1 = (bf16[256,128]{1,0:T(8,128)(2,1)}, bf16[256,128]{1,0:T(8,128)(2,1)S(1)}, u32[]{:S(2)}, u32[]{:S(2)}) collective-permute-start(bf16[256,128]{1,0:T(8,128)(2,1)} %param.13), channel_id=1, source_target_pairs={{0,56},{8,0},{16,8},{24,16},{32,24},{40,32},{48,40},{56,48},{64,12... | collective-permute-start | bytes 196616 | tf_op jit(solution)/shard_map/ppermute | solution.py:19
  13.2 0.8 copy.58
  14.7 1.3 fusion.25
  16.0 1.9 select_reduce_fusion
  17.9 0.9 convolution_convert_fusion
  18.8 2.0 collective-permute-start.2
  20.8 4.9 %all-to-all-start = ((bf16[8,80,128]{2,1,0:T(8,128)(2,1)}), bf16[8,80,128]{2,1,0:T(8,128)(2,1)S(1)}, u32[]{:S(2)}, u32[]{:S(2)}) async-start(bf16[8,80,128]{2,1,0:T(8,128)(2,1)} %bitcast.6), calls=%async_computation | async-start | bytes 327680 | tf_op jit(solution)/shard_map/all_to_all | solution.py:311
  25.7 3.2 %collective-permute-start.3 = (bf16[2,256,128]{2,1,0:T(8,128)(2,1)S(1)}, bf16[2,256,128]{2,1,0:T(8,128)(2,1)S(1)}, u32[]{:S(2)}, u32[]{:S(2)}) collective-permute-start(bf16[2,256,128]{2,1,0:T(8,128)(2,1)S(1)} %slice.45), channel_id=1, source_target_pairs={{0,40},{8,48},{16,56},{24,0},{32,8},{40,16},{48,24},{56,32},{64,10... | collective-permute-start | bytes 393224 | tf_op jit(solution)/shard_map/ppermute | solution.py:19
  29.0 4.4 %collective-permute-done.3 = bf16[2,256,128]{2,1,0:T(8,128)(2,1)S(1)} collective-permute-done((bf16[2,256,128]{2,1,0:T(8,128)(2,1)S(1)}, bf16[2,256,128]{2,1,0:T(8,128)(2,1)S(1)}, u32[]{:S(2)}, u32[]{:S(2)}) %collective-permute-start.3) | collective-permute-done | bytes 131104 | tf_op jit(solution)/shard_map/ppermute | solution.py:19
  33.4 0.7 collective-permute-done.2
  34.1 1.5 collective-permute-start.8
  35.6 2.7 %collective-permute-start.9 = (bf16[640,128]{1,0:T(8,128)(2,1)S(1)}, bf16[640,128]{1,0:T(8,128)(2,1)S(1)}, u32[]{:S(2)}, u32[]{:S(2)}) collective-permute-start(bf16[640,128]{1,0:T(8,128)(2,1)S(1)} %bitcast.160), channel_id=1, source_target_pairs={{0,128},{8,136},{16,144},{24,152},{32,160},{40,168},{48,176},{56,1... | collective-permute-start | bytes 491528 | tf_op jit(solution)/shard_map/ppermute | solution.py:24
  38.3 1.4 collective-permute-start.10
  39.7 1.7 collective-permute-done.8
  41.4 4.5 %collective-permute-done.9 = bf16[640,128]{1,0:T(8,128)(2,1)S(1)} collective-permute-done((bf16[640,128]{1,0:T(8,128)(2,1)S(1)}, bf16[640,128]{1,0:T(8,128)(2,1)S(1)}, u32[]{:S(2)}, u32[]{:S(2)}) %collective-permute-start.9) | collective-permute-done | bytes 163872 | tf_op jit(solution)/shard_map/ppermute | solution.py:24
  46.1 0.9 pad_maximum_fusion.2
  48.1 22.2 %all_to_all.20 = bf16[8,80,1024]{2,1,0:T(8,128)(2,1)S(1)} all-to-all(bf16[8,80,1024]{2,1,0:T(8,128)(2,1)S(1)} %bitcast.149), channel_id=1, replica_groups=mesh['section'=32,'expert'=8] {'expert'}, dimensions={0} | all-to-all | bytes 2621440 | tf_op jit(solution)/shard_map/all_to_all | solution.py:311
  70.4 1.4 collective-permute-start.4
  71.8 1.9 collective-permute-start.6
  73.8 3.1 %collective-permute-start.12 = (bf16[640,512]{1,0:T(8,128)(2,1)S(1)}, bf16[640,512]{1,0:T(8,128)(2,1)S(1)}, u32[]{:S(2)}, u32[]{:S(2)}) collective-permute-start(bf16[640,512]{1,0:T(8,128)(2,1)S(1)} %get-tuple-element.112.refs_0_.refs_3_), channel_id=1, source_target_pairs={{0,192},{8,200},{16,208},{24,216},{32,224},{40,232},{48,240},{56,2... | collective-permute-start | bytes 1966088 | tf_op jit(solution)/shard_map/ppermute | solution.py:24
  76.9 12.5 %collective-permute-done.4.refs_2_.refs_5_ = bf16[640,512]{1,0:T(8,128)(2,1)} collective-permute-done((bf16[640,512]{1,0:T(8,128)(2,1)S(1)}, bf16[640,512]{1,0:T(8,128)(2,1)}, u32[]{:S(2)}, u32[]{:S(2)}) %collective-permute-start.4) | collective-permute-done | bytes 655392 | tf_op jit(solution)/shard_map/ppermute | solution.py:24
  89.6 3.1 %collective-permute-start.7 = (bf16[640,512]{1,0:T(8,128)(2,1)}, bf16[640,512]{1,0:T(8,128)(2,1)}, u32[]{:S(2)}, u32[]{:S(2)}) collective-permute-start(bf16[640,512]{1,0:T(8,128)(2,1)} %collective-permute-done.6.refs_5_.refs_10_), channel_id=1, source_target_pairs={{0,192},{8,200},{16,208},{24,216},{32,224},{40,232},{48,240},{56,2... | collective-permute-start | bytes 1966088 | tf_op jit(solution)/shard_map/ppermute | solution.py:24
  92.7 10.7 %collective-permute-done.11.refs_3_.refs_6_ = bf16[640,512]{1,0:T(8,128)(2,1)S(1)} collective-permute-done((bf16[640,512]{1,0:T(8,128)(2,1)S(1)}, bf16[640,512]{1,0:T(8,128)(2,1)S(1)}, u32[]{:S(2)}, u32[]{:S(2)}) %collective-permute-start.11) | collective-permute-done | bytes 655392 | tf_op jit(solution)/shard_map/ppermute | solution.py:24
  103.5 0.7 copy-done.2
  104.2 0.8 copy-done.3
  105.0 5.6 %shard_map.118.refs_3_ = f32[640,256]{1,0:T(8,128)} custom-call(s32[1]{0:T(128)} %bitcast.2.x_ref, bf16[640,512]{1,0:T(8,128)(2,1)} %copy-done.1, bf16[640,512]{1,0:T(8,128)(2,1)} %copy-done, bf16[640,512]{1,0:T(8,128)(2,1)} %collective-permute-done.4.refs_2_.refs_5_, bf16[640,512]{1,0:T(8,128)(2,1)} %copy-done.2, bf16[640,512]{1,0:T(8,128)(2,1)} %copy-done.3, ...), custom_call_target="tpu_custom_call" | custom-call | tf_op jit(solution)/shard_map/pallas_call | solution.py:256
  110.6 4.8 %all-gather.2.cloned.1.call-done.tok_ref.refs_0_ = bf16[640,4096]{1,0:T(8,128)(2,1)} async-done(((bf16[640,512]{1,0:T(8,128)(2,1)}), bf16[640,4096]{1,0:T(8,128)(2,1)}) %all-gather.2.cloned.1.call-update) | async-done | bytes 5242896 | tf_op jit(solution)/shard_map/all_gather | solution.py:324
  115.4 7.5 %shard_map.119 = (f32[640,256]{1,0:T(8,128)}, f32[640,256]{1,0:T(8,128)}, bf16[640,256]{1,0:T(8,128)(2,1)}) custom-call(s32[1]{0:T(128)} %bitcast.2.x_ref, bf16[640,4096]{1,0:T(8,128)(2,1)} %all-gather.2.cloned.1.call-done.tok_ref.refs_0_, bf16[4,8,128,256]{3,2,1,0:T(8,128)(2,1)} %bitcast.155, bf16[4,8,128,256]{3,2,1,0:T(8,128)(2,1)} %bitcast.157), custom_call_target="tpu_custom_call" | custom-call | flops 2684354560 | bytes 9437184 | tf_op jit(solution)/shard_map/pallas_call | solution.py:256
  122.9 2.5 shard_map.121
  125.5 1.5 collective-permute-start.13
  126.9 1.8 collective-permute-start.14
  128.7 10.3 %shard_map.120 = (bf16[8,648,512]{2,1,0:T(8,128)(2,1)}, bf16[640,512]{1,0:T(8,128)(2,1)}) custom-call(s32[1]{0:T(128)} %bitcast.2.x_ref, bf16[640,512]{1,0:T(8,128)(2,1)} %collective-permute-done.5.refs_0_.refs_7_, bf16[640,512]{1,0:T(8,128)(2,1)} %collective-permute-done.7.refs_1_.refs_8_, bf16[256,4096]{1,0:T(8,128)(2,1)} %bitcast.144, ...), custom_call_target="tpu_custom_call" | custom-call | tf_op jit(solution)/shard_map/pallas_call | solution.py:256
  139.0 5.3 %shard_map.122 = (bf16[640,512]{1,0:T(8,128)(2,1)}, bf16[640,512]{1,0:T(8,128)(2,1)}, bf16[640,512]{1,0:T(8,128)(2,1)}, bf16[640,512]{1,0:T(8,128)(2,1)}, bf16[6...) custom-call(s32[1]{0:T(128)} %bitcast.2.x_ref, bf16[640,256]{1,0:T(8,128)(2,1)} %get-tuple-element.71.refs_8_.hid_ref.refs_2_, ...), custom_call_target="tpu_custom_call" | custom-call | tf_op jit(solution)/shard_map/pallas_call | solution.py:256
  144.4 1.1 copy-done.7
  145.4 2.2 add_convert_fusion.2
  147.6 2.0 collective-permute-start.18
  149.6 1.0 add_convert_fusion.3
  151.2 2.8 %collective-permute-start.17 = (bf16[640,512]{1,0:T(8,128)(2,1)}, bf16[640,512]{1,0:T(8,128)(2,1)}, u32[]{:S(2)}, u32[]{:S(2)}) collective-permute-start(bf16[640,512]{1,0:T(8,128)(2,1)} %get-tuple-element.82), channel_id=1, source_target_pairs={{0,192},{8,200},{16,208},{24,216},{32,224},{40,232},{48,240},{56,2... | collective-permute-start | bytes 1966088 | tf_op jit(solution)/shard_map/ppermute | solution.py:24
  153.9 12.5 %shard_map.123 = (bf16[4,8,128,256]{3,2,1,0:T(8,128)(2,1)}, bf16[4,8,128,256]{3,2,1,0:T(8,128)(2,1)}, bf16[256,4096]{1,0:T(8,128)(2,1)}) custom-call(s32[1]{0:T(128)} %bitcast.2.x_ref, bf16[640,4096]{1,0:T(8,128)(2,1)} %all-gather.2.cloned.1.call-done.tok_ref.refs_0_, bf16[640,512]{1,0:T(8,128)(2,1)} %get-tuple-element.85.refs_1_, ...), custom_call_target="tpu_custom_call" | custom-call | tf_op jit(solution)/shard_map/pallas_call | solution.py:256
  166.5 3.4 %collective-permute-done.15 = bf16[640,512]{1,0:T(8,128)(2,1)} collective-permute-done((bf16[640,512]{1,0:T(8,128)(2,1)}, bf16[640,512]{1,0:T(8,128)(2,1)}, u32[]{:S(2)}, u32[]{:S(2)}) %collective-permute-start.15) | collective-permute-done | bytes 655392 | tf_op jit(solution)/shard_map/ppermute | solution.py:24
  169.8 11.4 %collective-permute-done.16 = bf16[640,512]{1,0:T(8,128)(2,1)} collective-permute-done((bf16[640,512]{1,0:T(8,128)(2,1)}, bf16[640,512]{1,0:T(8,128)(2,1)}, u32[]{:S(2)}, u32[]{:S(2)}) %collective-permute-start.16) | collective-permute-done | bytes 655392 | tf_op jit(solution)/shard_map/ppermute | solution.py:24
  181.3 2.4 add_convert_fusion
  183.7 1.3 pad_maximum_fusion
  185.0 5.0 %all-to-all-start.2 = ((bf16[8,80,1024]{2,1,0:T(8,128)(2,1)}), bf16[8,80,1024]{2,1,0:T(8,128)(2,1)S(1)}, u32[]{:S(2)}, u32[]{:S(2)}) async-start(bf16[8,80,1024]{2,1,0:T(8,128)(2,1)} %bitcast.29), calls=%async_computation.2 | async-start | bytes 2621440 | tf_op jit(solution)/shard_map/all_to_all | solution.py:311
  190.0 17.3 %all-to-all-done.2 = bf16[8,80,1024]{2,1,0:T(8,128)(2,1)S(1)} async-done(((bf16[8,80,1024]{2,1,0:T(8,128)(2,1)}), bf16[8,80,1024]{2,1,0:T(8,128)(2,1)S(1)}, u32[]{:S(2)}, u32[]{:S(2)}) %all-to-all-start.2) | async-done | bytes 1310752 | tf_op jit(solution)/shard_map/all_to_all | solution.py:311
  207.3 1.4 fusion.31
  208.8 0.7 slice-done.1
  209.8 0.9 fusion.2
  210.8 4.9 %all-to-all-start.3 = ((bf16[8,88,512]{2,1,0:T(8,128)(2,1)}), bf16[8,88,512]{2,1,0:T(8,128)(2,1)S(1)}, u32[]{:S(2)}, u32[]{:S(2)}) async-start(bf16[8,88,512]{2,1,0:T(8,128)(2,1)} %fusion.2), calls=%async_computation.4 | async-start | bytes 1441792 | tf_op jit(solution)/shard_map/all_to_all | solution.py:311
  215.9 0.7 constant_dynamic-slice_fusion.1
  216.7 3.1 %collective-permute-start.19 = (bf16[3,256,128]{2,1,0:T(8,128)(2,1)S(1)}, bf16[3,256,128]{2,1,0:T(8,128)(2,1)S(1)}, u32[]{:S(2)}, u32[]{:S(2)}) collective-permute-start(bf16[3,256,128]{2,1,0:T(8,128)(2,1)S(1)} %pad_maximum_fusion.4), channel_id=1, source_target_pairs={{0,24},{8,32},{16,40},{24,48},{32,56},{40,0},{48,8},{56,16},{64,88... | collective-permute-start | bytes 589832 | tf_op jit(solution)/shard_map/ppermute | solution.py:19
  219.9 2.1 collective-permute-start.20
  222.0 9.2 %collective-permute-done.20 = bf16[2,256,128]{2,1,0:T(8,128)(2,1)S(1)} collective-permute-done((bf16[2,256,128]{2,1,0:T(8,128)(2,1)S(1)}, bf16[2,256,128]{2,1,0:T(8,128)(2,1)S(1)}, u32[]{:S(2)}, u32[]{:S(2)}) %collective-permute-start.20) | collective-permute-done | bytes 131104 | tf_op jit(solution)/shard_map/ppermute | solution.py:19
  231.2 0.6 collective-permute-done.19
  233.0 0.7 collective-permute-start.23
  233.7 2.7 %collective-permute-start.24 = (bf16[264,128]{1,0:T(8,128)(2,1)S(1)}, bf16[264,128]{1,0:T(8,128)(2,1)S(1)}, u32[]{:S(2)}, u32[]{:S(2)}) collective-permute-start(bf16[264,128]{1,0:T(8,128)(2,1)S(1)} %get-tuple-element.133), channel_id=1, source_target_pairs={{0,128},{8,136},{16,144},{24,152},{32,160},{40,168},{48,176},{56,1... | collective-permute-start | bytes 202760 | tf_op jit(solution)/shard_map/ppermute | solution.py:24
  236.4 1.5 collective-permute-start.25
  238.0 3.4 %collective-permute-start.21 = (bf16[256,128]{1,0:T(8,128)(2,1)S(1)}, bf16[256,128]{1,0:T(8,128)(2,1)S(1)}, u32[]{:S(2)}, u32[]{:S(2)}) collective-permute-start(bf16[256,128]{1,0:T(8,128)(2,1)S(1)} %get-tuple-element.128), channel_id=1, source_target_pairs={{0,8},{8,16},{16,24},{24,32},{32,40},{40,48},{48,56},{56,0},{64,72... | collective-permute-start | bytes 196616 | tf_op jit(solution)/shard_map/ppermute | solution.py:19
  241.4 2.2 collective-permute-done.21
  243.5 2.1 collective-permute-done.22
  245.6 0.7 fusion.18
  246.4 0.7 fusion.8
  247.0 0.6 bitcast_divide_fusion
  (108 shorter events, 4.9 us)
Async XLA Ops:
  7.2 11.6 %copy-start.10 = (bf16[256,128]{1,0:T(8,128)(2,1)S(1)}, bf16[256,128]{1,0:T(8,128)(2,1)}, u32[]{:S(2)}) copy-start(bf16[256,128]{1,0:T(8,128)(2,1)} %param.13) | copy-start | bytes 196612
  7.2 10.7 %copy-start.8 = (bf16[256,128]{1,0:T(8,128)(2,1)S(1)}, bf16[256,128]{1,0:T(8,128)(2,1)}, u32[]{:S(2)}) copy-start(bf16[256,128]{1,0:T(8,128)(2,1)} %param.7) | copy-start | bytes 196612
  7.2 11.6 %collective-permute-start = (bf16[256,128]{1,0:T(8,128)(2,1)}, bf16[256,128]{1,0:T(8,128)(2,1)S(1)}, u32[]{:S(2)}, u32[]{:S(2)}) collective-permute-start(bf16[256,128]{1,0:T(8,128)(2,1)} %param.13), channel_id=1, source_target_pairs={{0,8},{8,16},{16,24},{24,32},{32,40},{40,48},{48,56},{56,0},{64,72... | collective-permute-start | bytes 196616 | tf_op jit(solution)/shard_map/ppermute | solution.py:19
  9.2 9.6 %collective-permute-start.1 = (bf16[256,128]{1,0:T(8,128)(2,1)}, bf16[256,128]{1,0:T(8,128)(2,1)S(1)}, u32[]{:S(2)}, u32[]{:S(2)}) collective-permute-start(bf16[256,128]{1,0:T(8,128)(2,1)} %param.13), channel_id=1, source_target_pairs={{0,56},{8,0},{16,8},{24,16},{32,24},{40,32},{48,40},{56,48},{64,12... | collective-permute-start | bytes 196616 | tf_op jit(solution)/shard_map/ppermute | solution.py:19
  18.8 15.2 %collective-permute-start.2 = (bf16[3,256,128]{2,1,0:T(8,128)(2,1)S(1)}, bf16[3,256,128]{2,1,0:T(8,128)(2,1)S(1)}, u32[]{:S(2)}, u32[]{:S(2)}) collective-permute-start(bf16[3,256,128]{2,1,0:T(8,128)(2,1)S(1)} %pad_maximum_fusion.3), channel_id=1, source_target_pairs={{0,24},{8,32},{16,40},{24,48},{32,56},{40,0},{48,8},{56,16},{64,88... | collective-permute-start | bytes 589832 | tf_op jit(solution)/shard_map/ppermute | solution.py:19
  20.8 12.6 %all-to-all-start = ((bf16[8,80,128]{2,1,0:T(8,128)(2,1)}), bf16[8,80,128]{2,1,0:T(8,128)(2,1)S(1)}, u32[]{:S(2)}, u32[]{:S(2)}) async-start(bf16[8,80,128]{2,1,0:T(8,128)(2,1)} %bitcast.6), calls=%async_computation | async-start | bytes 327680 | tf_op jit(solution)/shard_map/all_to_all | solution.py:311
  25.7 89.7 %all-gather.2.cloned.1.call-start = ((), (), s32[]{:S(2)}) async-start(), calls=%async_computation.5 | async-start | bytes 5898240 | tf_op jit(solution)/shard_map/all_gather | solution.py:324
  25.7 7.6 %collective-permute-start.3 = (bf16[2,256,128]{2,1,0:T(8,128)(2,1)S(1)}, bf16[2,256,128]{2,1,0:T(8,128)(2,1)S(1)}, u32[]{:S(2)}, u32[]{:S(2)}) collective-permute-start(bf16[2,256,128]{2,1,0:T(8,128)(2,1)S(1)} %slice.45), channel_id=1, source_target_pairs={{0,40},{8,48},{16,56},{24,0},{32,8},{40,16},{48,24},{56,32},{64,10... | collective-permute-start | bytes 393224 | tf_op jit(solution)/shard_map/ppermute | solution.py:19
  34.1 7.3 %collective-permute-start.8 = (bf16[640,128]{1,0:T(8,128)(2,1)S(1)}, bf16[640,128]{1,0:T(8,128)(2,1)S(1)}, u32[]{:S(2)}, u32[]{:S(2)}) collective-permute-start(bf16[640,128]{1,0:T(8,128)(2,1)S(1)} %bitcast.159), channel_id=1, source_target_pairs={{0,64},{8,72},{16,80},{24,88},{32,96},{40,104},{48,112},{56,120},{... | collective-permute-start | bytes 491528 | tf_op jit(solution)/shard_map/ppermute | solution.py:24
  35.6 10.3 %collective-permute-start.9 = (bf16[640,128]{1,0:T(8,128)(2,1)S(1)}, bf16[640,128]{1,0:T(8,128)(2,1)S(1)}, u32[]{:S(2)}, u32[]{:S(2)}) collective-permute-start(bf16[640,128]{1,0:T(8,128)(2,1)S(1)} %bitcast.160), channel_id=1, source_target_pairs={{0,128},{8,136},{16,144},{24,152},{32,160},{40,168},{48,176},{56,1... | collective-permute-start | bytes 491528 | tf_op jit(solution)/shard_map/ppermute | solution.py:24
  38.3 7.6 %collective-permute-start.10 = (bf16[640,128]{1,0:T(8,128)(2,1)S(1)}, bf16[640,128]{1,0:T(8,128)(2,1)S(1)}, u32[]{:S(2)}, u32[]{:S(2)}) collective-permute-start(bf16[640,128]{1,0:T(8,128)(2,1)S(1)} %bitcast.161), channel_id=1, source_target_pairs={{0,192},{8,200},{16,208},{24,216},{32,224},{40,232},{48,240},{56,2... | collective-permute-start | bytes 491528 | tf_op jit(solution)/shard_map/ppermute | solution.py:24
  47.0 161.8 %reduce-scatter.2.cloned.1.call-start = ((), (), s32[]{:S(2)}) async-start(), calls=%async_computation.6 | async-start | bytes 5971968 | tf_op jit(solution)/shard_map/reduce_scatter | solution.py:421
  70.4 33.0 %copy-start.1 = (bf16[640,512]{1,0:T(8,128)(2,1)}, bf16[640,512]{1,0:T(8,128)(2,1)S(1)}, u32[]{:S(2)}) copy-start(bf16[640,512]{1,0:T(8,128)(2,1)S(1)} %get-tuple-element.112.refs_0_.refs_3_) | copy-start | bytes 1966084
  70.4 34.6 %copy-start = (bf16[640,512]{1,0:T(8,128)(2,1)}, bf16[640,512]{1,0:T(8,128)(2,1)S(1)}, u32[]{:S(2)}) copy-start(bf16[640,512]{1,0:T(8,128)(2,1)S(1)} %get-tuple-element.111.refs_1_.refs_4_) | copy-start | bytes 1966084
  70.4 19.0 %collective-permute-start.4 = (bf16[640,512]{1,0:T(8,128)(2,1)S(1)}, bf16[640,512]{1,0:T(8,128)(2,1)}, u32[]{:S(2)}, u32[]{:S(2)}) collective-permute-start(bf16[640,512]{1,0:T(8,128)(2,1)S(1)} %get-tuple-element.112.refs_0_.refs_3_), channel_id=1, source_target_pairs={{0,64},{8,72},{16,80},{24,88},{32,96},{40,104},{48,112},{56,120},{... | collective-permute-start | bytes 1966088 | tf_op jit(solution)/shard_map/ppermute | solution.py:24
  71.8 17.8 %collective-permute-start.6 = (bf16[640,512]{1,0:T(8,128)(2,1)S(1)}, bf16[640,512]{1,0:T(8,128)(2,1)}, u32[]{:S(2)}, u32[]{:S(2)}) collective-permute-start(bf16[640,512]{1,0:T(8,128)(2,1)S(1)} %get-tuple-element.111.refs_1_.refs_4_), channel_id=1, source_target_pairs={{0,192},{8,200},{16,208},{24,216},{32,224},{40,232},{48,240},{56,2... | collective-permute-start | bytes 1966088 | tf_op jit(solution)/shard_map/ppermute | solution.py:24
  73.7 29.6 %collective-permute-start.11 = (bf16[640,512]{1,0:T(8,128)(2,1)S(1)}, bf16[640,512]{1,0:T(8,128)(2,1)S(1)}, u32[]{:S(2)}, u32[]{:S(2)}) collective-permute-start(bf16[640,512]{1,0:T(8,128)(2,1)S(1)} %get-tuple-element.111.refs_1_.refs_4_), channel_id=1, source_target_pairs={{0,64},{8,72},{16,80},{24,88},{32,96},{40,104},{48,112},{56,120},{... | collective-permute-start | bytes 1966088 | tf_op jit(solution)/shard_map/ppermute | solution.py:24
  73.8 29.7 %collective-permute-start.12 = (bf16[640,512]{1,0:T(8,128)(2,1)S(1)}, bf16[640,512]{1,0:T(8,128)(2,1)S(1)}, u32[]{:S(2)}, u32[]{:S(2)}) collective-permute-start(bf16[640,512]{1,0:T(8,128)(2,1)S(1)} %get-tuple-element.112.refs_0_.refs_3_), channel_id=1, source_target_pairs={{0,192},{8,200},{16,208},{24,216},{32,224},{40,232},{48,240},{56,2... | collective-permute-start | bytes 1966088 | tf_op jit(solution)/shard_map/ppermute | solution.py:24
  89.4 39.3 %collective-permute-start.5 = (bf16[640,512]{1,0:T(8,128)(2,1)}, bf16[640,512]{1,0:T(8,128)(2,1)}, u32[]{:S(2)}, u32[]{:S(2)}) collective-permute-start(bf16[640,512]{1,0:T(8,128)(2,1)} %collective-permute-done.4.refs_2_.refs_5_), channel_id=1, source_target_pairs={{0,64},{8,72},{16,80},{24,88},{32,96},{40,104},{48,112},{56,120},{... | collective-permute-start | bytes 1966088 | tf_op jit(solution)/shard_map/ppermute | solution.py:24
  89.6 39.1 %collective-permute-start.7 = (bf16[640,512]{1,0:T(8,128)(2,1)}, bf16[640,512]{1,0:T(8,128)(2,1)}, u32[]{:S(2)}, u32[]{:S(2)}) collective-permute-start(bf16[640,512]{1,0:T(8,128)(2,1)} %collective-permute-done.6.refs_5_.refs_10_), channel_id=1, source_target_pairs={{0,192},{8,200},{16,208},{24,216},{32,224},{40,232},{48,240},{56,2... | collective-permute-start | bytes 1966088 | tf_op jit(solution)/shard_map/ppermute | solution.py:24
  103.3 0.9 copy-start.2
  104.2 0.8 copy-start.3
  125.5 18.9 %collective-permute-start.13 = (bf16[640,512]{1,0:T(8,128)(2,1)}, bf16[640,512]{1,0:T(8,128)(2,1)S(1)}, u32[]{:S(2)}, u32[]{:S(2)}) collective-permute-start(bf16[640,512]{1,0:T(8,128)(2,1)} %get-tuple-element.68), channel_id=1, source_target_pairs={{0,64},{8,72},{16,80},{24,88},{32,96},{40,104},{48,112},{56,120},{... | collective-permute-start | bytes 1966088 | tf_op jit(solution)/shard_map/ppermute | solution.py:24
  126.9 17.4 %collective-permute-start.14 = (bf16[640,512]{1,0:T(8,128)(2,1)}, bf16[640,512]{1,0:T(8,128)(2,1)}, u32[]{:S(2)}, u32[]{:S(2)}) collective-permute-start(bf16[640,512]{1,0:T(8,128)(2,1)} %get-tuple-element.69), channel_id=1, source_target_pairs={{0,192},{8,200},{16,208},{24,216},{32,224},{40,232},{48,240},{56,2... | collective-permute-start | bytes 1966088 | tf_op jit(solution)/shard_map/ppermute | solution.py:24
  144.3 1.1 copy-start.7
  145.4 4.2 %copy-start.6 = (bf16[640,512]{1,0:T(8,128)(2,1)S(1)}, bf16[640,512]{1,0:T(8,128)(2,1)}, u32[]{:S(2)}) copy-start(bf16[640,512]{1,0:T(8,128)(2,1)} %get-tuple-element.79) | copy-start | bytes 1966084
  147.6 18.9 %collective-permute-start.18 = (bf16[640,512]{1,0:T(8,128)(2,1)}, bf16[640,512]{1,0:T(8,128)(2,1)}, u32[]{:S(2)}, u32[]{:S(2)}) collective-permute-start(bf16[640,512]{1,0:T(8,128)(2,1)} %add_convert_fusion.2), channel_id=1, source_target_pairs={{0,192},{8,200},{16,208},{24,216},{32,224},{40,232},{48,240},{56,2... | collective-permute-start | bytes 1966088 | tf_op jit(solution)/shard_map/ppermute | solution.py:24
  150.6 30.6 %copy-start.5 = (bf16[640,512]{1,0:T(8,128)(2,1)S(1)}, bf16[640,512]{1,0:T(8,128)(2,1)}, u32[]{:S(2)}) copy-start(bf16[640,512]{1,0:T(8,128)(2,1)} %get-tuple-element.78) | copy-start | bytes 1966084
  150.6 19.2 %collective-permute-start.15 = (bf16[640,512]{1,0:T(8,128)(2,1)}, bf16[640,512]{1,0:T(8,128)(2,1)}, u32[]{:S(2)}, u32[]{:S(2)}) collective-permute-start(bf16[640,512]{1,0:T(8,128)(2,1)} %add_convert_fusion.3), channel_id=1, source_target_pairs={{0,64},{8,72},{16,80},{24,88},{32,96},{40,104},{48,112},{56,120},{... | collective-permute-start | bytes 1966088 | tf_op jit(solution)/shard_map/ppermute | solution.py:24
  150.7 30.6 %collective-permute-start.16 = (bf16[640,512]{1,0:T(8,128)(2,1)}, bf16[640,512]{1,0:T(8,128)(2,1)}, u32[]{:S(2)}, u32[]{:S(2)}) collective-permute-start(bf16[640,512]{1,0:T(8,128)(2,1)} %get-tuple-element.81), channel_id=1, source_target_pairs={{0,64},{8,72},{16,80},{24,88},{32,96},{40,104},{48,112},{56,120},{... | collective-permute-start | bytes 1966088 | tf_op jit(solution)/shard_map/ppermute | solution.py:24
  151.2 30.1 %collective-permute-start.17 = (bf16[640,512]{1,0:T(8,128)(2,1)}, bf16[640,512]{1,0:T(8,128)(2,1)}, u32[]{:S(2)}, u32[]{:S(2)}) collective-permute-start(bf16[640,512]{1,0:T(8,128)(2,1)} %get-tuple-element.82), channel_id=1, source_target_pairs={{0,192},{8,200},{16,208},{24,216},{32,224},{40,232},{48,240},{56,2... | collective-permute-start | bytes 1966088 | tf_op jit(solution)/shard_map/ppermute | solution.py:24
  185.0 22.3 %copy-start.4 = (f32[640,256]{1,0:T(8,128)S(1)}, f32[640,256]{1,0:T(8,128)}, u32[]{:S(2)}) copy-start(f32[640,256]{1,0:T(8,128)} %get-tuple-element.107) | copy-start | bytes 1966084
  185.0 22.3 %all-to-all-start.2 = ((bf16[8,80,1024]{2,1,0:T(8,128)(2,1)}), bf16[8,80,1024]{2,1,0:T(8,128)(2,1)S(1)}, u32[]{:S(2)}, u32[]{:S(2)}) async-start(bf16[8,80,1024]{2,1,0:T(8,128)(2,1)} %bitcast.29), calls=%async_computation.2 | async-start | bytes 2621440 | tf_op jit(solution)/shard_map/all_to_all | solution.py:311
  208.8 0.7 slice-start.1
  208.8 1.1 slice-start
  210.8 21.0 %all-to-all-start.3 = ((bf16[8,88,512]{2,1,0:T(8,128)(2,1)}), bf16[8,88,512]{2,1,0:T(8,128)(2,1)S(1)}, u32[]{:S(2)}, u32[]{:S(2)}) async-start(bf16[8,88,512]{2,1,0:T(8,128)(2,1)} %fusion.2), calls=%async_computation.4 | async-start | bytes 1441792 | tf_op jit(solution)/shard_map/all_to_all | solution.py:311
  216.6 5.3 %copy-start.13 = (s32[1,2,2,128]{3,2,1,0:T(2,128)S(1)}, s32[1,2,2,128]{3,2,1,0:T(2,128)}, u32[]{:S(2)}) copy-start(s32[1,2,2,128]{3,2,1,0:T(2,128)} %get-tuple-element.130) | copy-start | bytes 6148
  216.7 15.1 %collective-permute-start.19 = (bf16[3,256,128]{2,1,0:T(8,128)(2,1)S(1)}, bf16[3,256,128]{2,1,0:T(8,128)(2,1)S(1)}, u32[]{:S(2)}, u32[]{:S(2)}) collective-permute-start(bf16[3,256,128]{2,1,0:T(8,128)(2,1)S(1)} %pad_maximum_fusion.4), channel_id=1, source_target_pairs={{0,24},{8,32},{16,40},{24,48},{32,56},{40,0},{48,8},{56,16},{64,88... | collective-permute-start | bytes 589832 | tf_op jit(solution)/shard_map/ppermute | solution.py:19
  219.9 11.3 %collective-permute-start.20 = (bf16[2,256,128]{2,1,0:T(8,128)(2,1)S(1)}, bf16[2,256,128]{2,1,0:T(8,128)(2,1)S(1)}, u32[]{:S(2)}, u32[]{:S(2)}) collective-permute-start(bf16[2,256,128]{2,1,0:T(8,128)(2,1)S(1)} %pad_maximum_fusion.5), channel_id=1, source_target_pairs={{0,40},{8,48},{16,56},{24,0},{32,8},{40,16},{48,24},{56,32},{64,10... | collective-permute-start | bytes 393224 | tf_op jit(solution)/shard_map/ppermute | solution.py:19
  232.9 12.7 %copy-start.9 = (bf16[256,128]{1,0:T(8,128)(2,1)S(1)}, bf16[256,128]{1,0:T(8,128)(2,1)}, u32[]{:S(2)}) copy-start(bf16[256,128]{1,0:T(8,128)(2,1)} %param.7) | copy-start | bytes 196612
  233.0 13.3 %collective-permute-start.23 = (bf16[264,128]{1,0:T(8,128)(2,1)S(1)}, bf16[264,128]{1,0:T(8,128)(2,1)S(1)}, u32[]{:S(2)}, u32[]{:S(2)}) collective-permute-start(bf16[264,128]{1,0:T(8,128)(2,1)S(1)} %get-tuple-element.132), channel_id=1, source_target_pairs={{0,64},{8,72},{16,80},{24,88},{32,96},{40,104},{48,112},{56,120},{... | collective-permute-start | bytes 202760 | tf_op jit(solution)/shard_map/ppermute | solution.py:24
  233.7 12.6 %collective-permute-start.24 = (bf16[264,128]{1,0:T(8,128)(2,1)S(1)}, bf16[264,128]{1,0:T(8,128)(2,1)S(1)}, u32[]{:S(2)}, u32[]{:S(2)}) collective-permute-start(bf16[264,128]{1,0:T(8,128)(2,1)S(1)} %get-tuple-element.133), channel_id=1, source_target_pairs={{0,128},{8,136},{16,144},{24,152},{32,160},{40,168},{48,176},{56,1... | collective-permute-start | bytes 202760 | tf_op jit(solution)/shard_map/ppermute | solution.py:24
  236.4 10.0 %copy-start.11 = (bf16[256,128]{1,0:T(8,128)(2,1)S(1)}, bf16[256,128]{1,0:T(8,128)(2,1)}, u32[]{:S(2)}) copy-start(bf16[256,128]{1,0:T(8,128)(2,1)} %param.13) | copy-start | bytes 196612
  236.4 9.9 %collective-permute-start.25 = (bf16[264,128]{1,0:T(8,128)(2,1)S(1)}, bf16[264,128]{1,0:T(8,128)(2,1)S(1)}, u32[]{:S(2)}, u32[]{:S(2)}) collective-permute-start(bf16[264,128]{1,0:T(8,128)(2,1)S(1)} %get-tuple-element.134), channel_id=1, source_target_pairs={{0,192},{8,200},{16,208},{24,216},{32,224},{40,232},{48,240},{56,2... | collective-permute-start | bytes 202760 | tf_op jit(solution)/shard_map/ppermute | solution.py:24
  237.9 9.2 %copy-start.12 = (f32[256,2]{0,1:T(2,128)S(1)}, f32[256,2]{0,1:T(2,128)}, u32[]{:S(2)}) copy-start(f32[256,2]{0,1:T(2,128)} %param.9) | copy-start | bytes 6148
  238.0 5.6 %collective-permute-start.21 = (bf16[256,128]{1,0:T(8,128)(2,1)S(1)}, bf16[256,128]{1,0:T(8,128)(2,1)S(1)}, u32[]{:S(2)}, u32[]{:S(2)}) collective-permute-start(bf16[256,128]{1,0:T(8,128)(2,1)S(1)} %get-tuple-element.128), channel_id=1, source_target_pairs={{0,8},{8,16},{16,24},{24,32},{32,40},{40,48},{48,56},{56,0},{64,72... | collective-permute-start | bytes 196616 | tf_op jit(solution)/shard_map/ppermute | solution.py:19
  241.3 4.3 %collective-permute-start.22 = (bf16[256,128]{1,0:T(8,128)(2,1)S(1)}, bf16[256,128]{1,0:T(8,128)(2,1)S(1)}, u32[]{:S(2)}, u32[]{:S(2)}) collective-permute-start(bf16[256,128]{1,0:T(8,128)(2,1)S(1)} %get-tuple-element.129), channel_id=1, source_target_pairs={{0,56},{8,0},{16,8},{24,16},{32,24},{40,32},{48,40},{56,48},{64,12... | collective-permute-start | bytes 196616 | tf_op jit(solution)/shard_map/ppermute | solution.py:19
Sparse Core Ops, SparseCore 0:
  47.1 68.2 all-gather.1
  144.5 63.5 reduce-scatter.1

commit v5 on v4

--- a/solution.py
+++ b/solution.py
@@ -133,7 +133,11 @@
         acc[...] = jnp.zeros_like(acc)
 
     weights_by_z(weights, gate_ref, up_ref)
-    acc[...] += jnp.dot(tok_ref[...], weights[...], preferred_element_type=f32)
+    cut = tok_ref.shape[2]
+    acc[...] += sum(
+        jnp.dot(tok_ref[j], weights[j * cut : (j + 1) * cut], preferred_element_type=f32)
+        for j in range(PAIR)
+    )
 
     @pl.when(step == NZ // PAIR - 1)
     def _():
@@ -233,9 +237,8 @@
 
     @pl.when(step < first)
     def _():
-        grad = dot_tn(tok_ref[...], act_ref[...]).astype(bf16)
         for j in range(PAIR):
-            block = grad[j * grad.shape[0] // PAIR : (j + 1) * grad.shape[0] // PAIR]
+            block = dot_tn(tok_ref[j], act_ref[...]).astype(bf16)
             gate_out[:, j] = block[:, :ff].reshape(NX, -1, ff)
             up_out[:, j] = block[:, ff:].reshape(NX, -1, ff)
 
@@ -322,7 +325,7 @@
     up_rows = exchange(up_rows.astype(bf16))
 
     dispatched = lax.all_gather(
-        tok_x, "section", axis_index_groups=Z_GROUPS, axis=1, tiled=True
+        tok_x, "section", axis_index_groups=Z_GROUPS, axis=0, tiled=False
     )
     ups = [half for pair in ring_gather_x(up_rows) for half in pair]
 
@@ -340,7 +343,7 @@
     def struct(shape, kind):
         return jax.ShapeDtypeStruct(shape, kind)
 
-    tok_spec = pl.BlockSpec((rows, PAIR * wide_x), lambda i, s: (0, clip(i, 0, NZ // PAIR)))
+    tok_spec = pl.BlockSpec((PAIR, rows, wide_x), lambda i, s: (clip(i, 0, NZ // PAIR), 0, 0))
     weight_scratch = pltpu.VMEM((PAIR * wide_x, 2 * ff), bf16)
     (early,) = call(
         early_kernel,

time: 256 us -> 256 us (level)
  no operation moved by 1% of the time
where the time goes in v5:
time: 256 us; the launch traced here: 254 us
  waiting for transfers between devices  85.7 us (33%)
  starting transfers between devices  63.4 us (25%)
  Pallas kernels  43.7 us (17%)
  blocking collectives  22.2 us (9%)
  between operations  14.7 us (6%)
  other arithmetic  14.2 us (6%)
  local copies, waits for them, and re-layouts  6.73 us (3%)
  matrix products  3.75 us (1%)
    ppermute x18, waiting for transfers between devices, shift_x(): return lax.ppermute(value, 'section', pairs)  44.4 us
    pallas_call x6, Pallas kernels, call(): pl.pallas_call(kernel, grid_spec=pltpu.PrefetchScalarGridSpec(num_scalar_...  43.7 us
    ppermute x18, starting transfers between devices, shift_x(): return lax.ppermute(value, 'section', pairs)  28.8 us
    all_to_all x1, blocking collectives, exchange(): lax.all_to_all(value.reshape(experts, -1, value.shape[-1]), 'expert', spl...  22.2 us
    ppermute x8, starting transfers between devices, shift_z(): return lax.ppermute(value, 'section', pairs)  19.8 us
    ppermute x8, waiting for transfers between devices, shift_z(): return lax.ppermute(value, 'section', pairs)  19.2 us
    all_to_all x3, waiting for transfers between devices, exchange(): lax.all_to_all(value.reshape(experts, -1, value.shape[-1]), 'expert', spl...  17.3 us
    all_to_all x3, starting transfers between devices, exchange(): lax.all_to_all(value.reshape(experts, -1, value.shape[-1]), 'expert', spl...  14.8 us
  transfers between devices with their start and end apart: 31, of which 15 were waited for; matrix products, arithmetic and copies ran while one was open for 6% of the time, Pallas kernels for 17%

profile of v5, /device:TPU:8, one launch (start us, length us, event | category | flops | bytes accessed | tf_op | source)
XLA Modules:
  0.0 254.5 jit_solution(4924812159977364225)
XLA Ops:
  7.2 2.0 collective-permute-start
  9.2 4.0 %collective-permute-start.1 = (bf16[256,128]{1,0:T(8,128)(2,1)}, bf16[256,128]{1,0:T(8,128)(2,1)S(1)}, u32[]{:S(2)}, u32[]{:S(2)}) collective-permute-start(bf16[256,128]{1,0:T(8,128)(2,1)} %param.13), channel_id=1, source_target_pairs={{0,56},{8,0},{16,8},{24,16},{32,24},{40,32},{48,40},{56,48},{64,12... | collective-permute-start | bytes 196616 | tf_op jit(solution)/shard_map/ppermute | solution.py:19
  13.2 0.8 copy.58
  14.7 1.3 fusion.25
  16.0 1.9 select_reduce_fusion
  17.9 0.9 convolution_convert_fusion
  18.8 2.0 collective-permute-start.2
  20.8 4.9 %all-to-all-start = ((bf16[8,80,128]{2,1,0:T(8,128)(2,1)}), bf16[8,80,128]{2,1,0:T(8,128)(2,1)S(1)}, u32[]{:S(2)}, u32[]{:S(2)}) async-start(bf16[8,80,128]{2,1,0:T(8,128)(2,1)} %bitcast.6), calls=%async_computation | async-start | bytes 327680 | tf_op jit(solution)/shard_map/all_to_all | solution.py:314
  25.7 3.2 %collective-permute-start.3 = (bf16[2,256,128]{2,1,0:T(8,128)(2,1)S(1)}, bf16[2,256,128]{2,1,0:T(8,128)(2,1)S(1)}, u32[]{:S(2)}, u32[]{:S(2)}) collective-permute-start(bf16[2,256,128]{2,1,0:T(8,128)(2,1)S(1)} %slice.45), channel_id=1, source_target_pairs={{0,40},{8,48},{16,56},{24,0},{32,8},{40,16},{48,24},{56,32},{64,10... | collective-permute-start | bytes 393224 | tf_op jit(solution)/shard_map/ppermute | solution.py:19
  29.0 4.4 %collective-permute-done.3 = bf16[2,256,128]{2,1,0:T(8,128)(2,1)S(1)} collective-permute-done((bf16[2,256,128]{2,1,0:T(8,128)(2,1)S(1)}, bf16[2,256,128]{2,1,0:T(8,128)(2,1)S(1)}, u32[]{:S(2)}, u32[]{:S(2)}) %collective-permute-start.3) | collective-permute-done | bytes 131104 | tf_op jit(solution)/shard_map/ppermute | solution.py:19
  33.4 0.7 collective-permute-done.2
  34.1 1.5 collective-permute-start.8
  35.6 2.7 %collective-permute-start.9 = (bf16[640,128]{1,0:T(8,128)(2,1)S(1)}, bf16[640,128]{1,0:T(8,128)(2,1)S(1)}, u32[]{:S(2)}, u32[]{:S(2)}) collective-permute-start(bf16[640,128]{1,0:T(8,128)(2,1)S(1)} %bitcast.163), channel_id=1, source_target_pairs={{0,128},{8,136},{16,144},{24,152},{32,160},{40,168},{48,176},{56,1... | collective-permute-start | bytes 491528 | tf_op jit(solution)/shard_map/ppermute | solution.py:24
  38.3 1.4 collective-permute-start.10
  39.7 1.7 collective-permute-done.8
  41.4 4.5 %collective-permute-done.9 = bf16[640,128]{1,0:T(8,128)(2,1)S(1)} collective-permute-done((bf16[640,128]{1,0:T(8,128)(2,1)S(1)}, bf16[640,128]{1,0:T(8,128)(2,1)S(1)}, u32[]{:S(2)}, u32[]{:S(2)}) %collective-permute-start.9) | collective-permute-done | bytes 163872 | tf_op jit(solution)/shard_map/ppermute | solution.py:24
  46.1 0.9 pad_maximum_fusion.2
  48.1 22.2 %all_to_all.20 = bf16[8,80,1024]{2,1,0:T(8,128)(2,1)S(1)} all-to-all(bf16[8,80,1024]{2,1,0:T(8,128)(2,1)S(1)} %bitcast.152), channel_id=1, replica_groups=mesh['section'=32,'expert'=8] {'expert'}, dimensions={0} | all-to-all | bytes 2621440 | tf_op jit(solution)/shard_map/all_to_all | solution.py:314
  70.4 1.4 collective-permute-start.4
  71.8 1.9 collective-permute-start.6
  73.8 3.1 %collective-permute-start.12 = (bf16[640,512]{1,0:T(8,128)(2,1)S(1)}, bf16[640,512]{1,0:T(8,128)(2,1)S(1)}, u32[]{:S(2)}, u32[]{:S(2)}) collective-permute-start(bf16[640,512]{1,0:T(8,128)(2,1)S(1)} %get-tuple-element.112.refs_0_.refs_3_), channel_id=1, source_target_pairs={{0,192},{8,200},{16,208},{24,216},{32,224},{40,232},{48,240},{56,2... | collective-permute-start | bytes 1966088 | tf_op jit(solution)/shard_map/ppermute | solution.py:24
  76.9 12.5 %collective-permute-done.4.refs_2_.refs_5_ = bf16[640,512]{1,0:T(8,128)(2,1)} collective-permute-done((bf16[640,512]{1,0:T(8,128)(2,1)S(1)}, bf16[640,512]{1,0:T(8,128)(2,1)}, u32[]{:S(2)}, u32[]{:S(2)}) %collective-permute-start.4) | collective-permute-done | bytes 655392 | tf_op jit(solution)/shard_map/ppermute | solution.py:24
  89.6 3.1 %collective-permute-start.7 = (bf16[640,512]{1,0:T(8,128)(2,1)}, bf16[640,512]{1,0:T(8,128)(2,1)}, u32[]{:S(2)}, u32[]{:S(2)}) collective-permute-start(bf16[640,512]{1,0:T(8,128)(2,1)} %collective-permute-done.6.refs_5_.refs_10_), channel_id=1, source_target_pairs={{0,192},{8,200},{16,208},{24,216},{32,224},{40,232},{48,240},{56,2... | collective-permute-start | bytes 1966088 | tf_op jit(solution)/shard_map/ppermute | solution.py:24
  92.7 10.7 %collective-permute-done.11.refs_3_.refs_6_ = bf16[640,512]{1,0:T(8,128)(2,1)S(1)} collective-permute-done((bf16[640,512]{1,0:T(8,128)(2,1)S(1)}, bf16[640,512]{1,0:T(8,128)(2,1)S(1)}, u32[]{:S(2)}, u32[]{:S(2)}) %collective-permute-start.11) | collective-permute-done | bytes 655392 | tf_op jit(solution)/shard_map/ppermute | solution.py:24
  103.5 0.7 copy-done.2
  104.2 0.8 copy-done.3
  105.0 5.6 %shard_map.118.refs_3_ = f32[640,256]{1,0:T(8,128)} custom-call(s32[1]{0:T(128)} %bitcast.2.x_ref, bf16[640,512]{1,0:T(8,128)(2,1)} %copy-done.1, bf16[640,512]{1,0:T(8,128)(2,1)} %copy-done, bf16[640,512]{1,0:T(8,128)(2,1)} %collective-permute-done.4.refs_2_.refs_5_, bf16[640,512]{1,0:T(8,128)(2,1)} %copy-done.2, bf16[640,512]{1,0:T(8,128)(2,1)} %copy-done.3, ...), custom_call_target="tpu_custom_call" | custom-call | tf_op jit(solution)/shard_map/pallas_call | solution.py:259
  110.6 4.8 %all-gather.3.cloned.1.call-done = bf16[5120,512]{1,0:T(8,128)(2,1)} async-done(((bf16[640,512]{1,0:T(8,128)(2,1)}), bf16[5120,512]{1,0:T(8,128)(2,1)}) %all-gather.3.cloned.1.call-update) | async-done | bytes 5242896 | tf_op jit(solution)/shard_map/all_gather | solution.py:327
  115.4 7.5 %shard_map.119 = (f32[640,256]{1,0:T(8,128)}, f32[640,256]{1,0:T(8,128)}, bf16[640,256]{1,0:T(8,128)(2,1)}) custom-call(s32[1]{0:T(128)} %bitcast.2.x_ref, bf16[8,640,512]{2,1,0:T(8,128)(2,1)} %bitcast.148, bf16[4,8,128,256]{3,2,1,0:T(8,128)(2,1)} %bitcast.158, bf16[4,8,128,256]{3,2,1,0:T(8,128)(2,1)} %bitcast.160), custom_call_target="tpu_custom_call" | custom-call | flops 2684354560 | bytes 9437184 | tf_op jit(solution)/shard_map/pallas_call | solution.py:259
  122.9 2.5 shard_map.121
  125.4 1.5 collective-permute-start.13
  126.9 1.8 collective-permute-start.14
  128.7 10.3 %shard_map.120 = (bf16[8,648,512]{2,1,0:T(8,128)(2,1)}, bf16[640,512]{1,0:T(8,128)(2,1)}) custom-call(s32[1]{0:T(128)} %bitcast.2.x_ref, bf16[640,512]{1,0:T(8,128)(2,1)} %collective-permute-done.5.refs_0_.refs_7_, bf16[640,512]{1,0:T(8,128)(2,1)} %collective-permute-done.7.refs_1_.refs_8_, bf16[256,4096]{1,0:T(8,128)(2,1)} %bitcast.145, ...), custom_call_target="tpu_custom_call" | custom-call | tf_op jit(solution)/shard_map/pallas_call | solution.py:259
  139.0 5.3 %shard_map.122 = (bf16[640,512]{1,0:T(8,128)(2,1)}, bf16[640,512]{1,0:T(8,128)(2,1)}, bf16[640,512]{1,0:T(8,128)(2,1)}, bf16[640,512]{1,0:T(8,128)(2,1)}, bf16[6...) custom-call(s32[1]{0:T(128)} %bitcast.2.x_ref, bf16[640,256]{1,0:T(8,128)(2,1)} %get-tuple-element.71.refs_8_.hid_ref.refs_2_, ...), custom_call_target="tpu_custom_call" | custom-call | tf_op jit(solution)/shard_map/pallas_call | solution.py:259
  144.4 1.1 copy-done.7
  145.4 2.2 add_convert_fusion.2
  147.6 2.1 collective-permute-start.18
  149.6 1.0 add_convert_fusion.3
  151.2 2.8 %collective-permute-start.17 = (bf16[640,512]{1,0:T(8,128)(2,1)}, bf16[640,512]{1,0:T(8,128)(2,1)}, u32[]{:S(2)}, u32[]{:S(2)}) collective-permute-start(bf16[640,512]{1,0:T(8,128)(2,1)} %get-tuple-element.82), channel_id=1, source_target_pairs={{0,192},{8,200},{16,208},{24,216},{32,224},{40,232},{48,240},{56,2... | collective-permute-start | bytes 1966088 | tf_op jit(solution)/shard_map/ppermute | solution.py:24
  153.9 12.5 %shard_map.123 = (bf16[4,8,128,256]{3,2,1,0:T(8,128)(2,1)}, bf16[4,8,128,256]{3,2,1,0:T(8,128)(2,1)}, bf16[256,4096]{1,0:T(8,128)(2,1)}) custom-call(s32[1]{0:T(128)} %bitcast.2.x_ref, bf16[8,640,512]{2,1,0:T(8,128)(2,1)} %bitcast.149, bf16[640,512]{1,0:T(8,128)(2,1)} %get-tuple-element.85.refs_1_, ...), custom_call_target="tpu_custom_call" | custom-call | tf_op jit(solution)/shard_map/pallas_call | solution.py:259
  166.4 3.4 %collective-permute-done.15 = bf16[640,512]{1,0:T(8,128)(2,1)} collective-permute-done((bf16[640,512]{1,0:T(8,128)(2,1)}, bf16[640,512]{1,0:T(8,128)(2,1)}, u32[]{:S(2)}, u32[]{:S(2)}) %collective-permute-start.15) | collective-permute-done | bytes 655392 | tf_op jit(solution)/shard_map/ppermute | solution.py:24
  169.9 11.4 %collective-permute-done.16 = bf16[640,512]{1,0:T(8,128)(2,1)} collective-permute-done((bf16[640,512]{1,0:T(8,128)(2,1)}, bf16[640,512]{1,0:T(8,128)(2,1)}, u32[]{:S(2)}, u32[]{:S(2)}) %collective-permute-start.16) | collective-permute-done | bytes 655392 | tf_op jit(solution)/shard_map/ppermute | solution.py:24
  181.3 2.4 add_convert_fusion
  183.7 1.3 pad_maximum_fusion
  185.0 5.0 %all-to-all-start.2 = ((bf16[8,80,1024]{2,1,0:T(8,128)(2,1)}), bf16[8,80,1024]{2,1,0:T(8,128)(2,1)S(1)}, u32[]{:S(2)}, u32[]{:S(2)}) async-start(bf16[8,80,1024]{2,1,0:T(8,128)(2,1)} %bitcast.30), calls=%async_computation.2 | async-start | bytes 2621440 | tf_op jit(solution)/shard_map/all_to_all | solution.py:314
  190.0 17.3 %all-to-all-done.2 = bf16[8,80,1024]{2,1,0:T(8,128)(2,1)S(1)} async-done(((bf16[8,80,1024]{2,1,0:T(8,128)(2,1)}), bf16[8,80,1024]{2,1,0:T(8,128)(2,1)S(1)}, u32[]{:S(2)}, u32[]{:S(2)}) %all-to-all-start.2) | async-done | bytes 1310752 | tf_op jit(solution)/shard_map/all_to_all | solution.py:314
  207.3 1.4 fusion.31
  208.8 0.7 slice-done.1
  209.9 0.9 fusion.2
  210.8 4.9 %all-to-all-start.3 = ((bf16[8,88,512]{2,1,0:T(8,128)(2,1)}), bf16[8,88,512]{2,1,0:T(8,128)(2,1)S(1)}, u32[]{:S(2)}, u32[]{:S(2)}) async-start(bf16[8,88,512]{2,1,0:T(8,128)(2,1)} %fusion.2), calls=%async_computation.4 | async-start | bytes 1441792 | tf_op jit(solution)/shard_map/all_to_all | solution.py:314
  215.9 0.7 constant_dynamic-slice_fusion.1
  216.7 3.0 %collective-permute-start.19 = (bf16[3,256,128]{2,1,0:T(8,128)(2,1)S(1)}, bf16[3,256,128]{2,1,0:T(8,128)(2,1)S(1)}, u32[]{:S(2)}, u32[]{:S(2)}) collective-permute-start(bf16[3,256,128]{2,1,0:T(8,128)(2,1)S(1)} %pad_maximum_fusion.4), channel_id=1, source_target_pairs={{0,24},{8,32},{16,40},{24,48},{32,56},{40,0},{48,8},{56,16},{64,88... | collective-permute-start | bytes 589832 | tf_op jit(solution)/shard_map/ppermute | solution.py:19
  219.8 2.2 collective-permute-start.20
  222.0 9.2 %collective-permute-done.20 = bf16[2,256,128]{2,1,0:T(8,128)(2,1)S(1)} collective-permute-done((bf16[2,256,128]{2,1,0:T(8,128)(2,1)S(1)}, bf16[2,256,128]{2,1,0:T(8,128)(2,1)S(1)}, u32[]{:S(2)}, u32[]{:S(2)}) %collective-permute-start.20) | collective-permute-done | bytes 131104 | tf_op jit(solution)/shard_map/ppermute | solution.py:19
  231.2 0.6 collective-permute-done.19
  233.0 0.7 collective-permute-start.23
  233.7 2.7 %collective-permute-start.24 = (bf16[264,128]{1,0:T(8,128)(2,1)S(1)}, bf16[264,128]{1,0:T(8,128)(2,1)S(1)}, u32[]{:S(2)}, u32[]{:S(2)}) collective-permute-start(bf16[264,128]{1,0:T(8,128)(2,1)S(1)} %get-tuple-element.133), channel_id=1, source_target_pairs={{0,128},{8,136},{16,144},{24,152},{32,160},{40,168},{48,176},{56,1... | collective-permute-start | bytes 202760 | tf_op jit(solution)/shard_map/ppermute | solution.py:24
  236.4 1.5 collective-permute-start.25
  238.0 3.4 %collective-permute-start.21 = (bf16[256,128]{1,0:T(8,128)(2,1)S(1)}, bf16[256,128]{1,0:T(8,128)(2,1)S(1)}, u32[]{:S(2)}, u32[]{:S(2)}) collective-permute-start(bf16[256,128]{1,0:T(8,128)(2,1)S(1)} %get-tuple-element.128), channel_id=1, source_target_pairs={{0,8},{8,16},{16,24},{24,32},{32,40},{40,48},{48,56},{56,0},{64,72... | collective-permute-start | bytes 196616 | tf_op jit(solution)/shard_map/ppermute | solution.py:19
  241.3 2.2 collective-permute-done.21
  243.5 2.1 collective-permute-done.22
  245.6 0.7 fusion.18
  246.3 0.7 fusion.8
  247.0 0.6 bitcast_divide_fusion
  (108 shorter events, 4.9 us)
Async XLA Ops:
  7.2 11.6 %copy-start.10 = (bf16[256,128]{1,0:T(8,128)(2,1)S(1)}, bf16[256,128]{1,0:T(8,128)(2,1)}, u32[]{:S(2)}) copy-start(bf16[256,128]{1,0:T(8,128)(2,1)} %param.13) | copy-start | bytes 196612
  7.2 10.7 %copy-start.8 = (bf16[256,128]{1,0:T(8,128)(2,1)S(1)}, bf16[256,128]{1,0:T(8,128)(2,1)}, u32[]{:S(2)}) copy-start(bf16[256,128]{1,0:T(8,128)(2,1)} %param.7) | copy-start | bytes 196612
  7.2 11.6 %collective-permute-start = (bf16[256,128]{1,0:T(8,128)(2,1)}, bf16[256,128]{1,0:T(8,128)(2,1)S(1)}, u32[]{:S(2)}, u32[]{:S(2)}) collective-permute-start(bf16[256,128]{1,0:T(8,128)(2,1)} %param.13), channel_id=1, source_target_pairs={{0,8},{8,16},{16,24},{24,32},{32,40},{40,48},{48,56},{56,0},{64,72... | collective-permute-start | bytes 196616 | tf_op jit(solution)/shard_map/ppermute | solution.py:19
  9.2 9.6 %collective-permute-start.1 = (bf16[256,128]{1,0:T(8,128)(2,1)}, bf16[256,128]{1,0:T(8,128)(2,1)S(1)}, u32[]{:S(2)}, u32[]{:S(2)}) collective-permute-start(bf16[256,128]{1,0:T(8,128)(2,1)} %param.13), channel_id=1, source_target_pairs={{0,56},{8,0},{16,8},{24,16},{32,24},{40,32},{48,40},{56,48},{64,12... | collective-permute-start | bytes 196616 | tf_op jit(solution)/shard_map/ppermute | solution.py:19
  18.8 15.2 %collective-permute-start.2 = (bf16[3,256,128]{2,1,0:T(8,128)(2,1)S(1)}, bf16[3,256,128]{2,1,0:T(8,128)(2,1)S(1)}, u32[]{:S(2)}, u32[]{:S(2)}) collective-permute-start(bf16[3,256,128]{2,1,0:T(8,128)(2,1)S(1)} %pad_maximum_fusion.3), channel_id=1, source_target_pairs={{0,24},{8,32},{16,40},{24,48},{32,56},{40,0},{48,8},{56,16},{64,88... | collective-permute-start | bytes 589832 | tf_op jit(solution)/shard_map/ppermute | solution.py:19
  20.8 12.6 %all-to-all-start = ((bf16[8,80,128]{2,1,0:T(8,128)(2,1)}), bf16[8,80,128]{2,1,0:T(8,128)(2,1)S(1)}, u32[]{:S(2)}, u32[]{:S(2)}) async-start(bf16[8,80,128]{2,1,0:T(8,128)(2,1)} %bitcast.6), calls=%async_computation | async-start | bytes 327680 | tf_op jit(solution)/shard_map/all_to_all | solution.py:314
  25.7 89.7 %all-gather.3.cloned.1.call-start = ((), (), s32[]{:S(2)}) async-start(), calls=%async_computation.6 | async-start | bytes 5898240 | tf_op jit(solution)/shard_map/all_gather | solution.py:327
  25.7 7.6 %collective-permute-start.3 = (bf16[2,256,128]{2,1,0:T(8,128)(2,1)S(1)}, bf16[2,256,128]{2,1,0:T(8,128)(2,1)S(1)}, u32[]{:S(2)}, u32[]{:S(2)}) collective-permute-start(bf16[2,256,128]{2,1,0:T(8,128)(2,1)S(1)} %slice.45), channel_id=1, source_target_pairs={{0,40},{8,48},{16,56},{24,0},{32,8},{40,16},{48,24},{56,32},{64,10... | collective-permute-start | bytes 393224 | tf_op jit(solution)/shard_map/ppermute | solution.py:19
  34.1 7.3 %collective-permute-start.8 = (bf16[640,128]{1,0:T(8,128)(2,1)S(1)}, bf16[640,128]{1,0:T(8,128)(2,1)S(1)}, u32[]{:S(2)}, u32[]{:S(2)}) collective-permute-start(bf16[640,128]{1,0:T(8,128)(2,1)S(1)} %bitcast.162), channel_id=1, source_target_pairs={{0,64},{8,72},{16,80},{24,88},{32,96},{40,104},{48,112},{56,120},{... | collective-permute-start | bytes 491528 | tf_op jit(solution)/shard_map/ppermute | solution.py:24
  35.6 10.3 %collective-permute-start.9 = (bf16[640,128]{1,0:T(8,128)(2,1)S(1)}, bf16[640,128]{1,0:T(8,128)(2,1)S(1)}, u32[]{:S(2)}, u32[]{:S(2)}) collective-permute-start(bf16[640,128]{1,0:T(8,128)(2,1)S(1)} %bitcast.163), channel_id=1, source_target_pairs={{0,128},{8,136},{16,144},{24,152},{32,160},{40,168},{48,176},{56,1... | collective-permute-start | bytes 491528 | tf_op jit(solution)/shard_map/ppermute | solution.py:24
  38.3 7.6 %collective-permute-start.10 = (bf16[640,128]{1,0:T(8,128)(2,1)S(1)}, bf16[640,128]{1,0:T(8,128)(2,1)S(1)}, u32[]{:S(2)}, u32[]{:S(2)}) collective-permute-start(bf16[640,128]{1,0:T(8,128)(2,1)S(1)} %bitcast.164), channel_id=1, source_target_pairs={{0,192},{8,200},{16,208},{24,216},{32,224},{40,232},{48,240},{56,2... | collective-permute-start | bytes 491528 | tf_op jit(solution)/shard_map/ppermute | solution.py:24
  47.0 161.8 %reduce-scatter.2.cloned.1.call-start = ((), (), s32[]{:S(2)}) async-start(), calls=%async_computation.5 | async-start | bytes 5971968 | tf_op jit(solution)/shard_map/reduce_scatter | solution.py:424
  70.4 33.0 %copy-start.1 = (bf16[640,512]{1,0:T(8,128)(2,1)}, bf16[640,512]{1,0:T(8,128)(2,1)S(1)}, u32[]{:S(2)}) copy-start(bf16[640,512]{1,0:T(8,128)(2,1)S(1)} %get-tuple-element.112.refs_0_.refs_3_) | copy-start | bytes 1966084
  70.4 34.6 %copy-start = (bf16[640,512]{1,0:T(8,128)(2,1)}, bf16[640,512]{1,0:T(8,128)(2,1)S(1)}, u32[]{:S(2)}) copy-start(bf16[640,512]{1,0:T(8,128)(2,1)S(1)} %get-tuple-element.111.refs_1_.refs_4_) | copy-start | bytes 1966084
  70.4 19.0 %collective-permute-start.4 = (bf16[640,512]{1,0:T(8,128)(2,1)S(1)}, bf16[640,512]{1,0:T(8,128)(2,1)}, u32[]{:S(2)}, u32[]{:S(2)}) collective-permute-start(bf16[640,512]{1,0:T(8,128)(2,1)S(1)} %get-tuple-element.112.refs_0_.refs_3_), channel_id=1, source_target_pairs={{0,64},{8,72},{16,80},{24,88},{32,96},{40,104},{48,112},{56,120},{... | collective-permute-start | bytes 1966088 | tf_op jit(solution)/shard_map/ppermute | solution.py:24
  71.8 17.8 %collective-permute-start.6 = (bf16[640,512]{1,0:T(8,128)(2,1)S(1)}, bf16[640,512]{1,0:T(8,128)(2,1)}, u32[]{:S(2)}, u32[]{:S(2)}) collective-permute-start(bf16[640,512]{1,0:T(8,128)(2,1)S(1)} %get-tuple-element.111.refs_1_.refs_4_), channel_id=1, source_target_pairs={{0,192},{8,200},{16,208},{24,216},{32,224},{40,232},{48,240},{56,2... | collective-permute-start | bytes 1966088 | tf_op jit(solution)/shard_map/ppermute | solution.py:24
  73.7 29.6 %collective-permute-start.11 = (bf16[640,512]{1,0:T(8,128)(2,1)S(1)}, bf16[640,512]{1,0:T(8,128)(2,1)S(1)}, u32[]{:S(2)}, u32[]{:S(2)}) collective-permute-start(bf16[640,512]{1,0:T(8,128)(2,1)S(1)} %get-tuple-element.111.refs_1_.refs_4_), channel_id=1, source_target_pairs={{0,64},{8,72},{16,80},{24,88},{32,96},{40,104},{48,112},{56,120},{... | collective-permute-start | bytes 1966088 | tf_op jit(solution)/shard_map/ppermute | solution.py:24
  73.8 29.7 %collective-permute-start.12 = (bf16[640,512]{1,0:T(8,128)(2,1)S(1)}, bf16[640,512]{1,0:T(8,128)(2,1)S(1)}, u32[]{:S(2)}, u32[]{:S(2)}) collective-permute-start(bf16[640,512]{1,0:T(8,128)(2,1)S(1)} %get-tuple-element.112.refs_0_.refs_3_), channel_id=1, source_target_pairs={{0,192},{8,200},{16,208},{24,216},{32,224},{40,232},{48,240},{56,2... | collective-permute-start | bytes 1966088 | tf_op jit(solution)/shard_map/ppermute | solution.py:24
  89.4 39.3 %collective-permute-start.5 = (bf16[640,512]{1,0:T(8,128)(2,1)}, bf16[640,512]{1,0:T(8,128)(2,1)}, u32[]{:S(2)}, u32[]{:S(2)}) collective-permute-start(bf16[640,512]{1,0:T(8,128)(2,1)} %collective-permute-done.4.refs_2_.refs_5_), channel_id=1, source_target_pairs={{0,64},{8,72},{16,80},{24,88},{32,96},{40,104},{48,112},{56,120},{... | collective-permute-start | bytes 1966088 | tf_op jit(solution)/shard_map/ppermute | solution.py:24
  89.6 39.1 %collective-permute-start.7 = (bf16[640,512]{1,0:T(8,128)(2,1)}, bf16[640,512]{1,0:T(8,128)(2,1)}, u32[]{:S(2)}, u32[]{:S(2)}) collective-permute-start(bf16[640,512]{1,0:T(8,128)(2,1)} %collective-permute-done.6.refs_5_.refs_10_), channel_id=1, source_target_pairs={{0,192},{8,200},{16,208},{24,216},{32,224},{40,232},{48,240},{56,2... | collective-permute-start | bytes 1966088 | tf_op jit(solution)/shard_map/ppermute | solution.py:24
  103.3 0.9 copy-start.2
  104.2 0.8 copy-start.3
  125.4 18.9 %collective-permute-start.13 = (bf16[640,512]{1,0:T(8,128)(2,1)}, bf16[640,512]{1,0:T(8,128)(2,1)S(1)}, u32[]{:S(2)}, u32[]{:S(2)}) collective-permute-start(bf16[640,512]{1,0:T(8,128)(2,1)} %get-tuple-element.68), channel_id=1, source_target_pairs={{0,64},{8,72},{16,80},{24,88},{32,96},{40,104},{48,112},{56,120},{... | collective-permute-start | bytes 1966088 | tf_op jit(solution)/shard_map/ppermute | solution.py:24
  126.9 17.4 %collective-permute-start.14 = (bf16[640,512]{1,0:T(8,128)(2,1)}, bf16[640,512]{1,0:T(8,128)(2,1)}, u32[]{:S(2)}, u32[]{:S(2)}) collective-permute-start(bf16[640,512]{1,0:T(8,128)(2,1)} %get-tuple-element.69), channel_id=1, source_target_pairs={{0,192},{8,200},{16,208},{24,216},{32,224},{40,232},{48,240},{56,2... | collective-permute-start | bytes 1966088 | tf_op jit(solution)/shard_map/ppermute | solution.py:24
  144.3 1.1 copy-start.7
  145.4 4.2 %copy-start.6 = (bf16[640,512]{1,0:T(8,128)(2,1)S(1)}, bf16[640,512]{1,0:T(8,128)(2,1)}, u32[]{:S(2)}) copy-start(bf16[640,512]{1,0:T(8,128)(2,1)} %get-tuple-element.79) | copy-start | bytes 1966084
  147.6 18.9 %collective-permute-start.18 = (bf16[640,512]{1,0:T(8,128)(2,1)}, bf16[640,512]{1,0:T(8,128)(2,1)}, u32[]{:S(2)}, u32[]{:S(2)}) collective-permute-start(bf16[640,512]{1,0:T(8,128)(2,1)} %add_convert_fusion.2), channel_id=1, source_target_pairs={{0,192},{8,200},{16,208},{24,216},{32,224},{40,232},{48,240},{56,2... | collective-permute-start | bytes 1966088 | tf_op jit(solution)/shard_map/ppermute | solution.py:24
  150.7 30.6 %copy-start.5 = (bf16[640,512]{1,0:T(8,128)(2,1)S(1)}, bf16[640,512]{1,0:T(8,128)(2,1)}, u32[]{:S(2)}) copy-start(bf16[640,512]{1,0:T(8,128)(2,1)} %get-tuple-element.78) | copy-start | bytes 1966084
  150.7 19.2 %collective-permute-start.15 = (bf16[640,512]{1,0:T(8,128)(2,1)}, bf16[640,512]{1,0:T(8,128)(2,1)}, u32[]{:S(2)}, u32[]{:S(2)}) collective-permute-start(bf16[640,512]{1,0:T(8,128)(2,1)} %add_convert_fusion.3), channel_id=1, source_target_pairs={{0,64},{8,72},{16,80},{24,88},{32,96},{40,104},{48,112},{56,120},{... | collective-permute-start | bytes 1966088 | tf_op jit(solution)/shard_map/ppermute | solution.py:24
  150.7 30.6 %collective-permute-start.16 = (bf16[640,512]{1,0:T(8,128)(2,1)}, bf16[640,512]{1,0:T(8,128)(2,1)}, u32[]{:S(2)}, u32[]{:S(2)}) collective-permute-start(bf16[640,512]{1,0:T(8,128)(2,1)} %get-tuple-element.81), channel_id=1, source_target_pairs={{0,64},{8,72},{16,80},{24,88},{32,96},{40,104},{48,112},{56,120},{... | collective-permute-start | bytes 1966088 | tf_op jit(solution)/shard_map/ppermute | solution.py:24
  151.2 30.1 %collective-permute-start.17 = (bf16[640,512]{1,0:T(8,128)(2,1)}, bf16[640,512]{1,0:T(8,128)(2,1)}, u32[]{:S(2)}, u32[]{:S(2)}) collective-permute-start(bf16[640,512]{1,0:T(8,128)(2,1)} %get-tuple-element.82), channel_id=1, source_target_pairs={{0,192},{8,200},{16,208},{24,216},{32,224},{40,232},{48,240},{56,2... | collective-permute-start | bytes 1966088 | tf_op jit(solution)/shard_map/ppermute | solution.py:24
  185.0 22.3 %copy-start.4 = (f32[640,256]{1,0:T(8,128)S(1)}, f32[640,256]{1,0:T(8,128)}, u32[]{:S(2)}) copy-start(f32[640,256]{1,0:T(8,128)} %get-tuple-element.107) | copy-start | bytes 1966084
  185.0 22.3 %all-to-all-start.2 = ((bf16[8,80,1024]{2,1,0:T(8,128)(2,1)}), bf16[8,80,1024]{2,1,0:T(8,128)(2,1)S(1)}, u32[]{:S(2)}, u32[]{:S(2)}) async-start(bf16[8,80,1024]{2,1,0:T(8,128)(2,1)} %bitcast.30), calls=%async_computation.2 | async-start | bytes 2621440 | tf_op jit(solution)/shard_map/all_to_all | solution.py:314
  208.8 0.7 slice-start.1
  208.8 1.1 slice-start
  210.8 21.0 %all-to-all-start.3 = ((bf16[8,88,512]{2,1,0:T(8,128)(2,1)}), bf16[8,88,512]{2,1,0:T(8,128)(2,1)S(1)}, u32[]{:S(2)}, u32[]{:S(2)}) async-start(bf16[8,88,512]{2,1,0:T(8,128)(2,1)} %fusion.2), calls=%async_computation.4 | async-start | bytes 1441792 | tf_op jit(solution)/shard_map/all_to_all | solution.py:314
  216.6 5.3 %copy-start.13 = (s32[1,2,2,128]{3,2,1,0:T(2,128)S(1)}, s32[1,2,2,128]{3,2,1,0:T(2,128)}, u32[]{:S(2)}) copy-start(s32[1,2,2,128]{3,2,1,0:T(2,128)} %get-tuple-element.130) | copy-start | bytes 6148
  216.7 15.0 %collective-permute-start.19 = (bf16[3,256,128]{2,1,0:T(8,128)(2,1)S(1)}, bf16[3,256,128]{2,1,0:T(8,128)(2,1)S(1)}, u32[]{:S(2)}, u32[]{:S(2)}) collective-permute-start(bf16[3,256,128]{2,1,0:T(8,128)(2,1)S(1)} %pad_maximum_fusion.4), channel_id=1, source_target_pairs={{0,24},{8,32},{16,40},{24,48},{32,56},{40,0},{48,8},{56,16},{64,88... | collective-permute-start | bytes 589832 | tf_op jit(solution)/shard_map/ppermute | solution.py:19
  219.8 11.4 %collective-permute-start.20 = (bf16[2,256,128]{2,1,0:T(8,128)(2,1)S(1)}, bf16[2,256,128]{2,1,0:T(8,128)(2,1)S(1)}, u32[]{:S(2)}, u32[]{:S(2)}) collective-permute-start(bf16[2,256,128]{2,1,0:T(8,128)(2,1)S(1)} %pad_maximum_fusion.5), channel_id=1, source_target_pairs={{0,40},{8,48},{16,56},{24,0},{32,8},{40,16},{48,24},{56,32},{64,10... | collective-permute-start | bytes 393224 | tf_op jit(solution)/shard_map/ppermute | solution.py:19
  232.9 12.6 %copy-start.9 = (bf16[256,128]{1,0:T(8,128)(2,1)S(1)}, bf16[256,128]{1,0:T(8,128)(2,1)}, u32[]{:S(2)}) copy-start(bf16[256,128]{1,0:T(8,128)(2,1)} %param.7) | copy-start | bytes 196612
  233.0 13.3 %collective-permute-start.23 = (bf16[264,128]{1,0:T(8,128)(2,1)S(1)}, bf16[264,128]{1,0:T(8,128)(2,1)S(1)}, u32[]{:S(2)}, u32[]{:S(2)}) collective-permute-start(bf16[264,128]{1,0:T(8,128)(2,1)S(1)} %get-tuple-element.132), channel_id=1, source_target_pairs={{0,64},{8,72},{16,80},{24,88},{32,96},{40,104},{48,112},{56,120},{... | collective-permute-start | bytes 202760 | tf_op jit(solution)/shard_map/ppermute | solution.py:24
  233.7 12.6 %collective-permute-start.24 = (bf16[264,128]{1,0:T(8,128)(2,1)S(1)}, bf16[264,128]{1,0:T(8,128)(2,1)S(1)}, u32[]{:S(2)}, u32[]{:S(2)}) collective-permute-start(bf16[264,128]{1,0:T(8,128)(2,1)S(1)} %get-tuple-element.133), channel_id=1, source_target_pairs={{0,128},{8,136},{16,144},{24,152},{32,160},{40,168},{48,176},{56,1... | collective-permute-start | bytes 202760 | tf_op jit(solution)/shard_map/ppermute | solution.py:24
  236.4 9.9 %copy-start.11 = (bf16[256,128]{1,0:T(8,128)(2,1)S(1)}, bf16[256,128]{1,0:T(8,128)(2,1)}, u32[]{:S(2)}) copy-start(bf16[256,128]{1,0:T(8,128)(2,1)} %param.13) | copy-start | bytes 196612
  236.4 9.9 %collective-permute-start.25 = (bf16[264,128]{1,0:T(8,128)(2,1)S(1)}, bf16[264,128]{1,0:T(8,128)(2,1)S(1)}, u32[]{:S(2)}, u32[]{:S(2)}) collective-permute-start(bf16[264,128]{1,0:T(8,128)(2,1)S(1)} %get-tuple-element.134), channel_id=1, source_target_pairs={{0,192},{8,200},{16,208},{24,216},{32,224},{40,232},{48,240},{56,2... | collective-permute-start | bytes 202760 | tf_op jit(solution)/shard_map/ppermute | solution.py:24
  237.9 9.1 %copy-start.12 = (f32[256,2]{0,1:T(2,128)S(1)}, f32[256,2]{0,1:T(2,128)}, u32[]{:S(2)}) copy-start(f32[256,2]{0,1:T(2,128)} %param.9) | copy-start | bytes 6148
  238.0 5.6 %collective-permute-start.21 = (bf16[256,128]{1,0:T(8,128)(2,1)S(1)}, bf16[256,128]{1,0:T(8,128)(2,1)S(1)}, u32[]{:S(2)}, u32[]{:S(2)}) collective-permute-start(bf16[256,128]{1,0:T(8,128)(2,1)S(1)} %get-tuple-element.128), channel_id=1, source_target_pairs={{0,8},{8,16},{16,24},{24,32},{32,40},{40,48},{48,56},{56,0},{64,72... | collective-permute-start | bytes 196616 | tf_op jit(solution)/shard_map/ppermute | solution.py:19
  241.3 4.3 %collective-permute-start.22 = (bf16[256,128]{1,0:T(8,128)(2,1)S(1)}, bf16[256,128]{1,0:T(8,128)(2,1)S(1)}, u32[]{:S(2)}, u32[]{:S(2)}) collective-permute-start(bf16[256,128]{1,0:T(8,128)(2,1)S(1)} %get-tuple-element.129), channel_id=1, source_target_pairs={{0,56},{8,0},{16,8},{24,16},{32,24},{40,32},{48,40},{56,48},{64,12... | collective-permute-start | bytes 196616 | tf_op jit(solution)/shard_map/ppermute | solution.py:19
Sparse Core Ops, SparseCore 0:
  47.1 68.2 all-gather.2
  144.5 63.5 reduce-scatter.1
